TPU v7x, 32 devices: a whole 2x2x4 slice. The times are simulated.
32 devices in a mesh: rep: 2 (over x), fsdp: 4 (over z), tp: 4 (over y, core).
Axes of the slice: x: 2, y: 2, z: 4, core: 2. Of those that a mesh axis runs over, the one named last changes fastest.
Arguments:
- tokens: bfloat16 [4096, 8192], P(('rep', 'fsdp')), may hold values from -16 to 16, as said below
- doc_lengths: int32 [8, 8], P(('rep', 'fsdp')), may hold values from 1 to 192, 512 in all within a row
- w_query: bfloat16 [8192, 4096], P(('rep', 'fsdp'), 'tp'), as said below
- w_key: bfloat16 [8192, 512], P(('rep', 'fsdp'), 'tp'), as said below
- w_value: bfloat16 [8192, 512], P(('rep', 'fsdp'), 'tp'), may hold values from -0.0625 to 0.0625
- u_query: float32 [4096], P('tp'), may hold values from -6 to 6
- u_key: float32 [512], P('tp'), may hold values from -6 to 6
- u_value: float32 [512], P('tp'), may hold values from -6 to 6
- gammas: float32 [3], replicated, may hold values from 0.5 to 2
Outputs:
- context: bfloat16 [4096, 4096], P(('rep', 'fsdp'), 'tp')
- u_query_new: float32 [4096], P('tp')
- u_key_new: float32 [512], P('tp')
- u_value_new: float32 [512], P('tp')
- sigmas: float32 [3], replicated
Inputs may be any that keep to these rules, and one draw needn't show every extreme that they name: `tokens`: activations of order one. `w_query`: entries of order one over the square root of 8192. `w_key`: entries of order one over the square root of 8192.
All inputs are finite; a program needn't handle non-finite values.
Results may differ from a plain program's by a relative error of at most 0.0075.
Values may be sent and summed in bfloat16 or wider, within the bound.
No kernel may reach another device: no remote copies, remote signals or barrier semaphores. Data moves between devices by JAX's collectives and lax.ppermute only.
A program may use at most 128 MiB of HBM per device.

v0:
```python
import jax
import jax.numpy as jnp
from jax import lax
from jax.sharding import PartitionSpec as P

HEADS = 32
KV_HEADS = 4
HD = 128


EPSILON = 1e-12
HIGHEST = lax.Precision.HIGHEST
MASKED = -1e30


def attention(queries, key_heads, value_heads, lengths):
    tok_rows = queries.shape[0]
    scores = jnp.einsum(
        "tkgd,skd->kgts", queries, key_heads, preferred_element_type=jnp.float32
    ) * queries.shape[-1] ** (-0.5)
    doc_ends = jnp.cumsum(lengths)
    position = jnp.arange(tok_rows, dtype=jnp.int32)
    doc_ids = jnp.sum((position[:, None] >= doc_ends[None, :]).astype(jnp.int32), axis=1)
    allowed = (doc_ids[:, None] == doc_ids[None, :]) & (position[None, :] <= position[:, None])
    scores = jnp.where(allowed, scores, MASKED)
    row_max = jnp.max(scores, axis=-1, keepdims=True)
    exponent = jnp.exp(scores - row_max)
    attn_probs = (exponent / jnp.sum(exponent, axis=-1, keepdims=True)).astype(jnp.bfloat16)
    mixed = jnp.einsum(
        "kgts,skd->tkgd", attn_probs, value_heads, preferred_element_type=jnp.float32
    )
    return mixed.astype(jnp.bfloat16).reshape(tok_rows, -1)


def fold_rows(source, pieces):
    return tuple((jnp.dot(source, matrix, preferred_element_type=jnp.float32) for matrix in pieces))


def body(tokens, doc_lengths, w_query, w_key, w_value, u_query, u_key, u_value, gammas):
    tok_rows = tokens.shape[0]
    widened = [w_query.astype(jnp.float32), w_key.astype(jnp.float32), w_value.astype(jnp.float32)]
    local_images = [
        jnp.dot(matrix, vector, precision=HIGHEST)
        for matrix, vector in zip(widened, (u_query, u_key, u_value))
    ]
    images = lax.psum((local_images[0], local_images[1], local_images[2]), "tp")
    squares = [jnp.sum(image * image) for image in images]
    norms = lax.psum((squares[0], squares[1], squares[2]), ("rep", "fsdp"))
    partial_backs = [
        jnp.dot(image * lax.rsqrt(total_sq + EPSILON), matrix, precision=HIGHEST)
        for image, total_sq, matrix in zip(images, norms, widened)
    ]
    backs = lax.psum((partial_backs[0], partial_backs[1], partial_backs[2]), ("rep", "fsdp"))
    back_sq = lax.psum(
        (jnp.sum(backs[0] * backs[0]), jnp.sum(backs[1] * backs[1]), jnp.sum(backs[2] * backs[2])),
        "tp",
    )
    sigma_list = [jnp.sqrt(total_sq + EPSILON) for total_sq in back_sq]
    tp_count = lax.axis_size("tp")
    new_states = [
        backed * (jnp.sqrt(jnp.float32(backed.shape[0] * tp_count)) / sigma)
        for backed, sigma in zip(backs, sigma_list)
    ]
    sigmas = jnp.stack(sigma_list)
    tied = lax.optimization_barrier((sigmas, w_query, w_key, w_value))
    products = fold_rows(
        tokens,
        (
            lax.all_gather(tied[1], ("rep", "fsdp"), axis=0, tiled=True),
            lax.all_gather(tied[2], ("rep", "fsdp"), axis=0, tiled=True),
            lax.all_gather(tied[3], ("rep", "fsdp"), axis=0, tiled=True),
        ),
    )
    scales = gammas / sigmas
    scaled = [(scales[which] * products[which]).astype(jnp.bfloat16) for which in range(3)]
    per_group = HEADS // KV_HEADS
    queries = scaled[0].reshape(tok_rows, -1, per_group, HD)
    key_heads = scaled[1].reshape(tok_rows, -1, HD)
    value_heads = scaled[2].reshape(tok_rows, -1, HD)
    context = attention(queries, key_heads, value_heads, doc_lengths[0])
    return (context, new_states[0], new_states[1], new_states[2], sigmas)


def solution(mesh):
    in_specs = (
        P(("rep", "fsdp"), None),
        P(("rep", "fsdp"), None),
        P(("rep", "fsdp"), "tp"),
        P(("rep", "fsdp"), "tp"),
        P(("rep", "fsdp"), "tp"),
        P("tp"),
        P("tp"),
        P("tp"),
        P(),
    )
    out_specs = (P(("rep", "fsdp"), "tp"), P("tp"), P("tp"), P("tp"), P())
    return jax.shard_map(body, mesh=mesh, in_specs=in_specs, out_specs=out_specs, check_vma=False)
```

profile of v0, /device:TPU:8, one launch (start us, length us, event | category | flops | bytes accessed | tf_op | source)
XLA Modules:
  0.0 429.8 jit_solution(11408357073837659301)
XLA Ops:
  7.2 0.0 copy-start
  7.2 0.0 all-gather.8.cloned.1.call-start
  7.2 0.6 copy-done
  7.9 3.3 fusion.24
  11.2 1.3 fusion.16
  12.4 1.3 fusion.18
  13.7 11.2 %all-reduce.3 = (f32[1024]{0:T(1024)S(1)}, f32[1024]{0:T(1024)S(1)}, f32[1024]{0:T(1024)S(1)}) all-reduce(f32[1024]{0:T(1024)S(1)} %bitcast.85, f32[1024]{0:T(1024)S(1)} %bitcast.86, f32[1024]{0:T(1024)S(1)} %bitcast.84), channel_id=1, replica_groups=mesh['rep'=2,'fsdp'=4,'tp'=4] {'tp'}, use_global_device_ids=true, to_apply=%region_12.0 | all-reduce | flops 3072 | bytes 24576 | tf_op jit(solution)/shard_map/psum | solution.py:46
  24.9 0.6 multiply_reduce_fusion.3
  25.5 0.6 multiply_reduce_fusion
  26.1 18.5 %all-reduce.1 = (f32[]{:T(128)}, f32[]{:T(128)}, f32[]{:T(128)}) all-reduce(f32[]{:T(128)} %get-tuple-element.40, f32[]{:T(128)} %get-tuple-element.41, f32[]{:T(128)} %multiply_reduce_fusion.3), channel_id=1, replica_groups=mesh['rep'=2,'fsdp'=4,'tp'=4] {'rep','fsdp'}, use_global_device_ids=true, to_apply=%region_14.0 | all-reduce | flops 3 | bytes 24 | tf_op jit(solution)/shard_map/psum | solution.py:48
  45.3 2.5 fusion.25
  48.5 1.2 convolution_bitcast_fusion
  50.4 1.2 convolution_bitcast_fusion.1
  51.6 21.8 %all-reduce = (f32[128]{0:T(128)S(1)}, f32[128]{0:T(128)S(1)}, f32[1024]{0:T(1024)S(1)}) all-reduce(f32[128]{0:T(128)S(1)} %convolution_bitcast_fusion, f32[128]{0:T(128)S(1)} %convolution_bitcast_fusion.1, f32[1024]{0:T(1024)S(1)} %bitcast.87), channel_id=1, replica_groups=mesh['rep'=2,'fsdp'=4,'tp'=4] {'rep','fsdp'}, use_global_device_ids=true, to_apply=%region_15.0 | all-reduce | flops 1280 | bytes 10240 | tf_op jit(solution)/shard_map/psum | solution.py:53
  73.4 0.6 multiply_reduce_fusion.2
  74.0 0.6 multiply_reduce_fusion.4
  74.6 0.6 multiply_reduce_fusion.5
  75.2 6.4 %all-reduce.2 = (f32[]{:T(128)}, f32[]{:T(128)}, f32[]{:T(128)}) all-reduce(f32[]{:T(128)} %multiply_reduce_fusion.4, f32[]{:T(128)} %multiply_reduce_fusion.5, f32[]{:T(128)} %multiply_reduce_fusion.2), channel_id=1, replica_groups=mesh['rep'=2,'fsdp'=4,'tp'=4] {'tp'}, use_global_device_ids=true, to_apply=%region_17.0 | all-reduce | flops 3 | bytes 24 | tf_op jit(solution)/shard_map/psum | solution.py:54
  83.7 1.2 fusion.22
  84.9 0.0 all-gather.8.cloned.1.call-update
  84.9 0.0 all-gather.6.cloned.1.call-start
  85.0 0.7 all-gather.6.cloned.1.call-update
  85.7 0.0 all-gather.4.cloned.1.call-start
  85.7 0.7 all-gather.4.cloned.1.call-update
  86.5 0.6 fusion.23
  87.1 0.8 reduce-window.8
  88.0 0.1 convert_reduce_fusion
  88.0 0.2 fusion.13
  88.3 0.6 broadcast_multiply_fusion
  88.9 0.5 broadcast_multiply_fusion.4
  89.4 0.5 broadcast_multiply_fusion.5
  89.9 218.3 %all-gather.8.cloned.1.call-done = bf16[8192,1024]{1,0:T(8,128)(2,1)} async-done(((bf16[1024,1024]{1,0:T(8,128)(2,1)}), bf16[8192,1024]{1,0:T(8,128)(2,1)}) %all-gather.8.cloned.1.call-update) | async-done | bytes 16777232 | tf_op jit(solution)/shard_map/all_gather | solution.py:69
  308.2 15.7 %multiply_convert_fusion = bf16[1024,512]{1,0:T(8,128)(2,1)S(1)} fusion(bf16[8192,1024]{1,0:T(8,128)(2,1)} %all-gather.8.cloned.1.call-done, bf16[512,8192]{1,0:T(8,128)(2,1)} %param.9, f32[]{:T(128)} %bitcast.21), kind=kOutput, calls=%fused_computation.8 | convolution fusion | flops 8590983168 | bytes 26214404 | tf_op jit(solution)/shard_map/dot_general | solution.py:36
  323.9 35.8 %all-gather.6.cloned.1.call-done = bf16[8192,128]{1,0:T(8,128)(2,1)} async-done(((bf16[1024,128]{1,0:T(8,128)(2,1)}), bf16[8192,128]{1,0:T(8,128)(2,1)}) %all-gather.6.cloned.1.call-update) | async-done | bytes 2097168 | tf_op jit(solution)/shard_map/all_gather | solution.py:70
  359.7 13.4 %fusion.1 = (f32[8,512]{1,0:T(8,128)S(1)}, f32[512,512,8]{1,0,2:T(8,128)}) fusion(pred[512,512]{0,1:T(8,128)(4,1)S(1)} %fusion.13, bf16[512,8,128]{0,2,1:T(8,128)(2,1)S(1)} %bitcast.82, bf16[512,8192]{1,0:T(8,128)(2,1)} %param.9, bf16[8192,128]{1,0:T(8,128)(2,1)} %all-gather.6.cloned.1.call-done, f32[]{:T(128)} %bitcast.19), kind=kOutput, calls=%fused_computation.4 | convolution fusion | flops 1617031168 | bytes 20201476 | tf_op jit(solution)/shard_map/tkgd,skd->kgts/dot_general | solution.py:18
  373.1 5.2 %fusion = f32[8,512]{1,0:T(8,128)S(1)} fusion(f32[512,512,8]{1,0,2:T(8,128)} %get-tuple-element.39, f32[8,512]{1,0:T(8,128)S(1)} %get-tuple-element.38, pred[512,512]{0,1:T(8,128)(4,1)S(1)} %fusion.13), kind=kLoop, calls=%fused_computation.3 | loop fusion | flops 8384512 | bytes 8683520 | tf_op jit(solution)/shard_map/reduce_sum | solution.py:28
  378.3 31.3 %all-gather.4.cloned.1.call-done = bf16[8192,128]{1,0:T(8,128)(2,1)} async-done(((bf16[1024,128]{1,0:T(8,128)(2,1)}), bf16[8192,128]{1,0:T(8,128)(2,1)}) %all-gather.4.cloned.1.call-update) | async-done | bytes 2097168 | tf_op jit(solution)/shard_map/all_gather | solution.py:71
  409.6 12.3 %fusion.5 = bf16[128,8,512]{2,0,1:T(8,128)(2,1)S(1)} fusion(f32[8,512]{1,0:T(8,128)S(1)} %fusion, f32[8,512]{1,0:T(8,128)S(1)} %get-tuple-element.38, f32[512,512,8]{1,0,2:T(8,128)} %get-tuple-element.39, pred[512,512]{0,1:T(8,128)(4,1)S(1)} %fusion.13, bf16[8192,128]{1,0:T(8,128)(2,1)} %all-gather.4.cloned.1.call-done, bf16[512,8192]{1,0:T(8,128)(2,1)} %param.9, ...), kind=kOutput, calls=%fused_computation.9 | convolution fusion | flops 1621753856 | bytes 20217860 | tf_op jit(solution)/shard_map/kgts,skd->tkgd/dot_general | solution.py:29
  422.0 1.3 copy.19
  (3 shorter events, 0.0 us)
Async XLA Ops:
  7.2 0.7 copy-start
  7.2 301.0 %all-gather.8.cloned.1.call-start = ((), (), s32[]{:S(2)}) async-start(), calls=%async_computation.2 | async-start | bytes 18874368 | tf_op jit(solution)/shard_map/all_gather | solution.py:69
  84.9 274.7 %all-gather.6.cloned.1.call-start = ((), (), s32[]{:S(2)}) async-start(), calls=%async_computation.1 | async-start | bytes 2359296 | tf_op jit(solution)/shard_map/all_gather | solution.py:70
  85.7 323.9 %all-gather.4.cloned.1.call-start = ((), (), s32[]{:S(2)}) async-start(), calls=%async_computation | async-start | bytes 2359296 | tf_op jit(solution)/shard_map/all_gather | solution.py:71
Sparse Core Ops, SparseCore 0:
  85.1 223.0 all-gather.7
  310.3 49.3 all-gather.5
  361.8 47.7 all-gather.3
where the time goes:
time: 432 us; the launch traced here: 430 us
  waiting for transfers between devices  287 us (66%)
  blocking collectives  57.9 us (13%)
  matrix products  52.1 us (12%)
  between operations  18.1 us (4%)
  other arithmetic  12.2 us (3%)
    all_gather x1, waiting for transfers between devices, body(): lax.all_gather(tied[1], ('rep', 'fsdp'), axis=0, tiled=True)  218 us
    all_gather x1, waiting for transfers between devices, body(): lax.all_gather(tied[2], ('rep', 'fsdp'), axis=0, tiled=True)  35.8 us
    all_gather x1, waiting for transfers between devices, body(): lax.all_gather(tied[3], ('rep', 'fsdp'), axis=0, tiled=True)  31.3 us
    psum x1, blocking collectives, body(): lax.psum((partial_backs[0], partial_backs[1], partial_backs[2]), ('rep',...  21.8 us
    psum x1, blocking collectives, body(): norms = lax.psum((squares[0], squares[1], squares[2]), ('rep', 'fsdp'))  18.5 us
    dot_general x1, matrix products, fold_rows(): jnp.dot(source, matrix, preferred_element_type=jnp.float32)  15.7 us
    dot_general x1, matrix products, attention(): jnp.einsum('tkgd,skd->kgts', queries, key_heads, preferred_element_type=j...  13.4 us
    dot_general x1, matrix products, attention(): jnp.einsum('kgts,skd->tkgd', attn_probs, value_heads, preferred_element_t...  12.3 us
  transfers between devices with their start and end apart: 3, of which 3 were waited for; matrix products, arithmetic and copies ran while one was open for 9% of the time, Pallas kernels for 0%

commit v1 on v0

v1 whole, which is shorter than its diff:
```python
import functools

import jax
import jax.numpy as jnp
from jax import lax
from jax.experimental import pallas as pl
from jax.experimental.pallas import tpu as pltpu
from jax.sharding import PartitionSpec as P

HEADS = 32
KV_HEADS = 4
HD = 128
DOC_MOST = 192

EPSILON = 1e-12
HIGHEST = lax.Precision.HIGHEST
MASKED = -1e30
ROWS = ("rep", "fsdp")
F32 = jnp.float32
SMALL = pl.CostEstimate(flops=1, bytes_accessed=1, transcendentals=0)
BF16 = jnp.bfloat16
HALF = jnp.float16


def attention(queries, key_heads, value_heads, lengths):
    tok_rows = queries.shape[0]
    scores = jnp.einsum(
        "tkgd,skd->kgts", queries, key_heads, preferred_element_type=F32
    ) * queries.shape[-1] ** (-0.5)
    doc_ends = jnp.cumsum(lengths)
    position = jnp.arange(tok_rows, dtype=jnp.int32)
    doc_ids = jnp.sum((position[:, None] >= doc_ends[None, :]).astype(jnp.int32), axis=1)
    allowed = (doc_ids[:, None] == doc_ids[None, :]) & (position[None, :] <= position[:, None])
    scores = jnp.where(allowed, scores, MASKED)
    row_max = jnp.max(scores, axis=-1, keepdims=True)
    exponent = jnp.exp(scores - row_max)
    attn_probs = (exponent / jnp.sum(exponent, axis=-1, keepdims=True)).astype(BF16)
    mixed = jnp.einsum("kgts,skd->tkgd", attn_probs, value_heads, preferred_element_type=F32)
    return mixed.astype(BF16).reshape(tok_rows, -1)


def gather_body(tokens, doc_lengths, w_query, w_key, w_value, u_query, u_key, u_value, gammas):
    tok_rows = tokens.shape[0]
    widened = [w_query.astype(F32), w_key.astype(F32), w_value.astype(F32)]
    local_images = [
        jnp.dot(matrix, vector, precision=HIGHEST)
        for matrix, vector in zip(widened, (u_query, u_key, u_value))
    ]
    images = lax.psum((local_images[0], local_images[1], local_images[2]), "tp")
    squares = [jnp.sum(image * image) for image in images]
    norms = lax.psum((squares[0], squares[1], squares[2]), ROWS)
    partial_backs = [
        jnp.dot(image * lax.rsqrt(total_sq + EPSILON), matrix, precision=HIGHEST)
        for image, total_sq, matrix in zip(images, norms, widened)
    ]
    backs = lax.psum((partial_backs[0], partial_backs[1], partial_backs[2]), ROWS)
    back_sq = lax.psum(tuple(jnp.sum(back * back) for back in backs), "tp")
    sigma_list = [jnp.sqrt(total_sq + EPSILON) for total_sq in back_sq]
    tp_count = lax.axis_size("tp")
    new_states = [
        backed * (jnp.sqrt(F32(backed.shape[0] * tp_count)) / sigma)
        for backed, sigma in zip(backs, sigma_list)
    ]
    sigmas = jnp.stack(sigma_list)
    products = [
        jnp.dot(
            tokens, lax.all_gather(w, ROWS, axis=0, tiled=True), preferred_element_type=F32
        )
        for w in (w_query, w_key, w_value)
    ]
    scales = gammas / sigmas
    scaled = [(scales[which] * products[which]).astype(BF16) for which in range(3)]
    per_group = HEADS // KV_HEADS
    queries = scaled[0].reshape(tok_rows, -1, per_group, HD)
    key_heads = scaled[1].reshape(tok_rows, -1, HD)
    value_heads = scaled[2].reshape(tok_rows, -1, HD)
    context = attention(queries, key_heads, value_heads, doc_lengths[0])
    return (context, new_states[0], new_states[1], new_states[2], sigmas)


def stacked_terms(row):
    high = row.astype(BF16).astype(F32)
    rest = row - high
    middle = rest.astype(BF16).astype(F32)
    low = rest - middle
    which = lax.broadcasted_iota(jnp.int32, (8, row.shape[1]), 0)
    zero = jnp.zeros((8, row.shape[1]), F32)
    out = jnp.where(which == 0, high, jnp.where(which == 1, middle, jnp.where(which == 2, low, zero)))
    return out.astype(BF16)


def image_kernel(wq, wk, wv, uq, uk, uv, out):
    for i, (w, u) in enumerate(((wq, uq), (wk, uk), (wv, uv))):
        terms = lax.dot_general(
            stacked_terms(u[...]), w[...], (((1,), (1,)), ((), ())), preferred_element_type=F32
        )
        out[i : i + 1, :] = jnp.sum(terms, axis=0, keepdims=True)


def back_kernel(wq, wk, wv, image, out):
    lane = lax.broadcasted_iota(jnp.int32, (1, 128), 1)
    norms = jnp.zeros((1, 128), F32)
    at = 0
    for i, w in enumerate((wq, wk, wv)):
        row = image[i : i + 1, :]
        terms = jnp.dot(stacked_terms(row), w[...], preferred_element_type=F32)
        out[:, at : at + w.shape[1]] = jnp.sum(terms, axis=0, keepdims=True)
        at += w.shape[1]
        norms = jnp.where(lane == i, jnp.sum(row * row, axis=1, keepdims=True), norms)
    out[:, at : at + 128] = norms


def length_kernel(widths, summed, back, squares):
    lane = lax.broadcasted_iota(jnp.int32, (1, 128), 1)
    total = sum(widths)
    found = jnp.zeros((1, 128), F32)
    at = 0
    for i, width in enumerate(widths):
        norm = summed[:, total + i : total + i + 1]
        row = summed[:, at : at + width] * lax.rsqrt(norm + EPSILON)
        back[:, at : at + width] = row
        found = jnp.where(lane == i, jnp.sum(row * row, axis=1, keepdims=True), found)
        at += width
    squares[...] = found


def state_kernel(widths, tp_count, back, squares, new_q, new_k, new_v, sigmas):
    sigma = jnp.sqrt(squares[...] + EPSILON)
    sigmas[...] = sigma
    at = 0
    for i, (width, out) in enumerate(zip(widths, (new_q, new_k, new_v))):
        factor = jnp.sqrt(jnp.full((1, 1), width * tp_count, F32)) / sigma[:, i : i + 1]
        out[...] = back[:, at : at + width] * factor
        at += width


def whole(kernel, out_shape, *args):
    return pl.pallas_call(kernel, out_shape=out_shape, cost_estimate=SMALL)(*args)


def quarter_product(where, sources, w_own, w_other, index=None):
    deep, n = w_own.shape
    step = 512
    half = deep // step
    rows = sources[0].shape[0] if index is None else index[0]
    maps = [lambda k, where: (0, k)] * 4 if index is None else index[1](half)

    def kernel(where_ref, q0, q1, q2, q3, wa, wb, out):
        k = pl.program_id(0)
        x = jnp.concatenate([q[...] for q in (q0, q1, q2, q3)], axis=0)

        @pl.when(k == 0)
        def _():
            out[...] = jnp.dot(x, wa[...], preferred_element_type=F32)

        @pl.when((k > 0) & (k < half))
        def _():
            out[...] += jnp.dot(x, wa[...], preferred_element_type=F32)

        @pl.when(k >= half)
        def _():
            out[...] += jnp.dot(x, wb[...], preferred_element_type=F32)

    return pl.pallas_call(
        kernel,
        out_shape=jax.ShapeDtypeStruct((4 * rows, n), F32),
        grid_spec=pltpu.PrefetchScalarGridSpec(
            num_scalar_prefetch=1,
            grid=(2 * half,),
            in_specs=[pl.BlockSpec((rows, step), m) for m in maps]
            + [
                pl.BlockSpec((step, n), lambda k, where: (jnp.minimum(k, half - 1), 0)),
                pl.BlockSpec((step, n), lambda k, where: (jnp.maximum(k - half, 0), 0)),
            ],
            out_specs=pl.BlockSpec((4 * rows, n), lambda k, where: (0, 0)),
        ),
        cost_estimate=SMALL,
    )(where, *sources, w_own, w_other)


def context_kernel(first, heads, place, lengths, packed, *refs):
    if first:
        ctx, keys, values, scaled = refs
    else:
        keys, values, _, ctx, scaled = refs
    rows = packed.shape[0]
    block = rows // 4
    at = 2 * HD if first else 0
    for j in range(4):
        here = pl.ds(j * block, block)
        there = pl.ds(pl.multiple_of((place[0] ^ j) * block, block), block)
        if first:
            keys[there, :] = packed[here, :HD]
            values[there, :] = packed[here, HD:at]
        for h in range(heads):
            scaled[h, there, :] = packed[here, at + h * HD : at + (h + 1) * HD]
    for i in range(rows // block):
        low = max(0, (i * block - DOC_MOST + 1) // HD * HD)
        high = (i + 1) * block
        position = lax.broadcasted_iota(jnp.int32, (block, 1), 0) + i * block
        start = jnp.zeros((block, 1), jnp.int32)
        end = 0
        for k in range(lengths.shape[1]):
            end = end + lengths[0, k]
            start = jnp.where(position >= end, end, start)
        key_at = lax.broadcasted_iota(jnp.int32, (block, high - low), 1) + low
        allowed = ((key_at >= start) & (key_at <= position))[None]
        q = scaled[:, i * block : high, :].reshape(heads * block, HD)
        s = lax.dot_general(
            q, keys[low:high, :], (((1,), (1,)), ((), ())), preferred_element_type=F32
        ).reshape(heads, block, high - low)
        s = jnp.where(allowed, s * HD ** (-0.5), MASKED)
        e = jnp.exp(s - jnp.max(s, axis=2, keepdims=True))
        p = (e * (1.0 / jnp.sum(e, axis=2, keepdims=True))).astype(BF16)
        mixed = jnp.dot(
            p.reshape(heads * block, high - low), values[low:high, :], preferred_element_type=F32
        ).astype(BF16)
        for h in range(heads):
            ctx[i * block : high, h * HD : (h + 1) * HD] = mixed[h * block : (h + 1) * block, :]


def full(x):
    return pl.BlockSpec(x.shape, lambda i, place: (0,) * x.ndim)


def context_call(place, lengths, packed, width, kv=None, ctx=None):
    first = kv is None
    rows, n = packed.shape
    heads = (n - (2 * HD if first else 0)) // HD
    args = [lengths, packed]
    specs = [pl.BlockSpec(memory_space=pltpu.SMEM), full(packed)]
    half = jax.ShapeDtypeStruct((rows, HD), BF16)
    context = jax.ShapeDtypeStruct((rows, width), BF16)
    aliases = {}
    if first:
        out_shape = (context, half, half)
        out_specs = (
            pl.BlockSpec((rows, heads * HD), lambda i, place: (0, 0)),
            full(half),
            full(half),
        )
    else:
        args += [kv[0], kv[1], ctx]
        specs += [full(kv[0]), full(kv[1]), pl.BlockSpec(memory_space=pl.ANY)]
        out_shape = context
        out_specs = pl.BlockSpec((rows, heads * HD), lambda i, place: (0, 1))
        aliases = {len(args): 0}
    return pl.pallas_call(
        functools.partial(context_kernel, first, heads),
        out_shape=out_shape,
        grid_spec=pltpu.PrefetchScalarGridSpec(
            num_scalar_prefetch=1,
            grid=(1,),
            in_specs=specs,
            out_specs=out_specs,
            scratch_shapes=[pltpu.VMEM((heads, rows, HD), BF16)],
        ),
        input_output_aliases=aliases,
        cost_estimate=SMALL,
    )(place, *args)


class Order:
    def __init__(self):
        self.last = None

    def after(self, x):
        if self.last is None:
            return x
        x, self.last = lax.optimization_barrier((x, self.last))
        return x

    def note(self, x):
        self.last = x
        return x


def line_body(tokens, doc_lengths, w_query, w_key, w_value, u_query, u_key, u_value, gammas):
    tok_rows = tokens.shape[0]
    deep, q_width = w_query.shape
    kv_width = w_key.shape[1]
    widths = (q_width, kv_width, kv_width)
    reps, line, tp_count = lax.axis_size("rep"), lax.axis_size("fsdp"), lax.axis_size("tp")
    rep, slot, place = lax.axis_index("rep"), lax.axis_index("fsdp"), lax.axis_index("tp")
    quarter = tok_rows // tp_count
    send = lax.ppermute
    ends, mids, everyone = (0, line - 1), (1, line - 2), tuple(range(line))
    order = Order()
    after, note = order.after, order.note

    def swap(x, axis, mask, size):
        return send(x, axis, [(i, i ^ mask) for i in range(size)])

    def swap_tp(x, mask, who):
        pairs = [(s * tp_count + i, s * tp_count + (i ^ mask)) for s in who for i in range(tp_count)]
        return send(x, ("fsdp", "tp"), pairs)

    def cut(source, row, mask, rows):
        return jnp.concatenate(
            [
                lax.dynamic_slice(
                    source, (row, ((rep ^ r) * line + (slot ^ mask)) * deep), (rows, deep)
                )
                for r in range(reps)
            ],
            axis=1,
        )

    def product(parts, c):
        parts = after(tuple(parts))
        return note(quarter_product(where, parts, own_w[c], other_w[c]))

    def own_product(c):
        def maps(half):
            def one(j):
                def index(k, where):
                    column = ((where[1] ^ (k // half)) * line + where[2]) * half + k % half
                    return (where[0] ^ j, column)

                return index

            return [one(j) for j in range(tp_count)]

        source = after(tokens)
        return note(
            quarter_product(where, [source] * 4, own_w[c], other_w[c], (quarter, maps))
        )

    def arrived(x):
        return note(after(x))

    def joined(p, x):
        return note((p + after(x).astype(F32)).astype(HALF))

    def out(x):
        return send(x, "fsdp", [(0, 1), (3, 2)])

    def across(x):
        return send(x, "fsdp", [(1, 2), (2, 1)])

    where = jnp.stack([place, rep, slot]).astype(jnp.int32)
    split = q_width // 2
    total = sum(widths)
    row = jax.ShapeDtypeStruct((1, total), F32)
    lanes = jax.ShapeDtypeStruct((1, 128), F32)
    other_w = [None, None]

    mine = note(cut(tokens, place * quarter, 3, quarter))
    x3e = send(mine, "fsdp", [(0, 3), (3, 0)])
    own_w = [
        note(jnp.concatenate([after(w_key), w_value, w_query[:, :split]], axis=1)),
        w_query[:, split:],
    ]
    other_w[0] = swap(own_w[0], "rep", 1, reps)
    img = note(
        whole(
            image_kernel,
            jax.ShapeDtypeStruct((3, deep), F32),
            after(w_query),
            w_key,
            w_value,
            u_query[None],
            u_key[None],
            u_value[None],
        )
    )
    img_c = swap(img, "tp", 1, tp_count)
    x2 = note(cut(after(tokens), place * quarter, 2, quarter))
    img = note(img + after(img_c))
    img_y = swap(img, "tp", 2, tp_count)
    x2 = swap(after(x2), "fsdp", 2, line)
    x1 = note(cut(after(tokens), place * quarter, 1, quarter))
    img = note(img + after(img_y))
    back = note(
        whole(
            back_kernel,
            jax.ShapeDtypeStruct((1, total + 128), F32),
            w_query,
            w_key,
            w_value,
            after(img),
        )
    )
    x3e = arrived(x3e)
    x3e_far = swap_tp(x3e, 2, ends)
    x3e_near = swap_tp(x3e, 1, ends)
    x1 = swap(after(x1), "fsdp", 1, line)
    x3e_near = arrived(x3e_near)
    x3e_far = arrived(x3e_far)
    parts3e = (x3e, x3e_near, x3e_far, arrived(swap_tp(x3e_far, 1, ends)))
    other_w[0] = arrived(other_w[0])
    v = note(product(parts3e, 0).astype(HALF))
    a3 = out(v)
    back_x = swap(after(back), "rep", 1, reps)
    x2 = arrived(x2)
    x2_far = swap_tp(x2, 2, everyone)
    x2_near = arrived(swap_tp(x2, 1, everyone))
    back = note(back + after(back_x))
    back_z = swap(back, "fsdp", 1, line)
    other_w[1] = swap(after(own_w[1]), "rep", 1, reps)
    x1 = arrived(x1)
    x3m = across(after(mine))
    p0 = [own_product(0), None]
    x2_far = arrived(x2_far)
    x1_far = swap_tp(after(x1), 2, everyone)
    parts2 = (x2, x2_near, x2_far, arrived(swap_tp(x2_far, 1, everyone)))
    p2 = product(parts2, 0)
    x3m = arrived(x3m)
    x1_near = arrived(swap_tp(after(x1), 1, everyone))
    v = joined(p2, a3)
    a2e, a2m = out(v), across(v)
    back = note(back + after(back_z))
    back_z = swap(back, "fsdp", 2, line)
    x1_far = arrived(x1_far)
    parts1 = (x1, x1_near, x1_far, arrived(swap_tp(x1_far, 1, everyone)))
    p1 = product(parts1, 0)
    other_w[1] = arrived(other_w[1])
    v = note(product(parts3e, 1).astype(HALF))
    a3 = out(v)
    x3m_far = swap_tp(after(x3m), 2, mids)
    p2 = product(parts2, 1)
    x3m_far = arrived(x3m_far)
    x3m_near = swap_tp(after(x3m), 1, mids)
    x3m_last = swap_tp(x3m_far, 1, mids)
    parts3 = (x3m, arrived(x3m_near), x3m_far, arrived(x3m_last))
    p3 = product(parts3, 0)
    v = joined(p3, a2e)
    a1m = [across(v), None]
    v = joined(p1, a2m)
    a1p = [swap(v, "fsdp", 1, line), None]
    p1 = product(parts1, 1)
    back = note(back + after(back_z))
    back, squares = note(whole(functools.partial(length_kernel, widths), (row, lanes), back))
    squares_c = swap(squares, "tp", 1, tp_count)
    p3 = product(parts3, 1)
    squares = note(squares + after(squares_c))
    v = joined(p2, a3)
    a2e, a2m = out(v), across(v)
    squares_y = swap(after(squares), "tp", 2, tp_count)
    p0[1] = own_product(1)
    squares = note(squares + after(squares_y))
    states = note(
        whole(
            functools.partial(state_kernel, widths, tp_count),
            tuple(jax.ShapeDtypeStruct((1, n), F32) for n in widths) + (lanes,),
            back,
            squares,
        )
    )
    scales = gammas / states[3][0, :3]
    q_row = jnp.full((1, split), 1.0, F32) * scales[0]
    kv_row = [jnp.full((1, kv_width), 1.0, F32) * scales[i] for i in (1, 2)]
    factor = [jnp.concatenate(kv_row + [q_row], axis=1), q_row]
    factor = note(after(tuple(factor)))
    v = joined(p3, a2e)
    a1m[1] = across(v)
    v = joined(p1, a2m)
    a1p[1] = swap(v, "fsdp", 1, line)

    def packed(c):
        near, far = after((a1p[c], a1m[c]))
        return note((factor[c] * (p0[c] + near.astype(F32) + far.astype(F32))).astype(BF16))

    ctx, keys, values = note(context_call(where, doc_lengths, packed(0), q_width))
    context = context_call(where, doc_lengths, packed(1), q_width, (keys, values), ctx)
    return (context, states[0][0], states[1][0], states[2][0], states[3][0, :3])


def solution(mesh):
    in_specs = (
        P(("rep", "fsdp"), None),
        P(("rep", "fsdp"), None),
        P(("rep", "fsdp"), "tp"),
        P(("rep", "fsdp"), "tp"),
        P(("rep", "fsdp"), "tp"),
        P("tp"),
        P("tp"),
        P("tp"),
        P(),
    )
    out_specs = (P(("rep", "fsdp"), "tp"), P("tp"), P("tp"), P("tp"), P())
    sizes = tuple(mesh.shape[name] for name in ("rep", "fsdp", "tp"))
    body = line_body if sizes == (2, 4, 4) else gather_body
    return jax.shard_map(body, mesh=mesh, in_specs=in_specs, out_specs=out_specs, check_vma=False)
```

time: 432 us -> 253 us (0.59)
  waiting for transfers between devices: 287 us -> 72.8 us
  Pallas kernels: 0 us -> 81.7 us
  blocking collectives: 57.9 us -> 0 us
  starting transfers between devices: 0.12 us -> 55.9 us
  matrix products: 52.1 us -> 0 us
  between operations: 18.1 us -> 1.16 us
  other arithmetic: 12.2 us -> 26.5 us
  local copies, waits for them, and re-layouts: 2.57 us -> 13.3 us
    all_gather x3 -> x0, waiting for transfers between devices: 285 us -> none  [the longest x1 218 us: body(): lax.all_gather(tied[1], ('rep', 'fsdp'), axis=0, tiled=True)]
    pallas_call x0 -> x16, Pallas kernels: none -> 81.7 us  [the longest x10 63.5 us: quarter_product(): pl.pallas_call(kernel, out_shape=jax.ShapeDtypeStruct((4 * rows, n), F32)...]
    ppermute x0 -> x35, waiting for transfers between devices: none -> 72.8 us  [the longest x13 32 us: swap(): return send(x, axis, [(i, i ^ mask) for i in range(size)])]
    psum x4 -> x0, blocking collectives: 57.9 us -> none  [the longest x1 21.8 us: body(): lax.psum((partial_backs[0], partial_backs[1], partial_backs[2]), ('rep',...]
    ppermute x0 -> x35, starting transfers between devices: none -> 55.9 us  [the longest x13 21.6 us: swap(): return send(x, axis, [(i, i ^ mask) for i in range(size)])]
    dot_general x9 -> x0, matrix products: 52.1 us -> none  [the longest x1 15.7 us: fold_rows(): jnp.dot(source, matrix, preferred_element_type=jnp.float32)]
    convert_element_type x0 -> x10, other arithmetic: none -> 20.3 us  [the longest x6 10.8 us: joined(): return note((p + after(x).astype(F32)).astype(HALF))]
    reduce_sum x7 -> x0, other arithmetic: 8.33 us -> none  [the longest x1 5.24 us: attention(): jnp.sum(exponent, axis=-1, keepdims=True)]
  transfers between devices with their start and end apart: 3 -> 35, of which waited for: 3 -> 14; matrix products, arithmetic and copies ran while one was open for 9% -> 10% of each run, Pallas kernels for 0% -> 28%
where the time goes in v1:
time: 253 us; the launch traced here: 251 us
  Pallas kernels  81.7 us (32%)
  waiting for transfers between devices  72.8 us (29%)
  starting transfers between devices  55.9 us (22%)
  other arithmetic  26.5 us (10%)
  local copies, waits for them, and re-layouts  13.3 us (5%)
    pallas_call x10, Pallas kernels, quarter_product(): pl.pallas_call(kernel, out_shape=jax.ShapeDtypeStruct((4 * rows, n), F32)...  63.5 us
    ppermute x13, waiting for transfers between devices, swap(): return send(x, axis, [(i, i ^ mask) for i in range(size)])  32 us
    ppermute x5, waiting for transfers between devices, across(): return send(x, 'fsdp', [(1, 2), (2, 1)])  29.4 us
    ppermute x13, starting transfers between devices, swap(): return send(x, axis, [(i, i ^ mask) for i in range(size)])  21.6 us
    ppermute x5, starting transfers between devices, across(): return send(x, 'fsdp', [(1, 2), (2, 1)])  14.7 us
    ppermute x12, starting transfers between devices, swap_tp(): return send(x, ('fsdp', 'tp'), pairs)  12.7 us
    convert_element_type x6, other arithmetic, joined(): return note((p + after(x).astype(F32)).astype(HALF))  10.8 us
    pallas_call x2, Pallas kernels, context_call(): pl.pallas_call(functools.partial(context_kernel, first, heads), out_shape...  9.57 us
  transfers between devices with their start and end apart: 35, of which 14 were waited for; matrix products, arithmetic and copies ran while one was open for 10% of the time, Pallas kernels for 28%

profile of v1, /device:TPU:8, one launch (start us, length us, event | category | flops | bytes accessed | tf_op | source)
XLA Modules:
  0.0 251.5 jit_solution(7433513921869040322)
XLA Ops:
  0.7 1.2 fusion.3
  2.7 1.6 collective-permute-start.2
  4.4 1.1 fusion.5
  5.6 1.6 collective-permute-start.6
  7.2 3.1 %shard_map.128 = f32[3,1024]{1,0:T(4,128)} custom-call(bf16[1024,1024]{1,0:T(8,128)(2,1)} %wq.2, bf16[1024,128]{1,0:T(8,128)(2,1)} %wk.3, bf16[1024,128]{1,0:T(8,128)(2,1)} %wv.3, f32[1,1024]{1,0:T(1,128)} %bitcast.17, f32[1,128]{1,0:T(1,128)} %bitcast.18, f32[1,128]{1,0:T(1,128)} %bitcast.19), custom_call_target="tpu_custom_call" | custom-call | flops 1 | bytes 1 | tf_op jit(solution)/shard_map/pallas_call | solution.py:138
  10.3 1.1 fusion.2
  13.3 1.6 collective-permute-start.1
  15.8 1.4 collective-permute-done.1
  17.8 2.8 %shard_map.129 = f32[1,1408]{1,0:T(1,128)} custom-call(bf16[1024,1024]{1,0:T(8,128)(2,1)} %wq.2, bf16[1024,128]{1,0:T(8,128)(2,1)} %wk.3, bf16[1024,128]{1,0:T(8,128)(2,1)} %wv.3, f32[3,1024]{1,0:T(4,128)} %add.109.image), custom_call_target="tpu_custom_call" | custom-call | flops 1 | bytes 1 | tf_op jit(solution)/shard_map/pallas_call | solution.py:138
  20.5 1.4 collective-permute-start.3
  22.6 6.5 %collective-permute-start.8 = (bf16[128,2048]{1,0:T(8,128)(2,1)}, bf16[128,2048]{1,0:T(8,128)(2,1)}, u32[]{:S(2)}, u32[]{:S(2)}) collective-permute-start(bf16[128,2048]{1,0:T(8,128)(2,1)} %pad_maximum_fusion.2), channel_id=1, source_target_pairs={{0,8},{4,12},{8,0},{12,4},{1,9},{5,13},{9,1},{13,5},{2,10},{6,14},... | collective-permute-start | bytes 1572872 | tf_op jit(solution)/shard_map/ppermute | solution.py:292
  29.9 22.4 %collective-permute-done.8.q0 = bf16[128,2048]{1,0:T(8,128)(2,1)} collective-permute-done((bf16[128,2048]{1,0:T(8,128)(2,1)}, bf16[128,2048]{1,0:T(8,128)(2,1)}, u32[]{:S(2)}, u32[]{:S(2)}) %collective-permute-start.8) | collective-permute-done | bytes 524320 | tf_op jit(solution)/shard_map/ppermute | solution.py:292
  52.8 2.2 collective-permute-start.14
  56.5 1.1 copy-done.1
  57.6 6.9 %shard_map.131 = f32[512,768]{1,0:T(8,128)} custom-call(s32[3]{0:T(128)} %pad_add_fusion.where_ref.place, bf16[512,8192]{1,0:T(8,128)(2,1)} %q3.1, bf16[512,8192]{1,0:T(8,128)(2,1)} %q3.1, bf16[512,8192]{1,0:T(8,128)(2,1)} %q3.1, bf16[512,8192]{1,0:T(8,128)(2,1)} %q3.1, bf16[1024,768]{1,0:T(8,128)(2,1)} %copy-done, bf16[1024,768]{1,0:T(8,128)(2,1)} %copy-done.1), custom_call_target="tpu_custom_call" | custom-call | flops 1 | bytes 1 | tf_op jit(solution)/shard_map/pallas_call | solution.py:164
  64.5 1.3 collective-permute-done.11.q2
  65.8 1.3 collective-permute-done.14.q0
  67.2 3.0 %collective-permute-start.15 = (bf16[128,2048]{1,0:T(8,128)(2,1)}, bf16[128,2048]{1,0:T(8,128)(2,1)S(1)}, u32[]{:S(2)}, u32[]{:S(2)}) collective-permute-start(bf16[128,2048]{1,0:T(8,128)(2,1)} %pad_maximum_fusion.1), channel_id=1, source_target_pairs={{4,8},{8,4},{5,9},{9,5},{6,10},{10,6},{7,11},{11,7},{20,24},{24,20... | collective-permute-start | bytes 1572872 | tf_op jit(solution)/shard_map/ppermute | solution.py:339
  70.1 6.7 %shard_map.130 = f32[512,768]{1,0:T(8,128)} custom-call(s32[3]{0:T(128)} %pad_add_fusion.where_ref.place, bf16[128,2048]{1,0:T(8,128)(2,1)} %collective-permute-done.2.q0, bf16[128,2048]{1,0:T(8,128)(2,1)} %collective-permute-done.3.q1, bf16[128,2048]{1,0:T(8,128)(2,1)} %copy-done.14, bf16[128,2048]{1,0:T(8,128)(2,1)} %copy-done.15, ...), custom_call_target="tpu_custom_call" | custom-call | flops 1 | bytes 1 | tf_op jit(solution)/shard_map/pallas_call | solution.py:164
  76.9 2.4 convert_element_type.60
  79.3 1.4 collective-permute-start.13
  81.5 6.7 %shard_map.132 = f32[512,768]{1,0:T(8,128)} custom-call(s32[3]{0:T(128)} %pad_add_fusion.where_ref.place, bf16[128,2048]{1,0:T(8,128)(2,1)} %collective-permute-done.8.q0, bf16[128,2048]{1,0:T(8,128)(2,1)} %collective-permute-done.9.q1, bf16[128,2048]{1,0:T(8,128)(2,1)} %collective-permute-done.11.q2, bf16[128,2048]{1,0:T(8,128)(2,1)} %copy-done.18, ...), custom_call_target="tpu_custom_call" | custom-call | flops 1 | bytes 1 | tf_op jit(solution)/shard_map/pallas_call | solution.py:164
  89.3 1.5 collective-permute-start.18
  90.8 1.2 collective-permute-done.7
  93.0 3.5 %collective-permute-start.10 = (f32[1,1408]{1,0:T(1,128)S(1)}, f32[1,1408]{1,0:T(1,128)S(1)}, u32[]{:S(2)}, u32[]{:S(2)}) collective-permute-start(f32[1,1408]{1,0:T(1,128)S(1)} %add.110), channel_id=1, source_target_pairs={{0,4},{4,0},{8,12},{12,8},{1,5},{5,1},{9,13},{13,9},{2,6},{6,2},{1... | collective-permute-start | bytes 16904 | tf_op jit(solution)/shard_map/ppermute | solution.py:292
  96.5 3.3 %collective-permute-done.13 = f16[512,768]{1,0:T(8,128)(2,1)} collective-permute-done((f16[512,768]{1,0:T(8,128)(2,1)}, f16[512,768]{1,0:T(8,128)(2,1)}, u32[]{:S(2)}, u32[]{:S(2)}) %collective-permute-start.13) | collective-permute-done | bytes 786464 | tf_op jit(solution)/shard_map/ppermute | solution.py:336
  99.9 2.7 %add_convert_fusion.2 = f16[512,768]{1,0:T(8,128)(2,1)} fusion(f32[512,768]{1,0:T(8,128)} %shard_map.132, f16[512,768]{1,0:T(8,128)(2,1)} %collective-permute-done.13), kind=kLoop, calls=%fused_computation.4 | loop fusion | flops 1179648 | bytes 3145728 | tf_op jit(solution)/shard_map/convert_element_type | solution.py:333
  104.3 1.9 collective-permute-done.19.q3
  107.0 6.7 %shard_map.133 = f32[512,768]{1,0:T(8,128)} custom-call(s32[3]{0:T(128)} %pad_add_fusion.where_ref.place, bf16[128,2048]{1,0:T(8,128)(2,1)} %collective-permute-done.14.q0, bf16[128,2048]{1,0:T(8,128)(2,1)} %copy-done.16, bf16[128,2048]{1,0:T(8,128)(2,1)} %copy-done.17, bf16[128,2048]{1,0:T(8,128)(2,1)} %copy-done.19, bf16[1024,768]{1,0:T(8,128)(2,1)} %copy-done, ...), custom_call_target="tpu_custom_call" | custom-call | flops 1 | bytes 1 | tf_op jit(solution)/shard_map/pallas_call | solution.py:164
  113.8 3.1 %collective-permute-done.21.wb = bf16[1024,512]{1,0:T(8,128)(2,1)S(1)} collective-permute-done((bf16[1024,512]{1,0:T(8,128)(2,1)S(1)}, bf16[1024,512]{1,0:T(8,128)(2,1)S(1)}, u32[]{:S(2)}, u32[]{:S(2)}) %collective-permute-start.21) | collective-permute-done | bytes 1048608 | tf_op jit(solution)/shard_map/ppermute | solution.py:292
  117.9 5.9 %shard_map.134 = f32[512,512]{1,0:T(8,128)} custom-call(s32[3]{0:T(128)} %pad_add_fusion.where_ref.place, bf16[128,2048]{1,0:T(8,128)(2,1)} %collective-permute-done.2.q0, bf16[128,2048]{1,0:T(8,128)(2,1)} %collective-permute-done.3.q1, bf16[128,2048]{1,0:T(8,128)(2,1)} %copy-done.14, bf16[128,2048]{1,0:T(8,128)(2,1)} %copy-done.15, ...), custom_call_target="tpu_custom_call" | custom-call | flops 1 | bytes 1 | tf_op jit(solution)/shard_map/pallas_call | solution.py:164
  123.8 2.2 convert_element_type.63
  126.0 3.4 %collective-permute-start.22 = (bf16[128,2048]{1,0:T(8,128)(2,1)S(1)}, bf16[128,2048]{1,0:T(8,128)(2,1)S(1)}, u32[]{:S(2)}, u32[]{:S(2)}) collective-permute-start(bf16[128,2048]{1,0:T(8,128)(2,1)S(1)} %collective-permute-done.15.q0), channel_id=1, source_target_pairs={{4,6},{5,7},{6,4},{7,5},{8,10},{9,11},{10,8},{11,9},{20,22},{21,23... | collective-permute-start | bytes 1572872 | tf_op jit(solution)/shard_map/ppermute | solution.py:296
  129.4 1.3 collective-permute-start.25
  130.7 5.9 %shard_map.135 = f32[512,512]{1,0:T(8,128)} custom-call(s32[3]{0:T(128)} %pad_add_fusion.where_ref.place, bf16[128,2048]{1,0:T(8,128)(2,1)} %collective-permute-done.8.q0, bf16[128,2048]{1,0:T(8,128)(2,1)} %collective-permute-done.9.q1, bf16[128,2048]{1,0:T(8,128)(2,1)} %collective-permute-done.11.q2, bf16[128,2048]{1,0:T(8,128)(2,1)} %copy-done.18, ...), custom_call_target="tpu_custom_call" | custom-call | flops 1 | bytes 1 | tf_op jit(solution)/shard_map/pallas_call | solution.py:164
  136.6 3.9 %collective-permute-done.22.q2 = bf16[128,2048]{1,0:T(8,128)(2,1)S(1)} collective-permute-done((bf16[128,2048]{1,0:T(8,128)(2,1)S(1)}, bf16[128,2048]{1,0:T(8,128)(2,1)S(1)}, u32[]{:S(2)}, u32[]{:S(2)}) %collective-permute-start.22) | collective-permute-done | bytes 524320 | tf_op jit(solution)/shard_map/ppermute | solution.py:296
  140.5 1.9 collective-permute-start.23
  142.4 2.4 collective-permute-start.24
  144.8 3.0 %collective-permute-start.20 = (f16[512,768]{1,0:T(8,128)(2,1)S(1)}, f16[512,768]{1,0:T(8,128)(2,1)}, u32[]{:S(2)}, u32[]{:S(2)}) collective-permute-start(f16[512,768]{1,0:T(8,128)(2,1)S(1)} %copy-done.23), channel_id=1, source_target_pairs={{4,8},{8,4},{5,9},{9,5},{6,10},{10,6},{7,11},{11,7},{20,24},{24,20... | collective-permute-start | bytes 2359304 | tf_op jit(solution)/shard_map/ppermute | solution.py:339
  148.0 1.3 collective-permute-start.27
  150.1 6.7 %shard_map.136 = f32[512,768]{1,0:T(8,128)} custom-call(s32[3]{0:T(128)} %pad_add_fusion.where_ref.place, bf16[128,2048]{1,0:T(8,128)(2,1)} %copy-done.13, bf16[128,2048]{1,0:T(8,128)(2,1)} %copy-done.21, bf16[128,2048]{1,0:T(8,128)(2,1)} %copy-done.20, bf16[128,2048]{1,0:T(8,128)(2,1)} %copy-done.22, bf16[1024,768]{1,0:T(8,128)(2,1)} %copy-done, ...), custom_call_target="tpu_custom_call" | custom-call | flops 1 | bytes 1 | tf_op jit(solution)/shard_map/pallas_call | solution.py:164
  156.9 1.9 add_convert_fusion.1
  158.8 7.7 %collective-permute-done.20 = f16[512,768]{1,0:T(8,128)(2,1)} collective-permute-done((f16[512,768]{1,0:T(8,128)(2,1)S(1)}, f16[512,768]{1,0:T(8,128)(2,1)}, u32[]{:S(2)}, u32[]{:S(2)}) %collective-permute-start.20) | collective-permute-done | bytes 786464 | tf_op jit(solution)/shard_map/ppermute | solution.py:339
  166.5 2.3 add_convert_fusion
  168.8 5.9 %shard_map.137 = f32[512,512]{1,0:T(8,128)} custom-call(s32[3]{0:T(128)} %pad_add_fusion.where_ref.place, bf16[128,2048]{1,0:T(8,128)(2,1)} %collective-permute-done.14.q0, bf16[128,2048]{1,0:T(8,128)(2,1)} %copy-done.16, bf16[128,2048]{1,0:T(8,128)(2,1)} %copy-done.17, bf16[128,2048]{1,0:T(8,128)(2,1)} %copy-done.19, ...), custom_call_target="tpu_custom_call" | custom-call | flops 1 | bytes 1 | tf_op jit(solution)/shard_map/pallas_call | solution.py:164
  175.3 1.4 shard_map.138
  176.7 6.0 %shard_map.139 = f32[512,512]{1,0:T(8,128)} custom-call(s32[3]{0:T(128)} %pad_add_fusion.where_ref.place, bf16[128,2048]{1,0:T(8,128)(2,1)} %copy-done.13, bf16[128,2048]{1,0:T(8,128)(2,1)} %copy-done.21, bf16[128,2048]{1,0:T(8,128)(2,1)} %copy-done.20, bf16[128,2048]{1,0:T(8,128)(2,1)} %copy-done.22, bf16[1024,512]{1,0:T(8,128)(2,1)} %get-tuple-element.125.wa, ...), custom_call_target="tpu_custom_call" | custom-call | flops 1 | bytes 1 | tf_op jit(solution)/shard_map/pallas_call | solution.py:164
  183.7 1.4 collective-permute-start.30
  185.1 1.6 collective-permute-start.28
  186.7 6.0 %shard_map.140 = f32[512,512]{1,0:T(8,128)} custom-call(s32[3]{0:T(128)} %pad_add_fusion.where_ref.place, bf16[512,8192]{1,0:T(8,128)(2,1)} %q3.1, bf16[512,8192]{1,0:T(8,128)(2,1)} %q3.1, bf16[512,8192]{1,0:T(8,128)(2,1)} %q3.1, bf16[512,8192]{1,0:T(8,128)(2,1)} %q3.1, bf16[1024,512]{1,0:T(8,128)(2,1)} %get-tuple-element.125.wa, bf16[1024,512]{1,0:T(8,128)(2,1)} %copy-done.3), custom_call_target="tpu_custom_call" | custom-call | flops 1 | bytes 1 | tf_op jit(solution)/shard_map/pallas_call | solution.py:164
  192.7 2.7 %collective-permute-start.33 = (f16[512,768]{1,0:T(8,128)(2,1)}, f16[512,768]{1,0:T(8,128)(2,1)}, u32[]{:S(2)}, u32[]{:S(2)}) collective-permute-start(f16[512,768]{1,0:T(8,128)(2,1)} %add_convert_fusion), channel_id=1, source_target_pairs={{0,4},{4,0},{8,12},{12,8},{1,5},{5,1},{9,13},{13,9},{2,6},{6,2},{1... | collective-permute-start | bytes 2359304 | tf_op jit(solution)/shard_map/ppermute | solution.py:292
  195.3 2.8 %collective-permute-start.34 = (f16[512,768]{1,0:T(8,128)(2,1)S(1)}, f16[512,768]{1,0:T(8,128)(2,1)}, u32[]{:S(2)}, u32[]{:S(2)}) collective-permute-start(f16[512,768]{1,0:T(8,128)(2,1)S(1)} %add_convert_fusion.1), channel_id=1, source_target_pairs={{4,8},{8,4},{5,9},{9,5},{6,10},{10,6},{7,11},{11,7},{20,24},{24,20... | collective-permute-start | bytes 2359304 | tf_op jit(solution)/shard_map/ppermute | solution.py:339
  198.7 3.0 %collective-permute-start.29 = (f16[512,512]{1,0:T(8,128)(2,1)}, f16[512,512]{1,0:T(8,128)(2,1)}, u32[]{:S(2)}, u32[]{:S(2)}) collective-permute-start(f16[512,512]{1,0:T(8,128)(2,1)} %add_convert_fusion.5), channel_id=1, source_target_pairs={{4,8},{8,4},{5,9},{9,5},{6,10},{10,6},{7,11},{11,7},{20,24},{24,20... | collective-permute-start | bytes 1572872 | tf_op jit(solution)/shard_map/ppermute | solution.py:339
  201.7 1.4 shard_map.141
  203.1 1.2 fusion.1
  207.9 19.8 %collective-permute-done.29 = f16[512,512]{1,0:T(8,128)(2,1)} collective-permute-done((f16[512,512]{1,0:T(8,128)(2,1)}, f16[512,512]{1,0:T(8,128)(2,1)}, u32[]{:S(2)}, u32[]{:S(2)}) %collective-permute-start.29) | collective-permute-done | bytes 524320 | tf_op jit(solution)/shard_map/ppermute | solution.py:339
  227.7 2.0 add_convert_fusion.3
  229.7 2.8 %collective-permute-start.32 = (f16[512,512]{1,0:T(8,128)(2,1)}, f16[512,512]{1,0:T(8,128)(2,1)}, u32[]{:S(2)}, u32[]{:S(2)}) collective-permute-start(f16[512,512]{1,0:T(8,128)(2,1)} %add_convert_fusion.4), channel_id=1, source_target_pairs={{4,8},{8,4},{5,9},{9,5},{6,10},{10,6},{7,11},{11,7},{20,24},{24,20... | collective-permute-start | bytes 1572872 | tf_op jit(solution)/shard_map/ppermute | solution.py:339
  232.6 2.6 %multiply_convert_fusion.packed = bf16[512,768]{1,0:T(8,128)(2,1)} fusion(f16[512,768]{1,0:T(8,128)(2,1)} %collective-permute-done.34, f32[512,768]{1,0:T(8,128)S(1)} %copy-done.5, f16[512,768]{1,0:T(8,128)(2,1)} %collective-permute-done.33, f32[768]{0:T(1024)S(1)} %reduce), kind=kLoop, calls=%fused_computation.1 | loop fusion | flops 2359296 | bytes 3935232 | tf_op jit(solution)/shard_map/convert_element_type | solution.py:462
  235.2 4.8 %shard_map.142 = (bf16[512,1024]{1,0:T(8,128)(2,1)}, bf16[512,128]{1,0:T(8,128)(2,1)}, bf16[512,128]{1,0:T(8,128)(2,1)}) custom-call(s32[3]{0:T(128)} %pad_add_fusion.where_ref.place, s32[1,8]{1,0:T(1,128)} %lengths.3, bf16[512,768]{1,0:T(8,128)(2,1)} %multiply_convert_fusion.packed), custom_call_target="tpu_custom_call" | custom-call | flops 1 | bytes 1 | tf_op jit(solution)/shard_map/pallas_call | solution.py:248
  240.0 2.5 %collective-permute-done.31 = f16[512,512]{1,0:T(8,128)(2,1)} collective-permute-done((f16[512,512]{1,0:T(8,128)(2,1)}, f16[512,512]{1,0:T(8,128)(2,1)}, u32[]{:S(2)}, u32[]{:S(2)}) %collective-permute-start.31) | collective-permute-done | bytes 524320 | tf_op jit(solution)/shard_map/ppermute | solution.py:292
  242.6 1.9 collective-permute-done.32
  244.5 2.2 multiply_convert_fusion.1.packed
  246.7 4.8 %shard_map.143 = bf16[512,1024]{1,0:T(8,128)(2,1)} custom-call(s32[3]{0:T(128)} %pad_add_fusion.where_ref.place, s32[1,8]{1,0:T(1,128)} %lengths.3, bf16[512,512]{1,0:T(8,128)(2,1)} %multiply_convert_fusion.1.packed, bf16[512,128]{1,0:T(8,128)(2,1)} %get-tuple-element.171.refs_0_, ...), custom_call_target="tpu_custom_call", output_to_operand_aliasing={{}: (5, {})} | custom-call | flops 1 | bytes 1 | tf_op jit(solution)/shard_map/pallas_call | solution.py:248
  (113 shorter events, 20.6 us)
Async XLA Ops:
  0.6 3.7 %copy-start.4 = (bf16[1024,1024]{1,0:T(8,128)(2,1)S(1)}, bf16[1024,1024]{1,0:T(8,128)(2,1)}, u32[]{:S(2)}) copy-start(bf16[1024,1024]{1,0:T(8,128)(2,1)} %wq.2) | copy-start | bytes 6291460
  2.7 2.8 %copy-start.11 = (bf16[1024,128]{1,0:T(8,128)(2,1)S(1)}, bf16[1024,128]{1,0:T(8,128)(2,1)}, u32[]{:S(2)}) copy-start(bf16[1024,128]{1,0:T(8,128)(2,1)} %wk.3) | copy-start | bytes 786436
  2.7 2.8 %copy-start.12 = (bf16[1024,128]{1,0:T(8,128)(2,1)S(1)}, bf16[1024,128]{1,0:T(8,128)(2,1)}, u32[]{:S(2)}) copy-start(bf16[1024,128]{1,0:T(8,128)(2,1)} %wv.3) | copy-start | bytes 786436
  2.7 17.8 %collective-permute-start.2 = (bf16[128,2048]{1,0:T(8,128)(2,1)}, bf16[128,2048]{1,0:T(8,128)(2,1)}, u32[]{:S(2)}, u32[]{:S(2)}) collective-permute-start(bf16[128,2048]{1,0:T(8,128)(2,1)} %pad_maximum_fusion.1), channel_id=1, source_target_pairs={{0,12},{12,0},{1,13},{13,1},{2,14},{14,2},{3,15},{15,3},{16,28},{2... | collective-permute-start | bytes 1572872 | tf_op jit(solution)/shard_map/ppermute | solution.py:349
  5.6 5.8 %copy-start = (bf16[1024,768]{1,0:T(8,128)(2,1)}, bf16[1024,768]{1,0:T(8,128)(2,1)S(1)}, u32[]{:S(2)}) copy-start(bf16[1024,768]{1,0:T(8,128)(2,1)S(1)} %pad_maximum_fusion.wa) | copy-start | bytes 4718596
  5.6 50.8 %collective-permute-start.6 = (bf16[1024,768]{1,0:T(8,128)(2,1)S(1)}, bf16[1024,768]{1,0:T(8,128)(2,1)S(1)}, u32[]{:S(2)}, u32[]{:S(2)}) collective-permute-start(bf16[1024,768]{1,0:T(8,128)(2,1)S(1)} %pad_maximum_fusion.wa), channel_id=1, source_target_pairs={{0,16},{16,0},{1,17},{17,1},{2,18},{18,2},{3,19},{19,3},{4,20},{20... | collective-permute-start | bytes 4718600 | tf_op jit(solution)/shard_map/ppermute | solution.py:292
  10.3 3.0 %collective-permute-start = (f32[3,1024]{1,0:T(4,128)}, f32[3,1024]{1,0:T(4,128)S(1)}, u32[]{:S(2)}, u32[]{:S(2)}) collective-permute-start(f32[3,1024]{1,0:T(4,128)} %shard_map.128), channel_id=1, source_target_pairs={{0,1},{1,0},{2,3},{3,2},{4,5},{5,4},{6,7},{7,6},{8,9},{9,8},{10,11... | collective-permute-start | bytes 36872 | tf_op jit(solution)/shard_map/ppermute | solution.py:292
  10.3 3.0 %copy-start.24 = (f32[3,1024]{1,0:T(4,128)S(1)}, f32[3,1024]{1,0:T(4,128)}, u32[]{:S(2)}) copy-start(f32[3,1024]{1,0:T(4,128)} %shard_map.128) | copy-start | bytes 36868
  13.3 3.8 %collective-permute-start.1 = (f32[3,1024]{1,0:T(4,128)S(1)}, f32[3,1024]{1,0:T(4,128)S(1)}, u32[]{:S(2)}, u32[]{:S(2)}) collective-permute-start(f32[3,1024]{1,0:T(4,128)S(1)} %add.104), channel_id=1, source_target_pairs={{0,2},{1,3},{2,0},{3,1},{4,6},{5,7},{6,4},{7,5},{8,10},{9,11},{10,... | collective-permute-start | bytes 36872 | tf_op jit(solution)/shard_map/ppermute | solution.py:292
  20.5 8.6 %collective-permute-start.3 = (bf16[128,2048]{1,0:T(8,128)(2,1)}, bf16[128,2048]{1,0:T(8,128)(2,1)}, u32[]{:S(2)}, u32[]{:S(2)}) collective-permute-start(bf16[128,2048]{1,0:T(8,128)(2,1)} %collective-permute-done.2.q0), channel_id=1, source_target_pairs={{0,1},{1,0},{2,3},{3,2},{12,13},{13,12},{14,15},{15,14},{16,17},{1... | collective-permute-start | bytes 1572872 | tf_op jit(solution)/shard_map/ppermute | solution.py:296
  21.9 7.2 %collective-permute-start.4 = (bf16[128,2048]{1,0:T(8,128)(2,1)}, bf16[128,2048]{1,0:T(8,128)(2,1)S(1)}, u32[]{:S(2)}, u32[]{:S(2)}) collective-permute-start(bf16[128,2048]{1,0:T(8,128)(2,1)} %collective-permute-done.2.q0), channel_id=1, source_target_pairs={{0,2},{1,3},{2,0},{3,1},{12,14},{13,15},{14,12},{15,13},{16,18},{1... | collective-permute-start | bytes 1572872 | tf_op jit(solution)/shard_map/ppermute | solution.py:296
  22.6 29.6 %collective-permute-start.8 = (bf16[128,2048]{1,0:T(8,128)(2,1)}, bf16[128,2048]{1,0:T(8,128)(2,1)}, u32[]{:S(2)}, u32[]{:S(2)}) collective-permute-start(bf16[128,2048]{1,0:T(8,128)(2,1)} %pad_maximum_fusion.2), channel_id=1, source_target_pairs={{0,8},{4,12},{8,0},{12,4},{1,9},{5,13},{9,1},{13,5},{2,10},{6,14},... | collective-permute-start | bytes 1572872 | tf_op jit(solution)/shard_map/ppermute | solution.py:292
  29.2 26.5 %copy-start.14 = (bf16[128,2048]{1,0:T(8,128)(2,1)}, bf16[128,2048]{1,0:T(8,128)(2,1)S(1)}, u32[]{:S(2)}) copy-start(bf16[128,2048]{1,0:T(8,128)(2,1)S(1)} %collective-permute-done.4.q2) | copy-start | bytes 1572868
  29.2 26.5 %collective-permute-start.5 = (bf16[128,2048]{1,0:T(8,128)(2,1)S(1)}, bf16[128,2048]{1,0:T(8,128)(2,1)S(1)}, u32[]{:S(2)}, u32[]{:S(2)}) collective-permute-start(bf16[128,2048]{1,0:T(8,128)(2,1)S(1)} %collective-permute-done.4.q2), channel_id=1, source_target_pairs={{0,1},{1,0},{2,3},{3,2},{12,13},{13,12},{14,15},{15,14},{16,17},{1... | collective-permute-start | bytes 1572872 | tf_op jit(solution)/shard_map/ppermute | solution.py:296
  52.3 13.5 %collective-permute-start.11 = (bf16[128,2048]{1,0:T(8,128)(2,1)}, bf16[128,2048]{1,0:T(8,128)(2,1)}, u32[]{:S(2)}, u32[]{:S(2)}) collective-permute-start(bf16[128,2048]{1,0:T(8,128)(2,1)} %collective-permute-done.8.q0), channel_id=1, source_target_pairs={{0,2},{1,3},{2,0},{3,1},{4,6},{5,7},{6,4},{7,5},{8,10},{9,11},{10,... | collective-permute-start | bytes 1572872 | tf_op jit(solution)/shard_map/ppermute | solution.py:296
  52.8 14.4 %collective-permute-start.14 = (bf16[128,2048]{1,0:T(8,128)(2,1)}, bf16[128,2048]{1,0:T(8,128)(2,1)}, u32[]{:S(2)}, u32[]{:S(2)}) collective-permute-start(bf16[128,2048]{1,0:T(8,128)(2,1)} %pad_maximum_fusion.3), channel_id=1, source_target_pairs={{0,4},{4,0},{8,12},{12,8},{1,5},{5,1},{9,13},{13,9},{2,6},{6,2},{1... | collective-permute-start | bytes 1572872 | tf_op jit(solution)/shard_map/ppermute | solution.py:292
  55.6 25.1 %collective-permute-start.9 = (bf16[128,2048]{1,0:T(8,128)(2,1)}, bf16[128,2048]{1,0:T(8,128)(2,1)}, u32[]{:S(2)}, u32[]{:S(2)}) collective-permute-start(bf16[128,2048]{1,0:T(8,128)(2,1)} %collective-permute-done.8.q0), channel_id=1, source_target_pairs={{0,1},{1,0},{2,3},{3,2},{4,5},{5,4},{6,7},{7,6},{8,9},{9,8},{10,11... | collective-permute-start | bytes 1572872 | tf_op jit(solution)/shard_map/ppermute | solution.py:296
  55.6 0.8 copy-start.15
  56.5 1.1 copy-start.1
  65.8 14.9 %collective-permute-start.12 = (bf16[128,2048]{1,0:T(8,128)(2,1)}, bf16[128,2048]{1,0:T(8,128)(2,1)S(1)}, u32[]{:S(2)}, u32[]{:S(2)}) collective-permute-start(bf16[128,2048]{1,0:T(8,128)(2,1)} %collective-permute-done.11.q2), channel_id=1, source_target_pairs={{0,1},{1,0},{2,3},{3,2},{4,5},{5,4},{6,7},{7,6},{8,9},{9,8},{10,11... | collective-permute-start | bytes 1572872 | tf_op jit(solution)/shard_map/ppermute | solution.py:296
  67.2 21.1 %collective-permute-start.15 = (bf16[128,2048]{1,0:T(8,128)(2,1)}, bf16[128,2048]{1,0:T(8,128)(2,1)S(1)}, u32[]{:S(2)}, u32[]{:S(2)}) collective-permute-start(bf16[128,2048]{1,0:T(8,128)(2,1)} %pad_maximum_fusion.1), channel_id=1, source_target_pairs={{4,8},{8,4},{5,9},{9,5},{6,10},{10,6},{7,11},{11,7},{20,24},{24,20... | collective-permute-start | bytes 1572872 | tf_op jit(solution)/shard_map/ppermute | solution.py:339
  79.3 9.1 %copy-start.25 = (f32[1,1408]{1,0:T(1,128)S(1)}, f32[1,1408]{1,0:T(1,128)}, u32[]{:S(2)}) copy-start(f32[1,1408]{1,0:T(1,128)} %shard_map.129) | copy-start | bytes 16900
  79.3 12.8 %copy-start.2 = (bf16[1024,512]{1,0:T(8,128)(2,1)S(1)}, bf16[1024,512]{1,0:T(8,128)(2,1)}, u32[]{:S(2)}) copy-start(bf16[1024,512]{1,0:T(8,128)(2,1)} %get-tuple-element.125.wa) | copy-start | bytes 3145732
  79.3 20.6 %collective-permute-start.13 = (f16[512,768]{1,0:T(8,128)(2,1)}, f16[512,768]{1,0:T(8,128)(2,1)}, u32[]{:S(2)}, u32[]{:S(2)}) collective-permute-start(f16[512,768]{1,0:T(8,128)(2,1)} %convert_element_type.60), channel_id=1, source_target_pairs={{0,4},{12,8},{1,5},{13,9},{2,6},{14,10},{3,7},{15,11},{16,20},{28,... | collective-permute-start | bytes 2359304 | tf_op jit(solution)/shard_map/ppermute | solution.py:336
  80.7 0.8 copy-start.18
  88.3 52.2 %copy-start.13 = (bf16[128,2048]{1,0:T(8,128)(2,1)}, bf16[128,2048]{1,0:T(8,128)(2,1)S(1)}, u32[]{:S(2)}) copy-start(bf16[128,2048]{1,0:T(8,128)(2,1)S(1)} %collective-permute-done.15.q0) | copy-start | bytes 1572868
  88.3 8.2 %collective-permute-start.16 = (bf16[128,2048]{1,0:T(8,128)(2,1)}, bf16[128,2048]{1,0:T(8,128)(2,1)S(1)}, u32[]{:S(2)}, u32[]{:S(2)}) collective-permute-start(bf16[128,2048]{1,0:T(8,128)(2,1)} %collective-permute-done.14.q0), channel_id=1, source_target_pairs={{0,1},{1,0},{2,3},{3,2},{4,5},{5,4},{6,7},{7,6},{8,9},{9,8},{10,11... | collective-permute-start | bytes 1572872 | tf_op jit(solution)/shard_map/ppermute | solution.py:296
  88.4 3.7 %collective-permute-start.7 = (f32[1,1408]{1,0:T(1,128)S(1)}, f32[1,1408]{1,0:T(1,128)S(1)}, u32[]{:S(2)}, u32[]{:S(2)}) collective-permute-start(f32[1,1408]{1,0:T(1,128)S(1)} %copy-done.25), channel_id=1, source_target_pairs={{0,16},{16,0},{1,17},{17,1},{2,18},{18,2},{3,19},{19,3},{4,20},{20... | collective-permute-start | bytes 16904 | tf_op jit(solution)/shard_map/ppermute | solution.py:292
  89.3 14.2 %collective-permute-start.18 = (bf16[128,2048]{1,0:T(8,128)(2,1)}, bf16[128,2048]{1,0:T(8,128)(2,1)S(1)}, u32[]{:S(2)}, u32[]{:S(2)}) collective-permute-start(bf16[128,2048]{1,0:T(8,128)(2,1)} %collective-permute-done.14.q0), channel_id=1, source_target_pairs={{0,2},{1,3},{2,0},{3,1},{4,6},{5,7},{6,4},{7,5},{8,10},{9,11},{10,... | collective-permute-start | bytes 1572872 | tf_op jit(solution)/shard_map/ppermute | solution.py:296
  92.1 24.8 %collective-permute-start.21 = (bf16[1024,512]{1,0:T(8,128)(2,1)S(1)}, bf16[1024,512]{1,0:T(8,128)(2,1)S(1)}, u32[]{:S(2)}, u32[]{:S(2)}) collective-permute-start(bf16[1024,512]{1,0:T(8,128)(2,1)S(1)} %copy-done.2), channel_id=1, source_target_pairs={{0,16},{16,0},{1,17},{17,1},{2,18},{18,2},{3,19},{19,3},{4,20},{20... | collective-permute-start | bytes 3145736 | tf_op jit(solution)/shard_map/ppermute | solution.py:292
  93.0 9.6 %collective-permute-start.10 = (f32[1,1408]{1,0:T(1,128)S(1)}, f32[1,1408]{1,0:T(1,128)S(1)}, u32[]{:S(2)}, u32[]{:S(2)}) collective-permute-start(f32[1,1408]{1,0:T(1,128)S(1)} %add.110), channel_id=1, source_target_pairs={{0,4},{4,0},{8,12},{12,8},{1,5},{5,1},{9,13},{13,9},{2,6},{6,2},{1... | collective-permute-start | bytes 16904 | tf_op jit(solution)/shard_map/ppermute | solution.py:292
  96.5 6.0 %copy-start.16 = (bf16[128,2048]{1,0:T(8,128)(2,1)}, bf16[128,2048]{1,0:T(8,128)(2,1)S(1)}, u32[]{:S(2)}) copy-start(bf16[128,2048]{1,0:T(8,128)(2,1)S(1)} %collective-permute-done.16.q1) | copy-start | bytes 1572868
  103.5 0.8 copy-start.17
  104.3 1.9 collective-permute-start.19
  106.3 0.8 copy-start.19
  116.9 1.0 copy-start.3
  123.8 5.7 %copy-start.23 = (f16[512,768]{1,0:T(8,128)(2,1)S(1)}, f16[512,768]{1,0:T(8,128)(2,1)}, u32[]{:S(2)}) copy-start(f16[512,768]{1,0:T(8,128)(2,1)} %add_convert_fusion.2) | copy-start | bytes 2359300
  126.0 14.5 %collective-permute-start.22 = (bf16[128,2048]{1,0:T(8,128)(2,1)S(1)}, bf16[128,2048]{1,0:T(8,128)(2,1)S(1)}, u32[]{:S(2)}, u32[]{:S(2)}) collective-permute-start(bf16[128,2048]{1,0:T(8,128)(2,1)S(1)} %collective-permute-done.15.q0), channel_id=1, source_target_pairs={{4,6},{5,7},{6,4},{7,5},{8,10},{9,11},{10,8},{11,9},{20,22},{21,23... | collective-permute-start | bytes 1572872 | tf_op jit(solution)/shard_map/ppermute | solution.py:296
  129.4 27.4 %collective-permute-start.25 = (f16[512,768]{1,0:T(8,128)(2,1)S(1)}, f16[512,768]{1,0:T(8,128)(2,1)}, u32[]{:S(2)}, u32[]{:S(2)}) collective-permute-start(f16[512,768]{1,0:T(8,128)(2,1)S(1)} %copy-done.23), channel_id=1, source_target_pairs={{0,4},{12,8},{1,5},{13,9},{2,6},{14,10},{3,7},{15,11},{16,20},{28,... | collective-permute-start | bytes 2359304 | tf_op jit(solution)/shard_map/ppermute | solution.py:336
  140.5 8.8 %copy-start.20 = (bf16[128,2048]{1,0:T(8,128)(2,1)}, bf16[128,2048]{1,0:T(8,128)(2,1)S(1)}, u32[]{:S(2)}) copy-start(bf16[128,2048]{1,0:T(8,128)(2,1)S(1)} %collective-permute-done.22.q2) | copy-start | bytes 1572868
  140.5 7.5 %collective-permute-start.23 = (bf16[128,2048]{1,0:T(8,128)(2,1)S(1)}, bf16[128,2048]{1,0:T(8,128)(2,1)S(1)}, u32[]{:S(2)}, u32[]{:S(2)}) collective-permute-start(bf16[128,2048]{1,0:T(8,128)(2,1)S(1)} %collective-permute-done.15.q0), channel_id=1, source_target_pairs={{4,5},{5,4},{6,7},{7,6},{8,9},{9,8},{10,11},{11,10},{20,21},{21,20... | collective-permute-start | bytes 1572872 | tf_op jit(solution)/shard_map/ppermute | solution.py:296
  142.4 6.9 %collective-permute-start.24 = (bf16[128,2048]{1,0:T(8,128)(2,1)S(1)}, bf16[128,2048]{1,0:T(8,128)(2,1)S(1)}, u32[]{:S(2)}, u32[]{:S(2)}) collective-permute-start(bf16[128,2048]{1,0:T(8,128)(2,1)S(1)} %collective-permute-done.22.q2), channel_id=1, source_target_pairs={{4,5},{5,4},{6,7},{7,6},{8,9},{9,8},{10,11},{11,10},{20,21},{21,20... | collective-permute-start | bytes 1572872 | tf_op jit(solution)/shard_map/ppermute | solution.py:296
  144.8 21.6 %collective-permute-start.20 = (f16[512,768]{1,0:T(8,128)(2,1)S(1)}, f16[512,768]{1,0:T(8,128)(2,1)}, u32[]{:S(2)}, u32[]{:S(2)}) collective-permute-start(f16[512,768]{1,0:T(8,128)(2,1)S(1)} %copy-done.23), channel_id=1, source_target_pairs={{4,8},{8,4},{5,9},{9,5},{6,10},{10,6},{7,11},{11,7},{20,24},{24,20... | collective-permute-start | bytes 2359304 | tf_op jit(solution)/shard_map/ppermute | solution.py:339
  147.9 26.8 %collective-permute-start.17 = (f32[1,1408]{1,0:T(1,128)S(1)}, f32[1,1408]{1,0:T(1,128)S(1)}, u32[]{:S(2)}, u32[]{:S(2)}) collective-permute-start(f32[1,1408]{1,0:T(1,128)S(1)} %add.112), channel_id=1, source_target_pairs={{0,8},{4,12},{8,0},{12,4},{1,9},{5,13},{9,1},{13,5},{2,10},{6,14},... | collective-permute-start | bytes 16904 | tf_op jit(solution)/shard_map/ppermute | solution.py:292
  148.0 1.3 copy-start.21
  148.0 34.7 %collective-permute-start.27 = (f16[512,512]{1,0:T(8,128)(2,1)}, f16[512,512]{1,0:T(8,128)(2,1)S(1)}, u32[]{:S(2)}, u32[]{:S(2)}) collective-permute-start(f16[512,512]{1,0:T(8,128)(2,1)} %convert_element_type.63), channel_id=1, source_target_pairs={{0,4},{12,8},{1,5},{13,9},{2,6},{14,10},{3,7},{15,11},{16,20},{28,... | collective-permute-start | bytes 1572872 | tf_op jit(solution)/shard_map/ppermute | solution.py:336
  149.3 0.8 copy-start.22
  156.9 9.6 %copy-start.6 = (f32[512,768]{1,0:T(8,128)S(1)}, f32[512,768]{1,0:T(8,128)}, u32[]{:S(2)}) copy-start(f32[512,768]{1,0:T(8,128)} %shard_map.133) | copy-start | bytes 4718596
  176.7 6.0 %collective-permute-start.26 = (f32[1,128]{1,0:T(1,128)}, f32[1,128]{1,0:T(1,128)S(1)}, u32[]{:S(2)}, u32[]{:S(2)}) collective-permute-start(f32[1,128]{1,0:T(1,128)} %get-tuple-element.151), channel_id=1, source_target_pairs={{0,1},{1,0},{2,3},{3,2},{4,5},{5,4},{6,7},{7,6},{8,9},{9,8},{10,11... | collective-permute-start | bytes 1544 | tf_op jit(solution)/shard_map/ppermute | solution.py:292
  176.7 6.0 %copy-start.27 = (f32[1,128]{1,0:T(1,128)S(1)}, f32[1,128]{1,0:T(1,128)}, u32[]{:S(2)}) copy-start(f32[1,128]{1,0:T(1,128)} %get-tuple-element.151) | copy-start | bytes 1540
  176.7 6.0 %copy-start.9 = (f32[512,512]{1,0:T(8,128)S(1)}, f32[512,512]{1,0:T(8,128)}, u32[]{:S(2)}) copy-start(f32[512,512]{1,0:T(8,128)} %shard_map.135) | copy-start | bytes 3145732
  183.7 19.4 %copy-start.26 = (f32[3]{0:T(128)S(1)}, f32[3]{0:T(128)}, u32[]{:S(2)}) copy-start(f32[3]{0:T(128)} %param.17) | copy-start | bytes 40
  183.7 23.2 %copy-start.10 = (f32[512,512]{1,0:T(8,128)S(1)}, f32[512,512]{1,0:T(8,128)}, u32[]{:S(2)}) copy-start(f32[512,512]{1,0:T(8,128)} %shard_map.139) | copy-start | bytes 3145732
  183.7 23.2 %collective-permute-start.30 = (f16[512,512]{1,0:T(8,128)(2,1)}, f16[512,512]{1,0:T(8,128)(2,1)S(1)}, u32[]{:S(2)}, u32[]{:S(2)}) collective-permute-start(f16[512,512]{1,0:T(8,128)(2,1)} %add_convert_fusion.5), channel_id=1, source_target_pairs={{0,4},{12,8},{1,5},{13,9},{2,6},{14,10},{3,7},{15,11},{16,20},{28,... | collective-permute-start | bytes 1572872 | tf_op jit(solution)/shard_map/ppermute | solution.py:336
  185.1 13.1 %collective-permute-start.28 = (f32[1,128]{1,0:T(1,128)S(1)}, f32[1,128]{1,0:T(1,128)S(1)}, u32[]{:S(2)}, u32[]{:S(2)}) collective-permute-start(f32[1,128]{1,0:T(1,128)S(1)} %add.116), channel_id=1, source_target_pairs={{0,2},{1,3},{2,0},{3,1},{4,6},{5,7},{6,4},{7,5},{8,10},{9,11},{10,... | collective-permute-start | bytes 1544 | tf_op jit(solution)/shard_map/ppermute | solution.py:292
  192.7 35.0 %copy-start.8 = (f32[512,512]{1,0:T(8,128)S(1)}, f32[512,512]{1,0:T(8,128)}, u32[]{:S(2)}) copy-start(f32[512,512]{1,0:T(8,128)} %shard_map.137) | copy-start | bytes 3145732
  192.7 39.9 %collective-permute-start.33 = (f16[512,768]{1,0:T(8,128)(2,1)}, f16[512,768]{1,0:T(8,128)(2,1)}, u32[]{:S(2)}, u32[]{:S(2)}) collective-permute-start(f16[512,768]{1,0:T(8,128)(2,1)} %add_convert_fusion), channel_id=1, source_target_pairs={{0,4},{4,0},{8,12},{12,8},{1,5},{5,1},{9,13},{13,9},{2,6},{6,2},{1... | collective-permute-start | bytes 2359304 | tf_op jit(solution)/shard_map/ppermute | solution.py:292
  195.3 37.2 %collective-permute-start.34 = (f16[512,768]{1,0:T(8,128)(2,1)S(1)}, f16[512,768]{1,0:T(8,128)(2,1)}, u32[]{:S(2)}, u32[]{:S(2)}) collective-permute-start(f16[512,768]{1,0:T(8,128)(2,1)S(1)} %add_convert_fusion.1), channel_id=1, source_target_pairs={{4,8},{8,4},{5,9},{9,5},{6,10},{10,6},{7,11},{11,7},{20,24},{24,20... | collective-permute-start | bytes 2359304 | tf_op jit(solution)/shard_map/ppermute | solution.py:339
  198.7 29.0 %collective-permute-start.29 = (f16[512,512]{1,0:T(8,128)(2,1)}, f16[512,512]{1,0:T(8,128)(2,1)}, u32[]{:S(2)}, u32[]{:S(2)}) collective-permute-start(f16[512,512]{1,0:T(8,128)(2,1)} %add_convert_fusion.5), channel_id=1, source_target_pairs={{4,8},{8,4},{5,9},{9,5},{6,10},{10,6},{7,11},{11,7},{20,24},{24,20... | collective-permute-start | bytes 1572872 | tf_op jit(solution)/shard_map/ppermute | solution.py:339
  207.9 24.7 %copy-start.5 = (f32[512,768]{1,0:T(8,128)S(1)}, f32[512,768]{1,0:T(8,128)}, u32[]{:S(2)}) copy-start(f32[512,768]{1,0:T(8,128)} %shard_map.131) | copy-start | bytes 4718596
  229.7 12.9 %collective-permute-start.31 = (f16[512,512]{1,0:T(8,128)(2,1)}, f16[512,512]{1,0:T(8,128)(2,1)}, u32[]{:S(2)}, u32[]{:S(2)}) collective-permute-start(f16[512,512]{1,0:T(8,128)(2,1)} %add_convert_fusion.3), channel_id=1, source_target_pairs={{0,4},{4,0},{8,12},{12,8},{1,5},{5,1},{9,13},{13,9},{2,6},{6,2},{1... | collective-permute-start | bytes 1572872 | tf_op jit(solution)/shard_map/ppermute | solution.py:292
  229.7 14.8 %collective-permute-start.32 = (f16[512,512]{1,0:T(8,128)(2,1)}, f16[512,512]{1,0:T(8,128)(2,1)}, u32[]{:S(2)}, u32[]{:S(2)}) collective-permute-start(f16[512,512]{1,0:T(8,128)(2,1)} %add_convert_fusion.4), channel_id=1, source_target_pairs={{4,8},{8,4},{5,9},{9,5},{6,10},{10,6},{7,11},{11,7},{20,24},{24,20... | collective-permute-start | bytes 1572872 | tf_op jit(solution)/shard_map/ppermute | solution.py:339
  232.5 11.9 %copy-start.7 = (f32[512,512]{1,0:T(8,128)S(1)}, f32[512,512]{1,0:T(8,128)}, u32[]{:S(2)}) copy-start(f32[512,512]{1,0:T(8,128)} %shard_map.140) | copy-start | bytes 3145732

commit v2 on v1

--- a/solution.py
+++ b/solution.py
@@ -124,9 +124,15 @@
     squares[...] = found
 
 
-def state_kernel(widths, tp_count, back, squares, new_q, new_k, new_v, sigmas):
+def state_kernel(widths, tp_count, back, squares, gammas, new_q, new_k, new_v, sigmas, factors):
     sigma = jnp.sqrt(squares[...] + EPSILON)
     sigmas[...] = sigma
+    for i, (start, width) in enumerate(
+        ((2 * widths[1], widths[0]), (0, widths[1]), (widths[1], widths[2]))
+    ):
+        factors[:, start : start + width] = jnp.broadcast_to(
+            gammas[i] / sigma[:, i : i + 1], (1, width)
+        )
     at = 0
     for i, (width, out) in enumerate(zip(widths, (new_q, new_k, new_v))):
         factor = jnp.sqrt(jnp.full((1, 1), width * tp_count, F32)) / sigma[:, i : i + 1]
@@ -135,47 +141,41 @@
 
 
 def whole(kernel, out_shape, *args):
-    return pl.pallas_call(kernel, out_shape=out_shape, cost_estimate=SMALL)(*args)
-
-
-def quarter_product(where, sources, w_own, w_other, index=None):
-    deep, n = w_own.shape
-    step = 512
-    half = deep // step
-    rows = sources[0].shape[0] if index is None else index[0]
-    maps = [lambda k, where: (0, k)] * 4 if index is None else index[1](half)
-
-    def kernel(where_ref, q0, q1, q2, q3, wa, wb, out):
-        k = pl.program_id(0)
-        x = jnp.concatenate([q[...] for q in (q0, q1, q2, q3)], axis=0)
-
-        @pl.when(k == 0)
-        def _():
-            out[...] = jnp.dot(x, wa[...], preferred_element_type=F32)
-
-        @pl.when((k > 0) & (k < half))
-        def _():
-            out[...] += jnp.dot(x, wa[...], preferred_element_type=F32)
-
-        @pl.when(k >= half)
-        def _():
-            out[...] += jnp.dot(x, wb[...], preferred_element_type=F32)
-
+    specs = [
+        pl.BlockSpec(memory_space=pltpu.SMEM if a.ndim == 1 else pltpu.VMEM) for a in args
+    ]
+    return pl.pallas_call(kernel, out_shape=out_shape, in_specs=specs, cost_estimate=SMALL)(*args)
+
+
+def gather_blocks(where, sources, outs, plan):
+    count = len(plan([0, 0, 0]))
+    n = len(sources)
+
+    def kernel(where_ref, *refs):
+        sems = refs[-1]
+        place = [where_ref[i] for i in range(3)]
+        copies = [
+            pltpu.make_async_copy(refs[s].at[at], refs[n + o].at[to], sems.at[i])
+            for i, (s, at, o, to) in enumerate(plan(place))
+        ]
+        for copy in copies:
+            copy.start()
+        for copy in copies:
+            copy.wait()
+
+    anywhere = pl.BlockSpec(memory_space=pl.ANY)
     return pl.pallas_call(
         kernel,
-        out_shape=jax.ShapeDtypeStruct((4 * rows, n), F32),
+        out_shape=outs,
         grid_spec=pltpu.PrefetchScalarGridSpec(
             num_scalar_prefetch=1,
-            grid=(2 * half,),
-            in_specs=[pl.BlockSpec((rows, step), m) for m in maps]
-            + [
-                pl.BlockSpec((step, n), lambda k, where: (jnp.minimum(k, half - 1), 0)),
-                pl.BlockSpec((step, n), lambda k, where: (jnp.maximum(k - half, 0), 0)),
-            ],
-            out_specs=pl.BlockSpec((4 * rows, n), lambda k, where: (0, 0)),
+            grid=(1,),
+            in_specs=[anywhere] * n,
+            out_specs=tuple(pl.BlockSpec(o.shape, lambda i, where: (0, 0)) for o in outs),
+            scratch_shapes=[pltpu.SemaphoreType.DMA((count,))],
         ),
         cost_estimate=SMALL,
-    )(where, *sources, w_own, w_other)
+    )(where, *sources)
 
 
 def context_kernel(first, heads, place, lengths, packed, *refs):
@@ -186,8 +186,8 @@
     rows = packed.shape[0]
     block = rows // 4
     at = 2 * HD if first else 0
-    for j in range(4):
-        here = pl.ds(j * block, block)
+    for i, j in enumerate((0, 2, 1, 3)):
+        here = pl.ds(i * block, block)
         there = pl.ds(pl.multiple_of((place[0] ^ j) * block, block), block)
         if first:
             keys[there, :] = packed[here, :HD]
@@ -261,31 +261,26 @@
 
 
 class Order:
-    def __init__(self):
-        self.last = None
+    def __init__(self, token):
+        self.token = token
 
     def after(self, x):
-        if self.last is None:
-            return x
-        x, self.last = lax.optimization_barrier((x, self.last))
+        x, self.token = lax.optimization_barrier((x, self.token))
         return x
 
-    def note(self, x):
-        self.last = x
-        return x
+    note = after
 
 
 def line_body(tokens, doc_lengths, w_query, w_key, w_value, u_query, u_key, u_value, gammas):
-    tok_rows = tokens.shape[0]
     deep, q_width = w_query.shape
     kv_width = w_key.shape[1]
     widths = (q_width, kv_width, kv_width)
     reps, line, tp_count = lax.axis_size("rep"), lax.axis_size("fsdp"), lax.axis_size("tp")
     rep, slot, place = lax.axis_index("rep"), lax.axis_index("fsdp"), lax.axis_index("tp")
-    quarter = tok_rows // tp_count
     send = lax.ppermute
+    where = jnp.stack([place, rep, slot]).astype(jnp.int32)
     ends, mids, everyone = (0, line - 1), (1, line - 2), tuple(range(line))
-    order = Order()
+    order = Order(doc_lengths)
     after, note = order.after, order.note
 
     def swap(x, axis, mask, size):
@@ -295,42 +290,38 @@
         pairs = [(s * tp_count + i, s * tp_count + (i ^ mask)) for s in who for i in range(tp_count)]
         return send(x, ("fsdp", "tp"), pairs)
 
-    def cut(source, row, mask, rows):
-        return jnp.concatenate(
-            [
-                lax.dynamic_slice(
-                    source, (row, ((rep ^ r) * line + (slot ^ mask)) * deep), (rows, deep)
+    quarter = tokens.shape[0] // tp_count
+
+    def slab(source, mask, out, flips):
+        def plan(at):
+            return [
+                (
+                    source,
+                    (
+                        pl.ds(pl.multiple_of((at[0] ^ flip) * quarter, quarter), quarter),
+                        pl.ds(
+                            pl.multiple_of(((at[1] ^ r) * line + (at[2] ^ mask)) * deep, deep), deep
+                        ),
+                    ),
+                    out,
+                    (pl.ds(j * quarter, quarter), pl.ds(r * deep, deep)),
                 )
+                for j, flip in enumerate(flips)
                 for r in range(reps)
-            ],
-            axis=1,
-        )
-
-    def product(parts, c):
-        parts = after(tuple(parts))
-        return note(quarter_product(where, parts, own_w[c], other_w[c]))
-
-    def own_product(c):
-        def maps(half):
-            def one(j):
-                def index(k, where):
-                    column = ((where[1] ^ (k // half)) * line + where[2]) * half + k % half
-                    return (where[0] ^ j, column)
-
-                return index
-
-            return [one(j) for j in range(tp_count)]
-
-        source = after(tokens)
-        return note(
-            quarter_product(where, [source] * 4, own_w[c], other_w[c], (quarter, maps))
+            ]
+
+        return plan
+
+    def piece(rows, columns):
+        return jax.ShapeDtypeStruct((rows, columns), BF16)
+
+    def product(x, w):
+        return jnp.dot(x[:, :deep], w[0], preferred_element_type=F32) + jnp.dot(
+            x[:, deep:], w[1], preferred_element_type=F32
         )
 
     def arrived(x):
-        return note(after(x))
-
-    def joined(p, x):
-        return note((p + after(x).astype(F32)).astype(HALF))
+        return note(x)
 
     def out(x):
         return send(x, "fsdp", [(0, 1), (3, 2)])
@@ -338,39 +329,54 @@
     def across(x):
         return send(x, "fsdp", [(1, 2), (2, 1)])
 
-    where = jnp.stack([place, rep, slot]).astype(jnp.int32)
     split = q_width // 2
+    wide = 2 * kv_width + split
     total = sum(widths)
     row = jax.ShapeDtypeStruct((1, total), F32)
     lanes = jax.ShapeDtypeStruct((1, 128), F32)
-    other_w = [None, None]
-
-    mine = note(cut(tokens, place * quarter, 3, quarter))
+
+    every = pl.ds(0, deep)
+    own_w = [None, None]
+    mine, own_w[0] = note(
+        gather_blocks(
+            where,
+            (tokens, w_key, w_value, w_query),
+            (piece(quarter, reps * deep), piece(deep, wide)),
+            lambda at: slab(0, 3, 0, (0,))(at)
+            + [
+                (1, (every, pl.ds(0, kv_width)), 1, (every, pl.ds(0, kv_width))),
+                (2, (every, pl.ds(0, kv_width)), 1, (every, pl.ds(kv_width, kv_width))),
+                (3, (every, pl.ds(0, split)), 1, (every, pl.ds(2 * kv_width, split))),
+            ],
+        )
+    )
     x3e = send(mine, "fsdp", [(0, 3), (3, 0)])
-    own_w = [
-        note(jnp.concatenate([after(w_key), w_value, w_query[:, :split]], axis=1)),
-        w_query[:, split:],
-    ]
-    other_w[0] = swap(own_w[0], "rep", 1, reps)
+    other_w = [swap(own_w[0], "rep", 1, reps), None]
+    x2, x1, own_w[1] = note(
+        gather_blocks(
+            after(where),
+            (tokens, w_query),
+            (piece(quarter, reps * deep), piece(quarter, reps * deep), piece(deep, split)),
+            lambda at: slab(0, 2, 0, (0,))(at)
+            + slab(0, 1, 1, (0,))(at)
+            + [(1, (every, pl.ds(split, split)), 2, (every, pl.ds(0, split)))],
+        )
+    )
+    x2 = swap(x2, "fsdp", 2, line)
     img = note(
         whole(
             image_kernel,
             jax.ShapeDtypeStruct((3, deep), F32),
-            after(w_query),
+            w_query,
             w_key,
             w_value,
-            u_query[None],
+            after(u_query[None] + 0.0),
             u_key[None],
             u_value[None],
         )
     )
-    img_c = swap(img, "tp", 1, tp_count)
-    x2 = note(cut(after(tokens), place * quarter, 2, quarter))
-    img = note(img + after(img_c))
-    img_y = swap(img, "tp", 2, tp_count)
-    x2 = swap(after(x2), "fsdp", 2, line)
-    x1 = note(cut(after(tokens), place * quarter, 1, quarter))
-    img = note(img + after(img_y))
+    img = note(img + swap(img, "tp", 1, tp_count))
+    img = note(img + swap(img, "tp", 2, tp_count))
     back = note(
         whole(
             back_kernel,
@@ -378,91 +384,97 @@
             w_query,
             w_key,
             w_value,
-            after(img),
-        )
-    )
+            img,
+        )
+    )
+    back_x = swap(back, "rep", 1, reps)
+
+    def joint(a, b):
+        return note(jnp.concatenate([a, after(b)], axis=0))
+
+    def joined(p, x):
+        return note((p + after(x).astype(F32)).astype(HALF))
+
+    def summed(x, axis, size):
+        parts = [swap(x, axis, mask, size) for mask in (1, 2, 3)]
+        return lambda: note((x + after(parts[0])) + (parts[1] + parts[2]))
+
     x3e = arrived(x3e)
-    x3e_far = swap_tp(x3e, 2, ends)
-    x3e_near = swap_tp(x3e, 1, ends)
+    y3e = swap_tp(x3e, 2, ends)
+    x2 = arrived(x2)
+    y2 = swap_tp(x2, 2, everyone)
     x1 = swap(after(x1), "fsdp", 1, line)
-    x3e_near = arrived(x3e_near)
-    x3e_far = arrived(x3e_far)
-    parts3e = (x3e, x3e_near, x3e_far, arrived(swap_tp(x3e_far, 1, ends)))
-    other_w[0] = arrived(other_w[0])
-    v = note(product(parts3e, 0).astype(HALF))
-    a3 = out(v)
-    back_x = swap(after(back), "rep", 1, reps)
-    x2 = arrived(x2)
-    x2_far = swap_tp(x2, 2, everyone)
-    x2_near = arrived(swap_tp(x2, 1, everyone))
+    x3m = across(after(mine))
+    rows0 = note(
+        gather_blocks(
+            after(where),
+            (tokens,),
+            (piece(tp_count * quarter, reps * deep),),
+            slab(0, 0, 0, (0, 2, 1, 3)),
+        )[0]
+    )
+    pair = joint(x3e, y3e)
+    c3e = swap_tp(pair, 1, ends)
+    pair2 = joint(x2, y2)
+    c2 = swap_tp(pair2, 1, everyone)
+    w = [(own_w[0], arrived(other_w[0])), None]
     back = note(back + after(back_x))
-    back_z = swap(back, "fsdp", 1, line)
-    other_w[1] = swap(after(own_w[1]), "rep", 1, reps)
-    x1 = arrived(x1)
-    x3m = across(after(mine))
-    p0 = [own_product(0), None]
-    x2_far = arrived(x2_far)
-    x1_far = swap_tp(after(x1), 2, everyone)
-    parts2 = (x2, x2_near, x2_far, arrived(swap_tp(x2_far, 1, everyone)))
-    p2 = product(parts2, 0)
-    x3m = arrived(x3m)
-    x1_near = arrived(swap_tp(after(x1), 1, everyone))
-    v = joined(p2, a3)
-    a2e, a2m = out(v), across(v)
-    back = note(back + after(back_z))
-    back_z = swap(back, "fsdp", 2, line)
-    x1_far = arrived(x1_far)
-    parts1 = (x1, x1_near, x1_far, arrived(swap_tp(x1_far, 1, everyone)))
-    p1 = product(parts1, 0)
-    other_w[1] = arrived(other_w[1])
-    v = note(product(parts3e, 1).astype(HALF))
-    a3 = out(v)
-    x3m_far = swap_tp(after(x3m), 2, mids)
-    p2 = product(parts2, 1)
-    x3m_far = arrived(x3m_far)
-    x3m_near = swap_tp(after(x3m), 1, mids)
-    x3m_last = swap_tp(x3m_far, 1, mids)
-    parts3 = (x3m, arrived(x3m_near), x3m_far, arrived(x3m_last))
-    p3 = product(parts3, 0)
-    v = joined(p3, a2e)
-    a1m = [across(v), None]
-    v = joined(p1, a2m)
-    a1p = [swap(v, "fsdp", 1, line), None]
-    p1 = product(parts1, 1)
-    back = note(back + after(back_z))
-    back, squares = note(whole(functools.partial(length_kernel, widths), (row, lanes), back))
-    squares_c = swap(squares, "tp", 1, tp_count)
-    p3 = product(parts3, 1)
-    squares = note(squares + after(squares_c))
-    v = joined(p2, a3)
-    a2e, a2m = out(v), across(v)
-    squares_y = swap(after(squares), "tp", 2, tp_count)
-    p0[1] = own_product(1)
-    squares = note(squares + after(squares_y))
+    back_z = summed(back, "fsdp", line)
+    rows3e = joint(pair, c3e)
+    v = note(product(after(rows3e), w[0]).astype(HALF))
+    back, squares = note(
+        whole(functools.partial(length_kernel, widths), (row, lanes), back_z())
+    )
+    a3 = [out(after(v)), None]
+    squares = summed(after(squares), "tp", tp_count)()
     states = note(
         whole(
             functools.partial(state_kernel, widths, tp_count),
-            tuple(jax.ShapeDtypeStruct((1, n), F32) for n in widths) + (lanes,),
+            tuple(jax.ShapeDtypeStruct((1, n), F32) for n in widths) + (lanes, row),
             back,
             squares,
-        )
-    )
-    scales = gammas / states[3][0, :3]
-    q_row = jnp.full((1, split), 1.0, F32) * scales[0]
-    kv_row = [jnp.full((1, kv_width), 1.0, F32) * scales[i] for i in (1, 2)]
-    factor = [jnp.concatenate(kv_row + [q_row], axis=1), q_row]
-    factor = note(after(tuple(factor)))
-    v = joined(p3, a2e)
-    a1m[1] = across(v)
-    v = joined(p1, a2m)
-    a1p[1] = swap(v, "fsdp", 1, line)
+            gammas,
+        )
+    )
+    factors = states[4]
+    factor = [factors[:, :wide], factors[:, wide:]]
+    x1 = arrived(x1)
+    y1 = swap_tp(x1, 2, everyone)
+    x3m = arrived(x3m)
+    y3m = swap_tp(x3m, 2, mids)
+    other_w[1] = swap(after(own_w[1]), "rep", 1, reps)
+    rows2 = joint(pair2, c2)
+    p2 = [note(product(after(rows2), w[0])), None]
+    p0 = [note(product(after(rows0), w[0])), None]
+    v = joined(p2[0], a3[0])
+    a2e, a2m = [out(v), None], [across(v), None]
+    pair1 = joint(x1, y1)
+    c1 = swap_tp(pair1, 1, everyone)
+    pair3 = joint(x3m, y3m)
+    c3m = swap_tp(pair3, 1, mids)
+    w[1] = (own_w[1], arrived(other_w[1]))
+    a3[1] = out(note(product(after(rows3e), w[1]).astype(HALF)))
+    p0[1] = note(product(after(rows0), w[1]))
+    p2[1] = note(product(after(rows2), w[1]))
+    rows1 = joint(pair1, c1)
+    p1 = [note(product(after(rows1), w[c])) for c in range(2)]
+    rows3m = joint(pair3, c3m)
+    p3m = [note(product(after(rows3m), w[c])) for c in range(2)]
+    a1p = [swap(joined(p1[0], a2m[0]), "fsdp", 1, line), None]
+    a1m = [across(joined(p3m[0], a2e[0])), None]
+    v = joined(p2[1], a3[1])
+    a2e[1], a2m[1] = out(v), across(v)
+    a1p[1] = swap(joined(p1[1], a2m[1]), "fsdp", 1, line)
+    a1m[1] = across(joined(p3m[1], a2e[1]))
 
     def packed(c):
         near, far = after((a1p[c], a1m[c]))
         return note((factor[c] * (p0[c] + near.astype(F32) + far.astype(F32))).astype(BF16))
 
-    ctx, keys, values = note(context_call(where, doc_lengths, packed(0), q_width))
-    context = context_call(where, doc_lengths, packed(1), q_width, (keys, values), ctx)
+    first = packed(0)
+    ctx, keys, values = note(context_call(where, order.token, first, q_width))
+    second = packed(1)
+    context = context_call(where, order.token, second, q_width, (keys, values), ctx)
     return (context, states[0][0], states[1][0], states[2][0], states[3][0, :3])
 
 

time: 253 us -> 199 us (0.79)
  Pallas kernels: 81.7 us -> 29.1 us
  matrix products: 0 us -> 32.1 us
  other arithmetic: 26.5 us -> 12.8 us
  local copies, waits for them, and re-layouts: 13.3 us -> 0.56 us
  waiting for transfers between devices: 72.8 us -> 68.3 us
  starting transfers between devices: 55.9 us -> 52.9 us
    pallas_call x14 -> x7, Pallas kernels: 72.1 us -> 19.5 us  [the longest x3 10.8 us: gather_blocks(): pl.pallas_call(kernel, out_shape=outs, grid_spec=pltpu.PrefetchScalarGrid...]
    dot_general x0 -> x20, matrix products: none -> 32.1 us  [the longest x10 16.6 us: product(): jnp.dot(x[:, deep:], w[1], preferred_element_type=F32)]
    convert_element_type x6, other arithmetic: 10.8 us -> 2.39 us  [joined(): return note((p + after(x).astype(F32)).astype(HALF))]
    ppermute x5, waiting for transfers between devices: 29.4 us -> 21.4 us  [across(): return send(x, 'fsdp', [(1, 2), (2, 1)])]
    ppermute x12 -> x8, waiting for transfers between devices: 8.03 us -> 15.1 us  [swap_tp(): return send(x, ('fsdp', 'tp'), pairs)]
    unnamed x56 -> x12, local copies, waits for them, and re-layouts: 6.27 us -> 0.03 us
    convert_element_type x2 -> x0, other arithmetic: 4.64 us -> none  [the longest x1 2.41 us: line_body(): v = note(product(parts3e, 0).astype(HALF))]
    ppermute x13 -> x15, waiting for transfers between devices: 32 us -> 27.6 us  [swap(): return send(x, axis, [(i, i ^ mask) for i in range(size)])]
  transfers between devices with their start and end apart: 35 -> 33, of which waited for: 14 -> 12; matrix products, arithmetic and copies ran while one was open for 10% -> 22% of each run, Pallas kernels for 28% -> 11%
where the time goes in v2:
time: 199 us; the launch traced here: 197 us
  waiting for transfers between devices  68.3 us (34%)
  starting transfers between devices  52.9 us (27%)
  matrix products  32.1 us (16%)
  Pallas kernels  29.1 us (15%)
  other arithmetic  12.8 us (6%)
    ppermute x15, waiting for transfers between devices, swap(): return send(x, axis, [(i, i ^ mask) for i in range(size)])  27.6 us
    ppermute x15, starting transfers between devices, swap(): return send(x, axis, [(i, i ^ mask) for i in range(size)])  22 us
    ppermute x5, waiting for transfers between devices, across(): return send(x, 'fsdp', [(1, 2), (2, 1)])  21.4 us
    dot_general x10, matrix products, product(): jnp.dot(x[:, deep:], w[1], preferred_element_type=F32)  16.6 us
    dot_general x10, matrix products, product(): jnp.dot(x[:, :deep], w[0], preferred_element_type=F32)  15.5 us
    ppermute x5, starting transfers between devices, across(): return send(x, 'fsdp', [(1, 2), (2, 1)])  15.3 us
    ppermute x8, waiting for transfers between devices, swap_tp(): return send(x, ('fsdp', 'tp'), pairs)  15.1 us
    pallas_call x3, Pallas kernels, gather_blocks(): pl.pallas_call(kernel, out_shape=outs, grid_spec=pltpu.PrefetchScalarGrid...  10.8 us
  transfers between devices with their start and end apart: 33, of which 12 were waited for; matrix products, arithmetic and copies ran while one was open for 22% of the time, Pallas kernels for 11%

profile of v2, /device:TPU:8, one launch (start us, length us, event | category | flops | bytes accessed | tf_op | source)
XLA Modules:
  0.0 196.9 jit_solution(9235620757766263369)
XLA Ops:
  1.2 3.6 %shard_map.128 = (bf16[128,2048]{1,0:T(8,128)(2,1)}, bf16[1024,768]{1,0:T(8,128)(2,1)}) custom-call(s32[3]{0:T(128)} %pad_add_fusion.where_ref.place, bf16[512,8192]{1,0:T(8,128)(2,1)} %refs_0_.5, bf16[1024,128]{1,0:T(8,128)(2,1)} %wk.3, bf16[1024,128]{1,0:T(8,128)(2,1)} %wv.3, bf16[1024,1024]{1,0:T(8,128)(2,1)} %wq.3), custom_call_target="tpu_custom_call" | custom-call | flops 1 | bytes 1 | tf_op jit(solution)/shard_map/pallas_call | solution.py:167
  5.5 3.6 %shard_map.129 = (bf16[128,2048]{1,0:T(8,128)(2,1)}, bf16[128,2048]{1,0:T(8,128)(2,1)}, bf16[1024,512]{1,0:T(8,128)(2,1)}) custom-call(s32[3]{0:T(128)} %pad_add_fusion.where_ref.place, bf16[512,8192]{1,0:T(8,128)(2,1)} %refs_0_.5, bf16[1024,1024]{1,0:T(8,128)(2,1)} %wq.3), custom_call_target="tpu_custom_call" | custom-call | flops 1 | bytes 1 | tf_op jit(solution)/shard_map/pallas_call | solution.py:167
  9.1 3.2 %shard_map.130 = f32[3,1024]{1,0:T(4,128)} custom-call(bf16[1024,1024]{1,0:T(8,128)(2,1)} %wq.3, bf16[1024,128]{1,0:T(8,128)(2,1)} %wk.3, bf16[1024,128]{1,0:T(8,128)(2,1)} %wv.3, f32[1,1024]{1,0:T(1,128)} %bitcast.33, f32[1,128]{1,0:T(1,128)} %bitcast.34, f32[1,128]{1,0:T(1,128)} %bitcast.35), custom_call_target="tpu_custom_call" | custom-call | flops 1 | bytes 1 | tf_op jit(solution)/shard_map/pallas_call | solution.py:147
  12.3 1.4 collective-permute-done
  13.7 0.7 add.87
  14.4 1.5 collective-permute-start.1
  15.9 4.0 %collective-permute-start.4 = (bf16[128,2048]{1,0:T(8,128)(2,1)S(1)}, bf16[128,2048]{1,0:T(8,128)(2,1)S(1)}, u32[]{:S(2)}, u32[]{:S(2)}) collective-permute-start(bf16[128,2048]{1,0:T(8,128)(2,1)S(1)} %copy-done.4), channel_id=1, source_target_pairs={{0,8},{4,12},{8,0},{12,4},{1,9},{5,13},{9,1},{13,5},{2,10},{6,14},... | collective-permute-start | bytes 1572872 | tf_op jit(solution)/shard_map/ppermute | solution.py:287
  20.5 2.8 %shard_map.131 = f32[1,1408]{1,0:T(1,128)} custom-call(bf16[1024,1024]{1,0:T(8,128)(2,1)} %wq.3, bf16[1024,128]{1,0:T(8,128)(2,1)} %wk.3, bf16[1024,128]{1,0:T(8,128)(2,1)} %wv.3, f32[3,1024]{1,0:T(4,128)} %add.88.image), custom_call_target="tpu_custom_call" | custom-call | flops 1 | bytes 1 | tf_op jit(solution)/shard_map/pallas_call | solution.py:147
  24.0 1.6 collective-permute-start.3
  25.5 18.5 %collective-permute-done.4 = bf16[128,2048]{1,0:T(8,128)(2,1)S(1)} collective-permute-done((bf16[128,2048]{1,0:T(8,128)(2,1)S(1)}, bf16[128,2048]{1,0:T(8,128)(2,1)S(1)}, u32[]{:S(2)}, u32[]{:S(2)}) %collective-permute-start.4) | collective-permute-done | bytes 524320 | tf_op jit(solution)/shard_map/ppermute | solution.py:287
  44.0 3.6 %shard_map.132 = bf16[512,2048]{1,0:T(8,128)(2,1)} custom-call(s32[3]{0:T(128)} %pad_add_fusion.where_ref.place, bf16[512,8192]{1,0:T(8,128)(2,1)} %refs_0_.5), custom_call_target="tpu_custom_call" | custom-call | flops 1 | bytes 1 | tf_op jit(solution)/shard_map/pallas_call | solution.py:167
  47.7 0.7 collective-permute-start.9
  48.5 1.6 collective-permute-start.6
  50.1 1.5 collective-permute-start.2
  51.6 2.5 %collective-permute-start.16 = (bf16[128,2048]{1,0:T(8,128)(2,1)}, bf16[128,2048]{1,0:T(8,128)(2,1)}, u32[]{:S(2)}, u32[]{:S(2)}) collective-permute-start(bf16[128,2048]{1,0:T(8,128)(2,1)} %get-tuple-element.269), channel_id=1, source_target_pairs={{0,4},{4,0},{8,12},{12,8},{1,5},{5,1},{9,13},{13,9},{2,6},{6,2},{1... | collective-permute-start | bytes 1572872 | tf_op jit(solution)/shard_map/ppermute | solution.py:287
  54.1 8.3 %collective-permute-done.6 = bf16[128,2048]{1,0:T(8,128)(2,1)S(1)} collective-permute-done((bf16[128,2048]{1,0:T(8,128)(2,1)S(1)}, bf16[128,2048]{1,0:T(8,128)(2,1)S(1)}, u32[]{:S(2)}, u32[]{:S(2)}) %collective-permute-start.6) | collective-permute-done | bytes 524320 | tf_op jit(solution)/shard_map/ppermute | solution.py:291
  62.6 3.4 %collective-permute-start.8 = (f32[1,1408]{1,0:T(1,128)S(1)}, f32[1,1408]{1,0:T(1,128)S(1)}, u32[]{:S(2)}, u32[]{:S(2)}) collective-permute-start(f32[1,1408]{1,0:T(1,128)S(1)} %add.89), channel_id=1, source_target_pairs={{0,4},{4,0},{8,12},{12,8},{1,5},{5,1},{9,13},{13,9},{2,6},{6,2},{1... | collective-permute-start | bytes 16904 | tf_op jit(solution)/shard_map/ppermute | solution.py:287
  66.0 1.8 collective-permute-start.10
  68.4 2.4 %fusion.29 = f32[512,768]{1,0:T(8,128)S(1)} fusion(bf16[1024,768]{1,0:T(8,128)(2,1)} %get-tuple-element.210, bf16[512,2048]{1,0:T(8,128)(2,1)S(1)} %pad_maximum_fusion), kind=kOutput, calls=%fused_computation.55 | convolution fusion | flops 805306368 | bytes 4194304 | tf_op jit(solution)/shard_map/dot_general | solution.py:319
  70.8 3.3 %add_convert_fusion.3 = f16[512,768]{1,0:T(8,128)(2,1)} fusion(f32[512,768]{1,0:T(8,128)S(1)} %fusion.29, bf16[1024,768]{1,0:T(8,128)(2,1)} %collective-permute-done.3, bf16[512,2048]{1,0:T(8,128)(2,1)S(1)} %pad_maximum_fusion), kind=kOutput, calls=%fused_computation.8 | convolution fusion | flops 806092800 | bytes 4980736 | tf_op jit(solution)/shard_map/dot_general | solution.py:319
  74.1 3.4 %collective-permute-start.15 = (bf16[128,2048]{1,0:T(8,128)(2,1)}, bf16[128,2048]{1,0:T(8,128)(2,1)}, u32[]{:S(2)}, u32[]{:S(2)}) collective-permute-start(bf16[128,2048]{1,0:T(8,128)(2,1)} %get-tuple-element.268), channel_id=1, source_target_pairs={{4,8},{8,4},{5,9},{9,5},{6,10},{10,6},{7,11},{11,7},{20,24},{24,20... | collective-permute-start | bytes 1572872 | tf_op jit(solution)/shard_map/ppermute | solution.py:330
  78.2 1.4 shard_map.133
  79.5 1.5 collective-permute-start.13
  81.1 1.1 collective-permute-start.14
  82.1 1.1 collective-permute-done.13
  83.2 1.3 collective-permute-start.21
  84.5 1.2 add_add_fusion.1.squares
  85.7 1.5 shard_map.134
  87.2 2.9 %collective-permute-done.15 = bf16[128,2048]{1,0:T(8,128)(2,1)} collective-permute-done((bf16[128,2048]{1,0:T(8,128)(2,1)}, bf16[128,2048]{1,0:T(8,128)(2,1)}, u32[]{:S(2)}, u32[]{:S(2)}) %collective-permute-start.15) | collective-permute-done | bytes 524320 | tf_op jit(solution)/shard_map/ppermute | solution.py:330
  90.0 1.4 pad_maximum_fusion.1
  91.5 2.4 %fusion.26 = f32[512,768]{1,0:T(8,128)S(1)} fusion(bf16[1024,768]{1,0:T(8,128)(2,1)} %get-tuple-element.210, bf16[512,2048]{1,0:T(8,128)(2,1)S(1)} %pad_maximum_fusion.1), kind=kOutput, calls=%fused_computation.52 | convolution fusion | flops 805306368 | bytes 4194304 | tf_op jit(solution)/shard_map/dot_general | solution.py:319
  93.9 2.5 %convolution_add_fusion.3 = f32[512,768]{1,0:T(8,128)S(1)} fusion(f32[512,768]{1,0:T(8,128)S(1)} %fusion.26, bf16[1024,768]{1,0:T(8,128)(2,1)} %collective-permute-done.3, bf16[512,2048]{1,0:T(8,128)(2,1)S(1)} %pad_maximum_fusion.1), kind=kOutput, calls=%fused_computation.12 | convolution fusion | flops 805699584 | bytes 5767168 | tf_op jit(solution)/shard_map/dot_general | solution.py:319
  96.4 1.6 collective-permute-start.19
  98.0 1.5 collective-permute-start.17
  99.5 2.4 %fusion.23 = f32[512,768]{1,0:T(8,128)S(1)} fusion(bf16[1024,768]{1,0:T(8,128)(2,1)} %get-tuple-element.210, bf16[512,2048]{1,0:T(8,128)(2,1)S(1)} %copy-done), kind=kOutput, calls=%fused_computation.49 | convolution fusion | flops 805306368 | bytes 4194304 | tf_op jit(solution)/shard_map/dot_general | solution.py:319
  101.9 2.4 %convolution_add_fusion.2 = f32[512,768]{1,0:T(8,128)S(1)} fusion(f32[512,768]{1,0:T(8,128)S(1)} %fusion.23, bf16[1024,768]{1,0:T(8,128)(2,1)} %collective-permute-done.3, bf16[512,2048]{1,0:T(8,128)(2,1)S(1)} %copy-done), kind=kOutput, calls=%fused_computation.11 | convolution fusion | flops 805699584 | bytes 5767168 | tf_op jit(solution)/shard_map/dot_general | solution.py:319
  104.3 2.4 %collective-permute-start.18 = (bf16[128,2048]{1,0:T(8,128)(2,1)}, bf16[128,2048]{1,0:T(8,128)(2,1)S(1)}, u32[]{:S(2)}, u32[]{:S(2)}) collective-permute-start(bf16[128,2048]{1,0:T(8,128)(2,1)} %collective-permute-done.15), channel_id=1, source_target_pairs={{4,6},{5,7},{6,4},{7,5},{8,10},{9,11},{10,8},{11,9},{20,22},{21,23... | collective-permute-start | bytes 1572872 | tf_op jit(solution)/shard_map/ppermute | solution.py:291
  106.8 1.4 add_convert_fusion.2
  108.1 3.4 %collective-permute-start.26 = (f16[512,768]{1,0:T(8,128)(2,1)S(1)}, f16[512,768]{1,0:T(8,128)(2,1)S(1)}, u32[]{:S(2)}, u32[]{:S(2)}) collective-permute-start(f16[512,768]{1,0:T(8,128)(2,1)S(1)} %add_convert_fusion.2), channel_id=1, source_target_pairs={{4,8},{8,4},{5,9},{9,5},{6,10},{10,6},{7,11},{11,7},{20,24},{24,20... | collective-permute-start | bytes 2359304 | tf_op jit(solution)/shard_map/ppermute | solution.py:330
  111.6 1.3 collective-permute-start.25
  112.9 1.1 pad_maximum_fusion.6
  114.0 6.8 %collective-permute-done.18 = bf16[128,2048]{1,0:T(8,128)(2,1)S(1)} collective-permute-done((bf16[128,2048]{1,0:T(8,128)(2,1)}, bf16[128,2048]{1,0:T(8,128)(2,1)S(1)}, u32[]{:S(2)}, u32[]{:S(2)}) %collective-permute-start.18) | collective-permute-done | bytes 524320 | tf_op jit(solution)/shard_map/ppermute | solution.py:291
  120.8 1.1 pad_maximum_fusion.7
  122.1 2.6 %collective-permute-start.24 = (bf16[256,2048]{1,0:T(8,128)(2,1)S(1)}, bf16[256,2048]{1,0:T(8,128)(2,1)S(1)}, u32[]{:S(2)}, u32[]{:S(2)}) collective-permute-start(bf16[256,2048]{1,0:T(8,128)(2,1)S(1)} %pad_maximum_fusion.7), channel_id=1, source_target_pairs={{4,5},{5,4},{6,7},{7,6},{8,9},{9,8},{10,11},{11,10},{20,21},{21,20... | collective-permute-start | bytes 3145736 | tf_op jit(solution)/shard_map/ppermute | solution.py:291
  128.9 1.3 collective-permute-start.23
  130.5 2.4 %fusion.11 = f32[512,768]{1,0:T(8,128)S(1)} fusion(bf16[1024,768]{1,0:T(8,128)(2,1)} %get-tuple-element.210, bf16[512,2048]{1,0:T(8,128)(2,1)S(1)} %pad_maximum_fusion.2), kind=kOutput, calls=%fused_computation.37 | convolution fusion | flops 805306368 | bytes 4194304 | tf_op jit(solution)/shard_map/dot_general | solution.py:319
  132.9 2.4 %convolution_add_fusion.1 = f32[512,768]{1,0:T(8,128)S(1)} fusion(f32[512,768]{1,0:T(8,128)S(1)} %fusion.11, bf16[1024,768]{1,0:T(8,128)(2,1)} %collective-permute-done.3, bf16[512,2048]{1,0:T(8,128)(2,1)S(1)} %pad_maximum_fusion.2), kind=kOutput, calls=%fused_computation.10 | convolution fusion | flops 805699584 | bytes 5767168 | tf_op jit(solution)/shard_map/dot_general | solution.py:319
  137.0 2.4 %fusion.5 = f32[512,768]{1,0:T(8,128)S(1)} fusion(bf16[1024,768]{1,0:T(8,128)(2,1)} %get-tuple-element.210, bf16[512,2048]{1,0:T(8,128)(2,1)S(1)} %pad_maximum_fusion.3), kind=kOutput, calls=%fused_computation.31 | convolution fusion | flops 805306368 | bytes 4194304 | tf_op jit(solution)/shard_map/dot_general | solution.py:319
  139.4 2.4 %convolution_add_fusion = f32[512,768]{1,0:T(8,128)S(1)} fusion(f32[512,768]{1,0:T(8,128)S(1)} %fusion.5, bf16[1024,768]{1,0:T(8,128)(2,1)} %collective-permute-done.3, bf16[512,2048]{1,0:T(8,128)(2,1)S(1)} %pad_maximum_fusion.3), kind=kOutput, calls=%fused_computation.9 | convolution fusion | flops 805699584 | bytes 5767168 | tf_op jit(solution)/shard_map/dot_general | solution.py:319
  143.7 1.0 collective-permute-done.23
  144.9 3.4 %collective-permute-start.27 = (f16[512,512]{1,0:T(8,128)(2,1)S(1)}, f16[512,512]{1,0:T(8,128)(2,1)S(1)}, u32[]{:S(2)}, u32[]{:S(2)}) collective-permute-start(f16[512,512]{1,0:T(8,128)(2,1)S(1)} %add_convert_fusion.6), channel_id=1, source_target_pairs={{4,8},{8,4},{5,9},{9,5},{6,10},{10,6},{7,11},{11,7},{20,24},{24,20... | collective-permute-start | bytes 1572872 | tf_op jit(solution)/shard_map/ppermute | solution.py:330
  148.3 1.3 collective-permute-start.29
  149.6 2.4 %collective-permute-start.32 = (f16[512,768]{1,0:T(8,128)(2,1)S(1)}, f16[512,768]{1,0:T(8,128)(2,1)S(1)}, u32[]{:S(2)}, u32[]{:S(2)}) collective-permute-start(f16[512,768]{1,0:T(8,128)(2,1)S(1)} %add_convert_fusion), channel_id=1, source_target_pairs={{4,8},{8,4},{5,9},{9,5},{6,10},{10,6},{7,11},{11,7},{20,24},{24,20... | collective-permute-start | bytes 2359304 | tf_op jit(solution)/shard_map/ppermute | solution.py:330
  152.0 1.1 collective-permute-start.31
  153.1 8.5 %collective-permute-done.27 = f16[512,512]{1,0:T(8,128)(2,1)S(1)} collective-permute-done((f16[512,512]{1,0:T(8,128)(2,1)S(1)}, f16[512,512]{1,0:T(8,128)(2,1)S(1)}, u32[]{:S(2)}, u32[]{:S(2)}) %collective-permute-start.27) | collective-permute-done | bytes 524320 | tf_op jit(solution)/shard_map/ppermute | solution.py:330
  161.8 3.2 %collective-permute-done.29 = f16[512,512]{1,0:T(8,128)(2,1)S(1)} collective-permute-done((f16[512,512]{1,0:T(8,128)(2,1)S(1)}, f16[512,512]{1,0:T(8,128)(2,1)S(1)}, u32[]{:S(2)}, u32[]{:S(2)}) %collective-permute-start.29) | collective-permute-done | bytes 524320 | tf_op jit(solution)/shard_map/ppermute | solution.py:327
  165.3 2.6 %collective-permute-start.30 = (f16[512,512]{1,0:T(8,128)(2,1)S(1)}, f16[512,512]{1,0:T(8,128)(2,1)S(1)}, u32[]{:S(2)}, u32[]{:S(2)}) collective-permute-start(f16[512,512]{1,0:T(8,128)(2,1)S(1)} %add_convert_fusion.4), channel_id=1, source_target_pairs={{4,8},{8,4},{5,9},{9,5},{6,10},{10,6},{7,11},{11,7},{20,24},{24,20... | collective-permute-start | bytes 1572872 | tf_op jit(solution)/shard_map/ppermute | solution.py:330
  168.5 10.0 %collective-permute-done.32 = f16[512,768]{1,0:T(8,128)(2,1)S(1)} collective-permute-done((f16[512,768]{1,0:T(8,128)(2,1)S(1)}, f16[512,768]{1,0:T(8,128)(2,1)S(1)}, u32[]{:S(2)}, u32[]{:S(2)}) %collective-permute-start.32) | collective-permute-done | bytes 786464 | tf_op jit(solution)/shard_map/ppermute | solution.py:330
  178.5 3.5 %collective-permute-done.31 = f16[512,768]{1,0:T(8,128)(2,1)S(1)} collective-permute-done((f16[512,768]{1,0:T(8,128)(2,1)S(1)}, f16[512,768]{1,0:T(8,128)(2,1)S(1)}, u32[]{:S(2)}, u32[]{:S(2)}) %collective-permute-start.31) | collective-permute-done | bytes 786464 | tf_op jit(solution)/shard_map/ppermute | solution.py:287
  181.9 1.2 multiply_convert_fusion.packed
  183.1 4.8 %shard_map.135 = (bf16[512,1024]{1,0:T(8,128)(2,1)}, bf16[512,128]{1,0:T(8,128)(2,1)}, bf16[512,128]{1,0:T(8,128)(2,1)}) custom-call(s32[3]{0:T(128)} %pad_add_fusion.where_ref.place, s32[1,8]{1,0:T(1,128)} %lengths.1, bf16[512,768]{1,0:T(8,128)(2,1)} %multiply_convert_fusion.packed), custom_call_target="tpu_custom_call" | custom-call | flops 1 | bytes 1 | tf_op jit(solution)/shard_map/pallas_call | solution.py:248
  187.9 3.1 %collective-permute-done.28 = f16[512,512]{1,0:T(8,128)(2,1)S(1)} collective-permute-done((f16[512,512]{1,0:T(8,128)(2,1)S(1)}, f16[512,512]{1,0:T(8,128)(2,1)S(1)}, u32[]{:S(2)}, u32[]{:S(2)}) %collective-permute-start.28) | collective-permute-done | bytes 524320 | tf_op jit(solution)/shard_map/ppermute | solution.py:287
  191.0 1.1 multiply_convert_fusion.1.packed
  192.1 4.8 %shard_map.136 = bf16[512,1024]{1,0:T(8,128)(2,1)} custom-call(s32[3]{0:T(128)} %pad_add_fusion.where_ref.place, s32[1,8]{1,0:T(1,128)} %lengths.1, bf16[512,512]{1,0:T(8,128)(2,1)} %multiply_convert_fusion.1.packed, bf16[512,128]{1,0:T(8,128)(2,1)} %get-tuple-element.372.refs_0_, ...), custom_call_target="tpu_custom_call", output_to_operand_aliasing={{}: (5, {})} | custom-call | flops 1 | bytes 1 | tf_op jit(solution)/shard_map/pallas_call | solution.py:248
  (68 shorter events, 13.3 us)
Async XLA Ops:
  4.8 18.5 %collective-permute-start.5 = (bf16[128,2048]{1,0:T(8,128)(2,1)}, bf16[128,2048]{1,0:T(8,128)(2,1)S(1)}, u32[]{:S(2)}, u32[]{:S(2)}) collective-permute-start(bf16[128,2048]{1,0:T(8,128)(2,1)} %get-tuple-element.268), channel_id=1, source_target_pairs={{0,12},{12,0},{1,13},{13,1},{2,14},{14,2},{3,15},{15,3},{16,28},{2... | collective-permute-start | bytes 1572872 | tf_op jit(solution)/shard_map/ppermute | solution.py:353
  9.1 6.8 %copy-start.4 = (bf16[128,2048]{1,0:T(8,128)(2,1)S(1)}, bf16[128,2048]{1,0:T(8,128)(2,1)}, u32[]{:S(2)}) copy-start(bf16[128,2048]{1,0:T(8,128)(2,1)} %get-tuple-element.211) | copy-start | bytes 1572868
  12.3 1.4 collective-permute-start
  14.4 5.6 %collective-permute-start.1 = (f32[3,1024]{1,0:T(4,128)S(1)}, f32[3,1024]{1,0:T(4,128)S(1)}, u32[]{:S(2)}, u32[]{:S(2)}) collective-permute-start(f32[3,1024]{1,0:T(4,128)S(1)} %add.87), channel_id=1, source_target_pairs={{0,2},{1,3},{2,0},{3,1},{4,6},{5,7},{6,4},{7,5},{8,10},{9,11},{10,... | collective-permute-start | bytes 36872 | tf_op jit(solution)/shard_map/ppermute | solution.py:287
  15.9 28.1 %collective-permute-start.4 = (bf16[128,2048]{1,0:T(8,128)(2,1)S(1)}, bf16[128,2048]{1,0:T(8,128)(2,1)S(1)}, u32[]{:S(2)}, u32[]{:S(2)}) collective-permute-start(bf16[128,2048]{1,0:T(8,128)(2,1)S(1)} %copy-done.4), channel_id=1, source_target_pairs={{0,8},{4,12},{8,0},{12,4},{1,9},{5,13},{9,1},{13,5},{2,10},{6,14},... | collective-permute-start | bytes 1572872 | tf_op jit(solution)/shard_map/ppermute | solution.py:287
  23.3 24.4 %collective-permute-start.7 = (bf16[128,2048]{1,0:T(8,128)(2,1)S(1)}, bf16[128,2048]{1,0:T(8,128)(2,1)S(1)}, u32[]{:S(2)}, u32[]{:S(2)}) collective-permute-start(bf16[128,2048]{1,0:T(8,128)(2,1)S(1)} %collective-permute-done.5), channel_id=1, source_target_pairs={{0,2},{1,3},{2,0},{3,1},{12,14},{13,15},{14,12},{15,13},{16,18},{1... | collective-permute-start | bytes 1572872 | tf_op jit(solution)/shard_map/ppermute | solution.py:291
  24.0 38.6 %collective-permute-start.3 = (bf16[1024,768]{1,0:T(8,128)(2,1)}, bf16[1024,768]{1,0:T(8,128)(2,1)}, u32[]{:S(2)}, u32[]{:S(2)}) collective-permute-start(bf16[1024,768]{1,0:T(8,128)(2,1)} %get-tuple-element.210), channel_id=1, source_target_pairs={{0,16},{16,0},{1,17},{17,1},{2,18},{18,2},{3,19},{19,3},{4,20},{20... | collective-permute-start | bytes 4718600 | tf_op jit(solution)/shard_map/ppermute | solution.py:287
  47.6 2.4 %copy-start.1 = (f32[1,1408]{1,0:T(1,128)S(1)}, f32[1,1408]{1,0:T(1,128)}, u32[]{:S(2)}) copy-start(f32[1,1408]{1,0:T(1,128)} %shard_map.131) | copy-start | bytes 16900
  47.7 20.1 %collective-permute-start.9 = (bf16[256,2048]{1,0:T(8,128)(2,1)S(1)}, bf16[256,2048]{1,0:T(8,128)(2,1)S(1)}, u32[]{:S(2)}, u32[]{:S(2)}) collective-permute-start(bf16[256,2048]{1,0:T(8,128)(2,1)S(1)} %pad_maximum_fusion.4), channel_id=1, source_target_pairs={{0,1},{1,0},{2,3},{3,2},{12,13},{13,12},{14,15},{15,14},{16,17},{1... | collective-permute-start | bytes 3145736 | tf_op jit(solution)/shard_map/ppermute | solution.py:291
  48.5 13.9 %collective-permute-start.6 = (bf16[128,2048]{1,0:T(8,128)(2,1)S(1)}, bf16[128,2048]{1,0:T(8,128)(2,1)S(1)}, u32[]{:S(2)}, u32[]{:S(2)}) collective-permute-start(bf16[128,2048]{1,0:T(8,128)(2,1)S(1)} %collective-permute-done.4), channel_id=1, source_target_pairs={{0,2},{1,3},{2,0},{3,1},{4,6},{5,7},{6,4},{7,5},{8,10},{9,11},{10,... | collective-permute-start | bytes 1572872 | tf_op jit(solution)/shard_map/ppermute | solution.py:291
  50.1 12.5 %collective-permute-start.2 = (f32[1,1408]{1,0:T(1,128)S(1)}, f32[1,1408]{1,0:T(1,128)S(1)}, u32[]{:S(2)}, u32[]{:S(2)}) collective-permute-start(f32[1,1408]{1,0:T(1,128)S(1)} %copy-done.1), channel_id=1, source_target_pairs={{0,16},{16,0},{1,17},{17,1},{2,18},{18,2},{3,19},{19,3},{4,20},{20... | collective-permute-start | bytes 16904 | tf_op jit(solution)/shard_map/ppermute | solution.py:287
  51.6 35.6 %collective-permute-start.16 = (bf16[128,2048]{1,0:T(8,128)(2,1)}, bf16[128,2048]{1,0:T(8,128)(2,1)}, u32[]{:S(2)}, u32[]{:S(2)}) collective-permute-start(bf16[128,2048]{1,0:T(8,128)(2,1)} %get-tuple-element.269), channel_id=1, source_target_pairs={{0,4},{4,0},{8,12},{12,8},{1,5},{5,1},{9,13},{13,9},{2,6},{6,2},{1... | collective-permute-start | bytes 1572872 | tf_op jit(solution)/shard_map/ppermute | solution.py:287
  62.5 27.6 %collective-permute-start.20 = (bf16[256,2048]{1,0:T(8,128)(2,1)S(1)}, bf16[256,2048]{1,0:T(8,128)(2,1)}, u32[]{:S(2)}, u32[]{:S(2)}) collective-permute-start(bf16[256,2048]{1,0:T(8,128)(2,1)S(1)} %pad_maximum_fusion.5), channel_id=1, source_target_pairs={{0,1},{1,0},{2,3},{3,2},{4,5},{5,4},{6,7},{7,6},{8,9},{9,8},{10,11... | collective-permute-start | bytes 3145736 | tf_op jit(solution)/shard_map/ppermute | solution.py:291
  62.6 11.5 %collective-permute-start.8 = (f32[1,1408]{1,0:T(1,128)S(1)}, f32[1,1408]{1,0:T(1,128)S(1)}, u32[]{:S(2)}, u32[]{:S(2)}) collective-permute-start(f32[1,1408]{1,0:T(1,128)S(1)} %add.89), channel_id=1, source_target_pairs={{0,4},{4,0},{8,12},{12,8},{1,5},{5,1},{9,13},{13,9},{2,6},{6,2},{1... | collective-permute-start | bytes 16904 | tf_op jit(solution)/shard_map/ppermute | solution.py:287
  66.0 11.5 %collective-permute-start.10 = (f32[1,1408]{1,0:T(1,128)S(1)}, f32[1,1408]{1,0:T(1,128)S(1)}, u32[]{:S(2)}, u32[]{:S(2)}) collective-permute-start(f32[1,1408]{1,0:T(1,128)S(1)} %add.89), channel_id=1, source_target_pairs={{0,8},{4,12},{8,0},{12,4},{1,9},{5,13},{9,1},{13,5},{2,10},{6,14},... | collective-permute-start | bytes 16904 | tf_op jit(solution)/shard_map/ppermute | solution.py:287
  67.8 9.8 %collective-permute-start.11 = (f32[1,1408]{1,0:T(1,128)S(1)}, f32[1,1408]{1,0:T(1,128)S(1)}, u32[]{:S(2)}, u32[]{:S(2)}) collective-permute-start(f32[1,1408]{1,0:T(1,128)S(1)} %add.89), channel_id=1, source_target_pairs={{0,12},{4,8},{8,4},{12,0},{1,13},{5,9},{9,5},{13,1},{2,14},{6,10},... | collective-permute-start | bytes 16904 | tf_op jit(solution)/shard_map/ppermute | solution.py:287
  74.1 15.9 %collective-permute-start.15 = (bf16[128,2048]{1,0:T(8,128)(2,1)}, bf16[128,2048]{1,0:T(8,128)(2,1)}, u32[]{:S(2)}, u32[]{:S(2)}) collective-permute-start(bf16[128,2048]{1,0:T(8,128)(2,1)} %get-tuple-element.268), channel_id=1, source_target_pairs={{4,8},{8,4},{5,9},{9,5},{6,10},{10,6},{7,11},{11,7},{20,24},{24,20... | collective-permute-start | bytes 1572872 | tf_op jit(solution)/shard_map/ppermute | solution.py:330
  79.5 1.5 collective-permute-start.12
  79.5 3.7 %collective-permute-start.13 = (f32[1,128]{1,0:T(1,128)}, f32[1,128]{1,0:T(1,128)S(1)}, u32[]{:S(2)}, u32[]{:S(2)}) collective-permute-start(f32[1,128]{1,0:T(1,128)} %get-tuple-element.253), channel_id=1, source_target_pairs={{0,2},{1,3},{2,0},{3,1},{4,6},{5,7},{6,4},{7,5},{8,10},{9,11},{10,... | collective-permute-start | bytes 1544 | tf_op jit(solution)/shard_map/ppermute | solution.py:287
  81.1 3.4 %collective-permute-start.14 = (f32[1,128]{1,0:T(1,128)}, f32[1,128]{1,0:T(1,128)S(1)}, u32[]{:S(2)}, u32[]{:S(2)}) collective-permute-start(f32[1,128]{1,0:T(1,128)} %get-tuple-element.253), channel_id=1, source_target_pairs={{0,3},{1,2},{2,1},{3,0},{4,7},{5,6},{6,5},{7,4},{8,11},{9,10},{10,... | collective-permute-start | bytes 1544 | tf_op jit(solution)/shard_map/ppermute | solution.py:287
  83.2 23.5 %collective-permute-start.21 = (f16[512,768]{1,0:T(8,128)(2,1)}, f16[512,768]{1,0:T(8,128)(2,1)}, u32[]{:S(2)}, u32[]{:S(2)}) collective-permute-start(f16[512,768]{1,0:T(8,128)(2,1)} %add_convert_fusion.3), channel_id=1, source_target_pairs={{0,4},{12,8},{1,5},{13,9},{2,6},{14,10},{3,7},{15,11},{16,20},{28,... | collective-permute-start | bytes 2359304 | tf_op jit(solution)/shard_map/ppermute | solution.py:327
  93.9 4.2 %copy-start.3 = (bf16[1024,512]{1,0:T(8,128)(2,1)S(1)}, bf16[1024,512]{1,0:T(8,128)(2,1)}, u32[]{:S(2)}) copy-start(bf16[1024,512]{1,0:T(8,128)(2,1)} %get-tuple-element.273) | copy-start | bytes 3145732
  93.9 5.6 %copy-start = (bf16[512,2048]{1,0:T(8,128)(2,1)S(1)}, bf16[512,2048]{1,0:T(8,128)(2,1)}, u32[]{:S(2)}) copy-start(bf16[512,2048]{1,0:T(8,128)(2,1)} %shard_map.132) | copy-start | bytes 6291460
  96.4 16.4 %collective-permute-start.19 = (bf16[128,2048]{1,0:T(8,128)(2,1)}, bf16[128,2048]{1,0:T(8,128)(2,1)S(1)}, u32[]{:S(2)}, u32[]{:S(2)}) collective-permute-start(bf16[128,2048]{1,0:T(8,128)(2,1)} %collective-permute-done.16), channel_id=1, source_target_pairs={{0,2},{1,3},{2,0},{3,1},{4,6},{5,7},{6,4},{7,5},{8,10},{9,11},{10,... | collective-permute-start | bytes 1572872 | tf_op jit(solution)/shard_map/ppermute | solution.py:291
  98.0 26.6 %collective-permute-start.17 = (bf16[1024,512]{1,0:T(8,128)(2,1)S(1)}, bf16[1024,512]{1,0:T(8,128)(2,1)S(1)}, u32[]{:S(2)}, u32[]{:S(2)}) collective-permute-start(bf16[1024,512]{1,0:T(8,128)(2,1)S(1)} %copy-done.3), channel_id=1, source_target_pairs={{0,16},{16,0},{1,17},{17,1},{2,18},{18,2},{3,19},{19,3},{4,20},{20... | collective-permute-start | bytes 3145736 | tf_op jit(solution)/shard_map/ppermute | solution.py:287
  104.3 16.5 %collective-permute-start.18 = (bf16[128,2048]{1,0:T(8,128)(2,1)}, bf16[128,2048]{1,0:T(8,128)(2,1)S(1)}, u32[]{:S(2)}, u32[]{:S(2)}) collective-permute-start(bf16[128,2048]{1,0:T(8,128)(2,1)} %collective-permute-done.15), channel_id=1, source_target_pairs={{4,6},{5,7},{6,4},{7,5},{8,10},{9,11},{10,8},{11,9},{20,22},{21,23... | collective-permute-start | bytes 1572872 | tf_op jit(solution)/shard_map/ppermute | solution.py:291
  108.1 35.1 %collective-permute-start.26 = (f16[512,768]{1,0:T(8,128)(2,1)S(1)}, f16[512,768]{1,0:T(8,128)(2,1)S(1)}, u32[]{:S(2)}, u32[]{:S(2)}) collective-permute-start(f16[512,768]{1,0:T(8,128)(2,1)S(1)} %add_convert_fusion.2), channel_id=1, source_target_pairs={{4,8},{8,4},{5,9},{9,5},{6,10},{10,6},{7,11},{11,7},{20,24},{24,20... | collective-permute-start | bytes 2359304 | tf_op jit(solution)/shard_map/ppermute | solution.py:330
  111.6 31.9 %collective-permute-start.25 = (f16[512,768]{1,0:T(8,128)(2,1)S(1)}, f16[512,768]{1,0:T(8,128)(2,1)S(1)}, u32[]{:S(2)}, u32[]{:S(2)}) collective-permute-start(f16[512,768]{1,0:T(8,128)(2,1)S(1)} %add_convert_fusion.2), channel_id=1, source_target_pairs={{0,4},{12,8},{1,5},{13,9},{2,6},{14,10},{3,7},{15,11},{16,20},{28,... | collective-permute-start | bytes 2359304 | tf_op jit(solution)/shard_map/ppermute | solution.py:327
  122.0 8.3 %collective-permute-start.22 = (bf16[256,2048]{1,0:T(8,128)(2,1)S(1)}, bf16[256,2048]{1,0:T(8,128)(2,1)S(1)}, u32[]{:S(2)}, u32[]{:S(2)}) collective-permute-start(bf16[256,2048]{1,0:T(8,128)(2,1)S(1)} %pad_maximum_fusion.6), channel_id=1, source_target_pairs={{0,1},{1,0},{2,3},{3,2},{4,5},{5,4},{6,7},{7,6},{8,9},{9,8},{10,11... | collective-permute-start | bytes 3145736 | tf_op jit(solution)/shard_map/ppermute | solution.py:291
  122.1 14.7 %collective-permute-start.24 = (bf16[256,2048]{1,0:T(8,128)(2,1)S(1)}, bf16[256,2048]{1,0:T(8,128)(2,1)S(1)}, u32[]{:S(2)}, u32[]{:S(2)}) collective-permute-start(bf16[256,2048]{1,0:T(8,128)(2,1)S(1)} %pad_maximum_fusion.7), channel_id=1, source_target_pairs={{4,5},{5,4},{6,7},{7,6},{8,9},{9,8},{10,11},{11,10},{20,21},{21,20... | collective-permute-start | bytes 3145736 | tf_op jit(solution)/shard_map/ppermute | solution.py:291
  128.9 15.8 %collective-permute-start.23 = (f16[512,512]{1,0:T(8,128)(2,1)S(1)}, f16[512,512]{1,0:T(8,128)(2,1)S(1)}, u32[]{:S(2)}, u32[]{:S(2)}) collective-permute-start(f16[512,512]{1,0:T(8,128)(2,1)S(1)} %fusion), channel_id=1, source_target_pairs={{0,4},{12,8},{1,5},{13,9},{2,6},{14,10},{3,7},{15,11},{16,20},{28,... | collective-permute-start | bytes 1572872 | tf_op jit(solution)/shard_map/ppermute | solution.py:327
  143.4 9.6 %copy-start.2 = (f32[1,1280]{1,0:T(1,128)S(1)}, f32[1,1280]{1,0:T(1,128)}, u32[]{:S(2)}) copy-start(f32[1,1280]{1,0:T(1,128)} %get-tuple-element.264) | copy-start | bytes 15364
  144.9 16.8 %collective-permute-start.27 = (f16[512,512]{1,0:T(8,128)(2,1)S(1)}, f16[512,512]{1,0:T(8,128)(2,1)S(1)}, u32[]{:S(2)}, u32[]{:S(2)}) collective-permute-start(f16[512,512]{1,0:T(8,128)(2,1)S(1)} %add_convert_fusion.6), channel_id=1, source_target_pairs={{4,8},{8,4},{5,9},{9,5},{6,10},{10,6},{7,11},{11,7},{20,24},{24,20... | collective-permute-start | bytes 1572872 | tf_op jit(solution)/shard_map/ppermute | solution.py:330
  148.3 16.8 %collective-permute-start.29 = (f16[512,512]{1,0:T(8,128)(2,1)S(1)}, f16[512,512]{1,0:T(8,128)(2,1)S(1)}, u32[]{:S(2)}, u32[]{:S(2)}) collective-permute-start(f16[512,512]{1,0:T(8,128)(2,1)S(1)} %add_convert_fusion.6), channel_id=1, source_target_pairs={{0,4},{12,8},{1,5},{13,9},{2,6},{14,10},{3,7},{15,11},{16,20},{28,... | collective-permute-start | bytes 1572872 | tf_op jit(solution)/shard_map/ppermute | solution.py:327
  149.6 28.9 %collective-permute-start.32 = (f16[512,768]{1,0:T(8,128)(2,1)S(1)}, f16[512,768]{1,0:T(8,128)(2,1)S(1)}, u32[]{:S(2)}, u32[]{:S(2)}) collective-permute-start(f16[512,768]{1,0:T(8,128)(2,1)S(1)} %add_convert_fusion), channel_id=1, source_target_pairs={{4,8},{8,4},{5,9},{9,5},{6,10},{10,6},{7,11},{11,7},{20,24},{24,20... | collective-permute-start | bytes 2359304 | tf_op jit(solution)/shard_map/ppermute | solution.py:330
  152.0 29.9 %collective-permute-start.31 = (f16[512,768]{1,0:T(8,128)(2,1)S(1)}, f16[512,768]{1,0:T(8,128)(2,1)S(1)}, u32[]{:S(2)}, u32[]{:S(2)}) collective-permute-start(f16[512,768]{1,0:T(8,128)(2,1)S(1)} %add_convert_fusion.1), channel_id=1, source_target_pairs={{0,4},{4,0},{8,12},{12,8},{1,5},{5,1},{9,13},{13,9},{2,6},{6,2},{1... | collective-permute-start | bytes 2359304 | tf_op jit(solution)/shard_map/ppermute | solution.py:287
  153.1 14.8 %copy-start.5 = (f32[1,128]{1,0:T(1,128)S(1)}, f32[1,128]{1,0:T(1,128)}, u32[]{:S(2)}) copy-start(f32[1,128]{1,0:T(1,128)} %get-tuple-element.378) | copy-start | bytes 1540
  165.3 22.7 %collective-permute-start.30 = (f16[512,512]{1,0:T(8,128)(2,1)S(1)}, f16[512,512]{1,0:T(8,128)(2,1)S(1)}, u32[]{:S(2)}, u32[]{:S(2)}) collective-permute-start(f16[512,512]{1,0:T(8,128)(2,1)S(1)} %add_convert_fusion.4), channel_id=1, source_target_pairs={{4,8},{8,4},{5,9},{9,5},{6,10},{10,6},{7,11},{11,7},{20,24},{24,20... | collective-permute-start | bytes 1572872 | tf_op jit(solution)/shard_map/ppermute | solution.py:330
  167.9 23.2 %collective-permute-start.28 = (f16[512,512]{1,0:T(8,128)(2,1)S(1)}, f16[512,512]{1,0:T(8,128)(2,1)S(1)}, u32[]{:S(2)}, u32[]{:S(2)}) collective-permute-start(f16[512,512]{1,0:T(8,128)(2,1)S(1)} %add_convert_fusion.5), channel_id=1, source_target_pairs={{0,4},{4,0},{8,12},{12,8},{1,5},{5,1},{9,13},{13,9},{2,6},{6,2},{1... | collective-permute-start | bytes 1572872 | tf_op jit(solution)/shard_map/ppermute | solution.py:287

commit v3 on v2

--- a/solution.py
+++ b/solution.py
@@ -352,17 +352,24 @@
     )
     x3e = send(mine, "fsdp", [(0, 3), (3, 0)])
     other_w = [swap(own_w[0], "rep", 1, reps), None]
-    x2, x1, own_w[1] = note(
+    x2, x1, x3m, own_w[1] = note(
         gather_blocks(
             after(where),
             (tokens, w_query),
-            (piece(quarter, reps * deep), piece(quarter, reps * deep), piece(deep, split)),
+            (
+                piece(quarter, reps * deep),
+                piece(quarter, reps * deep),
+                piece(2 * quarter, reps * deep),
+                piece(deep, split),
+            ),
             lambda at: slab(0, 2, 0, (0,))(at)
             + slab(0, 1, 1, (0,))(at)
-            + [(1, (every, pl.ds(split, split)), 2, (every, pl.ds(0, split)))],
+            + slab(0, 3, 2, (0, 2))(at)
+            + [(1, (every, pl.ds(split, split)), 3, (every, pl.ds(0, split)))],
         )
     )
     x2 = swap(x2, "fsdp", 2, line)
+    x1 = swap(x1, "fsdp", 1, line)
     img = note(
         whole(
             image_kernel,
@@ -395,16 +402,8 @@
     def joined(p, x):
         return note((p + after(x).astype(F32)).astype(HALF))
 
-    def summed(x, axis, size):
-        parts = [swap(x, axis, mask, size) for mask in (1, 2, 3)]
-        return lambda: note((x + after(parts[0])) + (parts[1] + parts[2]))
-
     x3e = arrived(x3e)
     y3e = swap_tp(x3e, 2, ends)
-    x2 = arrived(x2)
-    y2 = swap_tp(x2, 2, everyone)
-    x1 = swap(after(x1), "fsdp", 1, line)
-    x3m = across(after(mine))
     rows0 = note(
         gather_blocks(
             after(where),
@@ -413,59 +412,67 @@
             slab(0, 0, 0, (0, 2, 1, 3)),
         )[0]
     )
+    x2 = arrived(x2)
+    y2 = swap_tp(x2, 2, everyone)
+    x1 = arrived(x1)
+    x3m = across(after(x3m))
+    w = [(own_w[0], arrived(other_w[0])), None]
+    back = note(back + after(back_x))
+    other_w[1] = swap(after(own_w[1]), "rep", 1, reps)
     pair = joint(x3e, y3e)
     c3e = swap_tp(pair, 1, ends)
+    back = note(back + after(swap(after(back), "fsdp", 1, line)))
+    rows3e = joint(pair, c3e)
+    a3 = [out(note(product(after(rows3e), w[0]).astype(HALF))), None]
+    y1 = swap_tp(after(x1), 2, everyone)
+    p0 = [note(product(after(rows0), w[0])), None]
     pair2 = joint(x2, y2)
-    c2 = swap_tp(pair2, 1, everyone)
-    w = [(own_w[0], arrived(other_w[0])), None]
-    back = note(back + after(back_x))
-    back_z = summed(back, "fsdp", line)
-    rows3e = joint(pair, c3e)
-    v = note(product(after(rows3e), w[0]).astype(HALF))
-    back, squares = note(
-        whole(functools.partial(length_kernel, widths), (row, lanes), back_z())
-    )
-    a3 = [out(after(v)), None]
-    squares = summed(after(squares), "tp", tp_count)()
+    pair1 = joint(x1, y1)
+    w[1] = (own_w[1], arrived(other_w[1]))
+    a3[1] = out(note(product(after(rows3e), w[1]).astype(HALF)))
+    a3[0] = arrived(a3[0])
+    x3m = arrived(x3m)
+    back_z = swap(after(back), "fsdp", 2, line)
+    c2 = swap_tp(after(pair2), 1, everyone)
+    c1 = swap_tp(after(pair1), 1, everyone)
+    c3m = swap_tp(after(x3m), 1, mids)
+    rows2 = joint(pair2, c2)
+    p2 = [note(product(after(rows2), w[0])), None]
+    v = joined(p2[0], a3[0])
+    a2e, a2m = [out(v), None], [across(v), None]
+    back = note(back + after(back_z))
+    rows1 = joint(pair1, c1)
+    rows3m = joint(x3m, c3m)
+    p2[1] = note(product(after(rows2), w[1]))
+    back, squares = note(whole(functools.partial(length_kernel, widths), (row, lanes), back))
+    p3m = [note(product(after(rows3m), w[0])), None]
+    a2m[0] = arrived(a2m[0])
+    a2e[0] = arrived(a2e[0])
+    v = joined(p2[1], a3[1])
+    a2e[1], a2m[1] = out(v), across(v)
+    a1m = [across(joined(p3m[0], a2e[0])), None]
+    p1 = [note(product(after(rows1), w[0])), None]
+    a1p = [swap(joined(p1[0], a2m[0]), "fsdp", 1, line), None]
+    squares = note(squares + after(swap(after(squares), "tp", 1, tp_count)))
+    squares = note(squares + after(swap(squares, "tp", 2, tp_count)))
+    a2m[1] = arrived(a2m[1])
+    a2e[1] = arrived(a2e[1])
+    p1[1] = note(product(after(rows1), w[1]))
+    a1p[1] = swap(joined(p1[1], a2m[1]), "fsdp", 1, line)
+    p3m[1] = note(product(after(rows3m), w[1]))
+    a1m[1] = across(joined(p3m[1], a2e[1]))
+    p0[1] = note(product(after(rows0), w[1]))
     states = note(
         whole(
             functools.partial(state_kernel, widths, tp_count),
             tuple(jax.ShapeDtypeStruct((1, n), F32) for n in widths) + (lanes, row),
             back,
-            squares,
+            after(squares),
             gammas,
         )
     )
     factors = states[4]
     factor = [factors[:, :wide], factors[:, wide:]]
-    x1 = arrived(x1)
-    y1 = swap_tp(x1, 2, everyone)
-    x3m = arrived(x3m)
-    y3m = swap_tp(x3m, 2, mids)
-    other_w[1] = swap(after(own_w[1]), "rep", 1, reps)
-    rows2 = joint(pair2, c2)
-    p2 = [note(product(after(rows2), w[0])), None]
-    p0 = [note(product(after(rows0), w[0])), None]
-    v = joined(p2[0], a3[0])
-    a2e, a2m = [out(v), None], [across(v), None]
-    pair1 = joint(x1, y1)
-    c1 = swap_tp(pair1, 1, everyone)
-    pair3 = joint(x3m, y3m)
-    c3m = swap_tp(pair3, 1, mids)
-    w[1] = (own_w[1], arrived(other_w[1]))
-    a3[1] = out(note(product(after(rows3e), w[1]).astype(HALF)))
-    p0[1] = note(product(after(rows0), w[1]))
-    p2[1] = note(product(after(rows2), w[1]))
-    rows1 = joint(pair1, c1)
-    p1 = [note(product(after(rows1), w[c])) for c in range(2)]
-    rows3m = joint(pair3, c3m)
-    p3m = [note(product(after(rows3m), w[c])) for c in range(2)]
-    a1p = [swap(joined(p1[0], a2m[0]), "fsdp", 1, line), None]
-    a1m = [across(joined(p3m[0], a2e[0])), None]
-    v = joined(p2[1], a3[1])
-    a2e[1], a2m[1] = out(v), across(v)
-    a1p[1] = swap(joined(p1[1], a2m[1]), "fsdp", 1, line)
-    a1m[1] = across(joined(p3m[1], a2e[1]))
 
     def packed(c):
         near, far = after((a1p[c], a1m[c]))

time: 199 us -> 181 us (0.910)
  waiting for transfers between devices: 68.3 us -> 53.4 us
  starting transfers between devices: 52.9 us -> 44.8 us
  other arithmetic: 12.8 us -> 18.8 us
  matrix products: 32.1 us -> 28.7 us
  local copies, waits for them, and re-layouts: 0.56 us -> 3.62 us
    ppermute x5, waiting for transfers between devices: 21.4 us -> 10.7 us  [across(): return send(x, 'fsdp', [(1, 2), (2, 1)])]
    ppermute x8 -> x7, waiting for transfers between devices: 15.1 us -> 8.68 us  [swap_tp(): return send(x, ('fsdp', 'tp'), pairs)]
    convert_element_type x6, other arithmetic: 2.39 us -> 8.3 us  [joined(): return note((p + after(x).astype(F32)).astype(HALF))]
    dot_general x10, matrix products: 15.5 us -> 9.88 us  [product(): jnp.dot(x[:, :deep], w[0], preferred_element_type=F32)]
    ppermute x8 -> x7, starting transfers between devices: 9.74 us -> 5.33 us  [swap_tp(): return send(x, ('fsdp', 'tp'), pairs)]
    ppermute x15 -> x13, starting transfers between devices: 22 us -> 17.7 us  [swap(): return send(x, axis, [(i, i ^ mask) for i in range(size)])]
    convert_element_type x2, other arithmetic: 2.25 us -> 5.09 us  [packed(): (factor[c] * (p0[c] + near.astype(F32) + far.astype(F32))).astype(BF16)]
    dot_general x10, matrix products: 16.6 us -> 18.8 us  [product(): jnp.dot(x[:, deep:], w[1], preferred_element_type=F32)]
  transfers between devices with their start and end apart: 33 -> 30, of which waited for: 12 -> 13; matrix products, arithmetic and copies ran while one was open for 22% -> 25% of each run, Pallas kernels for 11% -> 12%
where the time goes in v3:
time: 181 us; the launch traced here: 180 us
  waiting for transfers between devices  53.4 us (30%)
  starting transfers between devices  44.8 us (25%)
  Pallas kernels  29.9 us (17%)
  matrix products  28.7 us (16%)
  other arithmetic  18.8 us (10%)
  local copies, waits for them, and re-layouts  3.62 us (2%)
    ppermute x13, waiting for transfers between devices, swap(): return send(x, axis, [(i, i ^ mask) for i in range(size)])  29.6 us
    dot_general x10, matrix products, product(): jnp.dot(x[:, deep:], w[1], preferred_element_type=F32)  18.8 us
    ppermute x13, starting transfers between devices, swap(): return send(x, axis, [(i, i ^ mask) for i in range(size)])  17.7 us
    ppermute x5, starting transfers between devices, across(): return send(x, 'fsdp', [(1, 2), (2, 1)])  15.8 us
    pallas_call x3, Pallas kernels, gather_blocks(): pl.pallas_call(kernel, out_shape=outs, grid_spec=pltpu.PrefetchScalarGrid...  11.6 us
    ppermute x5, waiting for transfers between devices, across(): return send(x, 'fsdp', [(1, 2), (2, 1)])  10.7 us
    dot_general x10, matrix products, product(): jnp.dot(x[:, :deep], w[0], preferred_element_type=F32)  9.88 us
    pallas_call x2, Pallas kernels, context_call(): pl.pallas_call(functools.partial(context_kernel, first, heads), out_shape...  9.57 us
  transfers between devices with their start and end apart: 30, of which 13 were waited for; matrix products, arithmetic and copies ran while one was open for 25% of the time, Pallas kernels for 12%

profile of v3, /device:TPU:8, one launch (start us, length us, event | category | flops | bytes accessed | tf_op | source)
XLA Modules:
  0.0 180.4 jit_solution(14501607558854423911)
XLA Ops:
  1.3 3.7 %shard_map.128 = (bf16[128,2048]{1,0:T(8,128)(2,1)}, bf16[1024,768]{1,0:T(8,128)(2,1)}) custom-call(s32[3]{0:T(128)} %pad_add_fusion.where_ref.place, bf16[512,8192]{1,0:T(8,128)(2,1)} %refs_0_.5, bf16[1024,128]{1,0:T(8,128)(2,1)} %wk.3, bf16[1024,128]{1,0:T(8,128)(2,1)} %wv.3, bf16[1024,1024]{1,0:T(8,128)(2,1)} %wq.3), custom_call_target="tpu_custom_call" | custom-call | flops 1 | bytes 1 | tf_op jit(solution)/shard_map/pallas_call | solution.py:167
  4.9 1.6 collective-permute-start.3
  7.2 4.3 %shard_map.129 = (bf16[128,2048]{1,0:T(8,128)(2,1)}, bf16[128,2048]{1,0:T(8,128)(2,1)}, bf16[256,2048]{1,0:T(8,128)(2,1)}, bf16[1024,512]{1,0:T(8,128)(2,1)}) custom-call(s32[3]{0:T(128)} %pad_add_fusion.where_ref.place, bf16[512,8192]{1,0:T(8,128)(2,1)} %refs_0_.5, bf16[1024,1024]{1,0:T(8,128)(2,1)} %wq.3), custom_call_target="tpu_custom_call" | custom-call | flops 1 | bytes 1 | tf_op jit(solution)/shard_map/pallas_call | solution.py:167
  11.5 3.2 %shard_map.130 = f32[3,1024]{1,0:T(4,128)} custom-call(bf16[1024,1024]{1,0:T(8,128)(2,1)} %wq.3, bf16[1024,128]{1,0:T(8,128)(2,1)} %wk.3, bf16[1024,128]{1,0:T(8,128)(2,1)} %wv.3, f32[1,1024]{1,0:T(1,128)} %bitcast.33, f32[1,128]{1,0:T(1,128)} %bitcast.34, f32[1,128]{1,0:T(1,128)} %bitcast.35), custom_call_target="tpu_custom_call" | custom-call | flops 1 | bytes 1 | tf_op jit(solution)/shard_map/pallas_call | solution.py:147
  14.7 1.4 collective-permute-done
  16.1 0.7 add.81
  16.8 1.5 collective-permute-start.1
  18.3 4.0 %collective-permute-start.5 = (bf16[128,2048]{1,0:T(8,128)(2,1)S(1)}, bf16[128,2048]{1,0:T(8,128)(2,1)S(1)}, u32[]{:S(2)}, u32[]{:S(2)}) collective-permute-start(bf16[128,2048]{1,0:T(8,128)(2,1)S(1)} %copy-done.11), channel_id=1, source_target_pairs={{0,8},{4,12},{8,0},{12,4},{1,9},{5,13},{9,1},{13,5},{2,10},{6,14},... | collective-permute-start | bytes 1572872 | tf_op jit(solution)/shard_map/ppermute | solution.py:287
  22.4 1.3 collective-permute-start.4
  24.3 2.8 %shard_map.131 = f32[1,1408]{1,0:T(1,128)} custom-call(bf16[1024,1024]{1,0:T(8,128)(2,1)} %wq.3, bf16[1024,128]{1,0:T(8,128)(2,1)} %wk.3, bf16[1024,128]{1,0:T(8,128)(2,1)} %wv.3, f32[3,1024]{1,0:T(4,128)} %add.82.image), custom_call_target="tpu_custom_call" | custom-call | flops 1 | bytes 1 | tf_op jit(solution)/shard_map/pallas_call | solution.py:147
  27.0 0.8 collective-permute-start.7
  28.5 3.6 %shard_map.132 = bf16[512,2048]{1,0:T(8,128)(2,1)} custom-call(s32[3]{0:T(128)} %pad_add_fusion.where_ref.place, bf16[512,8192]{1,0:T(8,128)(2,1)} %refs_0_.5), custom_call_target="tpu_custom_call" | custom-call | flops 1 | bytes 1 | tf_op jit(solution)/shard_map/pallas_call | solution.py:167
  32.1 13.4 %collective-permute-done.5 = bf16[128,2048]{1,0:T(8,128)(2,1)S(1)} collective-permute-done((bf16[128,2048]{1,0:T(8,128)(2,1)S(1)}, bf16[128,2048]{1,0:T(8,128)(2,1)S(1)}, u32[]{:S(2)}, u32[]{:S(2)}) %collective-permute-start.5) | collective-permute-done | bytes 524320 | tf_op jit(solution)/shard_map/ppermute | solution.py:287
  45.5 1.3 collective-permute-done.4
  47.0 0.7 collective-permute-start.10
  47.7 3.1 %collective-permute-start.8 = (f32[1,1408]{1,0:T(1,128)S(1)}, f32[1,1408]{1,0:T(1,128)S(1)}, u32[]{:S(2)}, u32[]{:S(2)}) collective-permute-start(f32[1,1408]{1,0:T(1,128)S(1)} %add.83), channel_id=1, source_target_pairs={{0,4},{4,0},{8,12},{12,8},{1,5},{5,1},{9,13},{13,9},{2,6},{6,2},{1... | collective-permute-start | bytes 16904 | tf_op jit(solution)/shard_map/ppermute | solution.py:287
  51.3 3.7 %collective-permute-start.9 = (bf16[256,2048]{1,0:T(8,128)(2,1)S(1)}, bf16[256,2048]{1,0:T(8,128)(2,1)S(1)}, u32[]{:S(2)}, u32[]{:S(2)}) collective-permute-start(bf16[256,2048]{1,0:T(8,128)(2,1)S(1)} %copy-done.9), channel_id=1, source_target_pairs={{4,8},{8,4},{5,9},{9,5},{6,10},{10,6},{7,11},{11,7},{20,24},{24,20... | collective-permute-start | bytes 3145736 | tf_op jit(solution)/shard_map/ppermute | solution.py:330
  55.9 1.1 copy-done.5
  57.1 1.0 fusion.29
  58.1 2.5 %add_convert_fusion.3 = f16[512,768]{1,0:T(8,128)(2,1)S(1)} fusion(f32[512,768]{1,0:T(8,128)S(1)} %fusion.29, bf16[1024,768]{1,0:T(8,128)(2,1)} %collective-permute-done.3, bf16[512,2048]{1,0:T(8,128)(2,1)S(1)} %pad_maximum_fusion), kind=kOutput, calls=%fused_computation.8 | convolution fusion | flops 806092800 | bytes 4980736 | tf_op jit(solution)/shard_map/dot_general | solution.py:319
  60.6 0.8 collective-permute-start.13
  61.4 1.0 fusion.26
  62.4 3.6 %convolution_add_fusion.3 = f32[512,768]{1,0:T(8,128)} fusion(f32[512,768]{1,0:T(8,128)S(1)} %fusion.26, bf16[1024,768]{1,0:T(8,128)(2,1)} %collective-permute-done.3, bf16[512,2048]{1,0:T(8,128)(2,1)S(1)} %copy-done.1), kind=kOutput, calls=%fused_computation.12 | convolution fusion | flops 805699584 | bytes 5767168 | tf_op jit(solution)/shard_map/dot_general | solution.py:319
  66.1 1.3 collective-permute-start.11
  67.4 8.7 %collective-permute-done.13 = bf16[128,2048]{1,0:T(8,128)(2,1)S(1)} collective-permute-done((bf16[128,2048]{1,0:T(8,128)(2,1)S(1)}, bf16[128,2048]{1,0:T(8,128)(2,1)S(1)}, u32[]{:S(2)}, u32[]{:S(2)}) %collective-permute-start.13) | collective-permute-done | bytes 524320 | tf_op jit(solution)/shard_map/ppermute | solution.py:291
  76.1 3.7 %collective-permute-done.12 = bf16[1024,512]{1,0:T(8,128)(2,1)S(1)} collective-permute-done((bf16[1024,512]{1,0:T(8,128)(2,1)S(1)}, bf16[1024,512]{1,0:T(8,128)(2,1)S(1)}, u32[]{:S(2)}, u32[]{:S(2)}) %collective-permute-start.12) | collective-permute-done | bytes 1048608 | tf_op jit(solution)/shard_map/ppermute | solution.py:287
  80.5 1.6 fusion
  82.1 4.4 %collective-permute-done.11 = f16[512,768]{1,0:T(8,128)(2,1)S(1)} collective-permute-done((f16[512,768]{1,0:T(8,128)(2,1)S(1)}, f16[512,768]{1,0:T(8,128)(2,1)S(1)}, u32[]{:S(2)}, u32[]{:S(2)}) %collective-permute-start.11) | collective-permute-done | bytes 786464 | tf_op jit(solution)/shard_map/ppermute | solution.py:327
  86.5 1.3 collective-permute-start.21
  88.4 3.5 %collective-permute-start.15 = (f32[1,1408]{1,0:T(1,128)S(1)}, f32[1,1408]{1,0:T(1,128)S(1)}, u32[]{:S(2)}, u32[]{:S(2)}) collective-permute-start(f32[1,1408]{1,0:T(1,128)S(1)} %add.84), channel_id=1, source_target_pairs={{0,8},{4,12},{8,0},{12,4},{1,9},{5,13},{9,1},{13,5},{2,10},{6,14},... | collective-permute-start | bytes 16904 | tf_op jit(solution)/shard_map/ppermute | solution.py:287
  91.9 1.9 %collective-permute-start.17 = (bf16[256,2048]{1,0:T(8,128)(2,1)S(1)}, bf16[256,2048]{1,0:T(8,128)(2,1)S(1)}, u32[]{:S(2)}, u32[]{:S(2)}) collective-permute-start(bf16[256,2048]{1,0:T(8,128)(2,1)S(1)} %collective-permute-done.9), channel_id=1, source_target_pairs={{4,5},{5,4},{6,7},{7,6},{8,9},{9,8},{10,11},{11,10},{20,21},{21,20... | collective-permute-start | bytes 3145736 | tf_op jit(solution)/shard_map/ppermute | solution.py:291
  94.0 1.0 fusion.20
  95.0 2.4 %convolution_add_fusion.2 = f32[512,768]{1,0:T(8,128)S(1)} fusion(f32[512,768]{1,0:T(8,128)S(1)} %fusion.20, bf16[1024,768]{1,0:T(8,128)(2,1)} %collective-permute-done.3, bf16[512,2048]{1,0:T(8,128)(2,1)S(1)} %pad_maximum_fusion.1), kind=kOutput, calls=%fused_computation.11 | convolution fusion | flops 805699584 | bytes 5767168 | tf_op jit(solution)/shard_map/dot_general | solution.py:319
  97.4 1.1 add_convert_fusion.2
  98.5 1.3 collective-permute-start.19
  99.8 3.7 %collective-permute-done.15 = f32[1,1408]{1,0:T(1,128)S(1)} collective-permute-done((f32[1,1408]{1,0:T(1,128)S(1)}, f32[1,1408]{1,0:T(1,128)S(1)}, u32[]{:S(2)}, u32[]{:S(2)}) %collective-permute-start.15) | collective-permute-done | bytes 5664 | tf_op jit(solution)/shard_map/ppermute | solution.py:287
  103.5 3.1 %collective-permute-start.20 = (f16[512,768]{1,0:T(8,128)(2,1)}, f16[512,768]{1,0:T(8,128)(2,1)}, u32[]{:S(2)}, u32[]{:S(2)}) collective-permute-start(f16[512,768]{1,0:T(8,128)(2,1)} %add_convert_fusion.2), channel_id=1, source_target_pairs={{4,8},{8,4},{5,9},{9,5},{6,10},{10,6},{7,11},{11,7},{20,24},{24,20... | collective-permute-start | bytes 2359304 | tf_op jit(solution)/shard_map/ppermute | solution.py:330
  107.2 1.5 pad_maximum_fusion.2
  109.6 1.7 convolution_add_fusion.7
  111.3 1.4 shard_map.133
  112.7 2.4 %fusion.14 = f32[512,768]{1,0:T(8,128)S(1)} fusion(bf16[1024,768]{1,0:T(8,128)(2,1)} %get-tuple-element.239, bf16[512,2048]{1,0:T(8,128)(2,1)S(1)} %pad_maximum_fusion.3), kind=kOutput, calls=%fused_computation.39 | convolution fusion | flops 805306368 | bytes 4194304 | tf_op jit(solution)/shard_map/dot_general | solution.py:319
  115.1 2.5 %convolution_add_fusion.1 = f32[512,768]{1,0:T(8,128)S(1)} fusion(f32[512,768]{1,0:T(8,128)S(1)} %fusion.14, bf16[1024,768]{1,0:T(8,128)(2,1)} %collective-permute-done.3, bf16[512,2048]{1,0:T(8,128)(2,1)S(1)} %pad_maximum_fusion.3), kind=kOutput, calls=%fused_computation.10 | convolution fusion | flops 805699584 | bytes 5767168 | tf_op jit(solution)/shard_map/dot_general | solution.py:319
  117.6 7.0 %collective-permute-done.20 = f16[512,768]{1,0:T(8,128)(2,1)} collective-permute-done((f16[512,768]{1,0:T(8,128)(2,1)}, f16[512,768]{1,0:T(8,128)(2,1)}, u32[]{:S(2)}, u32[]{:S(2)}) %collective-permute-start.20) | collective-permute-done | bytes 786464 | tf_op jit(solution)/shard_map/ppermute | solution.py:330
  124.6 1.4 add_convert_fusion.6
  126.0 1.4 collective-permute-start.24
  127.4 3.0 %collective-permute-start.25 = (f16[512,512]{1,0:T(8,128)(2,1)S(1)}, f16[512,512]{1,0:T(8,128)(2,1)S(1)}, u32[]{:S(2)}, u32[]{:S(2)}) collective-permute-start(f16[512,512]{1,0:T(8,128)(2,1)S(1)} %add_convert_fusion.6), channel_id=1, source_target_pairs={{4,8},{8,4},{5,9},{9,5},{6,10},{10,6},{7,11},{11,7},{20,24},{24,20... | collective-permute-start | bytes 1572872 | tf_op jit(solution)/shard_map/ppermute | solution.py:330
  130.4 2.3 %add_convert_fusion.1 = f16[512,768]{1,0:T(8,128)(2,1)} fusion(f32[512,768]{1,0:T(8,128)S(1)} %convolution_add_fusion.1, f16[512,768]{1,0:T(8,128)(2,1)} %collective-permute-done.19), kind=kLoop, calls=%fused_computation.6 | loop fusion | flops 1179648 | bytes 3145728 | tf_op jit(solution)/shard_map/convert_element_type | solution.py:403
  132.6 1.0 fusion.11
  133.6 2.4 %convolution_add_fusion = f32[512,768]{1,0:T(8,128)S(1)} fusion(f32[512,768]{1,0:T(8,128)S(1)} %fusion.11, bf16[1024,768]{1,0:T(8,128)(2,1)} %collective-permute-done.3, bf16[512,2048]{1,0:T(8,128)(2,1)S(1)} %copy-done), kind=kOutput, calls=%fused_computation.9 | convolution fusion | flops 805699584 | bytes 5767168 | tf_op jit(solution)/shard_map/dot_general | solution.py:319
  136.0 2.4 %add_convert_fusion = f16[512,768]{1,0:T(8,128)(2,1)} fusion(f32[512,768]{1,0:T(8,128)S(1)} %convolution_add_fusion, f16[512,768]{1,0:T(8,128)(2,1)} %collective-permute-done.20), kind=kLoop, calls=%fused_computation.5 | loop fusion | flops 1179648 | bytes 3145728 | tf_op jit(solution)/shard_map/convert_element_type | solution.py:403
  138.4 1.1 collective-permute-done.22
  139.5 1.3 collective-permute-start.23
  140.9 3.3 %collective-permute-start.29 = (f16[512,768]{1,0:T(8,128)(2,1)}, f16[512,768]{1,0:T(8,128)(2,1)}, u32[]{:S(2)}, u32[]{:S(2)}) collective-permute-start(f16[512,768]{1,0:T(8,128)(2,1)} %add_convert_fusion.1), channel_id=1, source_target_pairs={{4,8},{8,4},{5,9},{9,5},{6,10},{10,6},{7,11},{11,7},{20,24},{24,20... | collective-permute-start | bytes 2359304 | tf_op jit(solution)/shard_map/ppermute | solution.py:330
  146.2 1.0 add_convert_fusion.5
  149.0 2.6 %collective-permute-start.27 = (f16[512,512]{1,0:T(8,128)(2,1)S(1)}, f16[512,512]{1,0:T(8,128)(2,1)S(1)}, u32[]{:S(2)}, u32[]{:S(2)}) collective-permute-start(f16[512,512]{1,0:T(8,128)(2,1)S(1)} %add_convert_fusion.4), channel_id=1, source_target_pairs={{4,8},{8,4},{5,9},{9,5},{6,10},{10,6},{7,11},{11,7},{20,24},{24,20... | collective-permute-start | bytes 1572872 | tf_op jit(solution)/shard_map/ppermute | solution.py:330
  153.1 1.5 shard_map.134
  155.9 1.1 slice_bitcast_fusion
  157.0 4.5 %collective-permute-done.28 = f16[512,768]{1,0:T(8,128)(2,1)} collective-permute-done((f16[512,768]{1,0:T(8,128)(2,1)}, f16[512,768]{1,0:T(8,128)(2,1)}, u32[]{:S(2)}, u32[]{:S(2)}) %collective-permute-start.28) | collective-permute-done | bytes 786464 | tf_op jit(solution)/shard_map/ppermute | solution.py:287
  161.6 1.9 %collective-permute-done.29 = f16[512,768]{1,0:T(8,128)(2,1)} collective-permute-done((f16[512,768]{1,0:T(8,128)(2,1)}, f16[512,768]{1,0:T(8,128)(2,1)}, u32[]{:S(2)}, u32[]{:S(2)}) %collective-permute-start.29) | collective-permute-done | bytes 786464 | tf_op jit(solution)/shard_map/ppermute | solution.py:330
  163.5 3.0 %multiply_convert_fusion.packed = bf16[512,768]{1,0:T(8,128)(2,1)} fusion(f16[512,768]{1,0:T(8,128)(2,1)} %collective-permute-done.29, f32[512,768]{1,0:T(8,128)} %convolution_add_fusion.3, f16[512,768]{1,0:T(8,128)(2,1)} %collective-permute-done.28, f32[768]{0:T(1024)S(1)} %slice_reduce_fusion), kind=kLoop, calls=%fused_computation.4 | loop fusion | flops 2359296 | bytes 3935232 | tf_op jit(solution)/shard_map/convert_element_type | solution.py:479
  166.5 4.8 %shard_map.135 = (bf16[512,1024]{1,0:T(8,128)(2,1)}, bf16[512,128]{1,0:T(8,128)(2,1)}, bf16[512,128]{1,0:T(8,128)(2,1)}) custom-call(s32[3]{0:T(128)} %pad_add_fusion.where_ref.place, s32[1,8]{1,0:T(1,128)} %lengths.1, bf16[512,768]{1,0:T(8,128)(2,1)} %multiply_convert_fusion.packed), custom_call_target="tpu_custom_call" | custom-call | flops 1 | bytes 1 | tf_op jit(solution)/shard_map/pallas_call | solution.py:248
  171.8 1.8 collective-permute-done.27
  173.6 2.1 %multiply_convert_fusion.1.packed = bf16[512,512]{1,0:T(8,128)(2,1)} fusion(f16[512,512]{1,0:T(8,128)(2,1)S(1)} %collective-permute-done.27, f32[512,512]{1,0:T(8,128)S(1)} %convolution_add_fusion.4, f16[512,512]{1,0:T(8,128)(2,1)} %collective-permute-done.26, f32[512]{0:T(512)S(1)} %bitcast.32), kind=kLoop, calls=%fused_computation.22 | loop fusion | flops 1572864 | bytes 2623488 | tf_op jit(solution)/shard_map/convert_element_type | solution.py:479
  175.6 4.8 %shard_map.136 = bf16[512,1024]{1,0:T(8,128)(2,1)} custom-call(s32[3]{0:T(128)} %pad_add_fusion.where_ref.place, s32[1,8]{1,0:T(1,128)} %lengths.1, bf16[512,512]{1,0:T(8,128)(2,1)} %multiply_convert_fusion.1.packed, bf16[512,128]{1,0:T(8,128)(2,1)} %get-tuple-element.428.refs_0_, ...), custom_call_target="tpu_custom_call", output_to_operand_aliasing={{}: (5, {})} | custom-call | flops 1 | bytes 1 | tf_op jit(solution)/shard_map/pallas_call | solution.py:248
  (77 shorter events, 14.2 us)
Async XLA Ops:
  4.9 41.9 %collective-permute-start.3 = (bf16[1024,768]{1,0:T(8,128)(2,1)}, bf16[1024,768]{1,0:T(8,128)(2,1)}, u32[]{:S(2)}, u32[]{:S(2)}) collective-permute-start(bf16[1024,768]{1,0:T(8,128)(2,1)} %get-tuple-element.239), channel_id=1, source_target_pairs={{0,16},{16,0},{1,17},{17,1},{2,18},{18,2},{3,19},{19,3},{4,20},{20... | collective-permute-start | bytes 4718600 | tf_op jit(solution)/shard_map/ppermute | solution.py:287
  6.5 20.6 %collective-permute-start.6 = (bf16[128,2048]{1,0:T(8,128)(2,1)}, bf16[128,2048]{1,0:T(8,128)(2,1)S(1)}, u32[]{:S(2)}, u32[]{:S(2)}) collective-permute-start(bf16[128,2048]{1,0:T(8,128)(2,1)} %get-tuple-element.243), channel_id=1, source_target_pairs={{0,12},{12,0},{1,13},{13,1},{2,14},{14,2},{3,15},{15,3},{16,28},{2... | collective-permute-start | bytes 1572872 | tf_op jit(solution)/shard_map/ppermute | solution.py:353
  11.5 6.9 %copy-start.11 = (bf16[128,2048]{1,0:T(8,128)(2,1)S(1)}, bf16[128,2048]{1,0:T(8,128)(2,1)}, u32[]{:S(2)}) copy-start(bf16[128,2048]{1,0:T(8,128)(2,1)} %get-tuple-element.242) | copy-start | bytes 1572868
  11.5 10.9 %copy-start.10 = (bf16[128,2048]{1,0:T(8,128)(2,1)S(1)}, bf16[128,2048]{1,0:T(8,128)(2,1)}, u32[]{:S(2)}) copy-start(bf16[128,2048]{1,0:T(8,128)(2,1)} %get-tuple-element.241) | copy-start | bytes 1572868
  14.7 1.4 collective-permute-start
  16.8 6.9 %collective-permute-start.1 = (f32[3,1024]{1,0:T(4,128)S(1)}, f32[3,1024]{1,0:T(4,128)S(1)}, u32[]{:S(2)}, u32[]{:S(2)}) collective-permute-start(f32[3,1024]{1,0:T(4,128)S(1)} %add.81), channel_id=1, source_target_pairs={{0,2},{1,3},{2,0},{3,1},{4,6},{5,7},{6,4},{7,5},{8,10},{9,11},{10,... | collective-permute-start | bytes 36872 | tf_op jit(solution)/shard_map/ppermute | solution.py:287
  18.3 27.2 %collective-permute-start.5 = (bf16[128,2048]{1,0:T(8,128)(2,1)S(1)}, bf16[128,2048]{1,0:T(8,128)(2,1)S(1)}, u32[]{:S(2)}, u32[]{:S(2)}) collective-permute-start(bf16[128,2048]{1,0:T(8,128)(2,1)S(1)} %copy-done.11), channel_id=1, source_target_pairs={{0,8},{4,12},{8,0},{12,4},{1,9},{5,13},{9,1},{13,5},{2,10},{6,14},... | collective-permute-start | bytes 1572872 | tf_op jit(solution)/shard_map/ppermute | solution.py:287
  22.4 24.4 %collective-permute-start.4 = (bf16[128,2048]{1,0:T(8,128)(2,1)S(1)}, bf16[128,2048]{1,0:T(8,128)(2,1)S(1)}, u32[]{:S(2)}, u32[]{:S(2)}) collective-permute-start(bf16[128,2048]{1,0:T(8,128)(2,1)S(1)} %copy-done.10), channel_id=1, source_target_pairs={{0,4},{4,0},{8,12},{12,8},{1,5},{5,1},{9,13},{13,9},{2,6},{6,2},{1... | collective-permute-start | bytes 1572872 | tf_op jit(solution)/shard_map/ppermute | solution.py:287
  27.0 19.8 %copy-start.4 = (f32[1,1408]{1,0:T(1,128)S(1)}, f32[1,1408]{1,0:T(1,128)}, u32[]{:S(2)}) copy-start(f32[1,1408]{1,0:T(1,128)} %shard_map.131) | copy-start | bytes 16900
  27.0 19.8 %collective-permute-start.7 = (bf16[128,2048]{1,0:T(8,128)(2,1)S(1)}, bf16[128,2048]{1,0:T(8,128)(2,1)S(1)}, u32[]{:S(2)}, u32[]{:S(2)}) collective-permute-start(bf16[128,2048]{1,0:T(8,128)(2,1)S(1)} %collective-permute-done.6), channel_id=1, source_target_pairs={{0,2},{1,3},{2,0},{3,1},{12,14},{13,15},{14,12},{15,13},{16,18},{1... | collective-permute-start | bytes 1572872 | tf_op jit(solution)/shard_map/ppermute | solution.py:291
  27.9 18.9 %collective-permute-start.2 = (f32[1,1408]{1,0:T(1,128)}, f32[1,1408]{1,0:T(1,128)S(1)}, u32[]{:S(2)}, u32[]{:S(2)}) collective-permute-start(f32[1,1408]{1,0:T(1,128)} %shard_map.131), channel_id=1, source_target_pairs={{0,16},{16,0},{1,17},{17,1},{2,18},{18,2},{3,19},{19,3},{4,20},{20... | collective-permute-start | bytes 16904 | tf_op jit(solution)/shard_map/ppermute | solution.py:287
  32.1 19.2 %copy-start.9 = (bf16[256,2048]{1,0:T(8,128)(2,1)S(1)}, bf16[256,2048]{1,0:T(8,128)(2,1)}, u32[]{:S(2)}) copy-start(bf16[256,2048]{1,0:T(8,128)(2,1)} %get-tuple-element.268) | copy-start | bytes 3145732
  32.1 22.9 %copy-start.7 = (bf16[1024,512]{1,0:T(8,128)(2,1)S(1)}, bf16[1024,512]{1,0:T(8,128)(2,1)}, u32[]{:S(2)}) copy-start(bf16[1024,512]{1,0:T(8,128)(2,1)} %get-tuple-element.278) | copy-start | bytes 3145732
  47.0 8.7 %collective-permute-start.10 = (bf16[256,2048]{1,0:T(8,128)(2,1)S(1)}, bf16[256,2048]{1,0:T(8,128)(2,1)S(1)}, u32[]{:S(2)}, u32[]{:S(2)}) collective-permute-start(bf16[256,2048]{1,0:T(8,128)(2,1)S(1)} %pad_maximum_fusion.4), channel_id=1, source_target_pairs={{0,1},{1,0},{2,3},{3,2},{12,13},{13,12},{14,15},{15,14},{16,17},{1... | collective-permute-start | bytes 3145736 | tf_op jit(solution)/shard_map/ppermute | solution.py:291
  47.7 8.0 %collective-permute-start.8 = (f32[1,1408]{1,0:T(1,128)S(1)}, f32[1,1408]{1,0:T(1,128)S(1)}, u32[]{:S(2)}, u32[]{:S(2)}) collective-permute-start(f32[1,1408]{1,0:T(1,128)S(1)} %add.83), channel_id=1, source_target_pairs={{0,4},{4,0},{8,12},{12,8},{1,5},{5,1},{9,13},{13,9},{2,6},{6,2},{1... | collective-permute-start | bytes 16904 | tf_op jit(solution)/shard_map/ppermute | solution.py:287
  50.8 15.2 %collective-permute-start.14 = (bf16[128,2048]{1,0:T(8,128)(2,1)S(1)}, bf16[128,2048]{1,0:T(8,128)(2,1)S(1)}, u32[]{:S(2)}, u32[]{:S(2)}) collective-permute-start(bf16[128,2048]{1,0:T(8,128)(2,1)S(1)} %collective-permute-done.5), channel_id=1, source_target_pairs={{0,2},{1,3},{2,0},{3,1},{4,6},{5,7},{6,4},{7,5},{8,10},{9,11},{10,... | collective-permute-start | bytes 1572872 | tf_op jit(solution)/shard_map/ppermute | solution.py:291
  51.3 35.2 %collective-permute-start.9 = (bf16[256,2048]{1,0:T(8,128)(2,1)S(1)}, bf16[256,2048]{1,0:T(8,128)(2,1)S(1)}, u32[]{:S(2)}, u32[]{:S(2)}) collective-permute-start(bf16[256,2048]{1,0:T(8,128)(2,1)S(1)} %copy-done.9), channel_id=1, source_target_pairs={{4,8},{8,4},{5,9},{9,5},{6,10},{10,6},{7,11},{11,7},{20,24},{24,20... | collective-permute-start | bytes 3145736 | tf_op jit(solution)/shard_map/ppermute | solution.py:330
  55.0 24.8 %collective-permute-start.12 = (bf16[1024,512]{1,0:T(8,128)(2,1)S(1)}, bf16[1024,512]{1,0:T(8,128)(2,1)S(1)}, u32[]{:S(2)}, u32[]{:S(2)}) collective-permute-start(bf16[1024,512]{1,0:T(8,128)(2,1)S(1)} %copy-done.7), channel_id=1, source_target_pairs={{0,16},{16,0},{1,17},{17,1},{2,18},{18,2},{3,19},{19,3},{4,20},{20... | collective-permute-start | bytes 3145736 | tf_op jit(solution)/shard_map/ppermute | solution.py:287
  55.6 1.4 copy-start.5
  58.1 3.4 %copy-start.1 = (bf16[512,2048]{1,0:T(8,128)(2,1)S(1)}, bf16[512,2048]{1,0:T(8,128)(2,1)}, u32[]{:S(2)}) copy-start(bf16[512,2048]{1,0:T(8,128)(2,1)} %shard_map.132) | copy-start | bytes 6291460
  60.6 15.4 %collective-permute-start.13 = (bf16[128,2048]{1,0:T(8,128)(2,1)S(1)}, bf16[128,2048]{1,0:T(8,128)(2,1)S(1)}, u32[]{:S(2)}, u32[]{:S(2)}) collective-permute-start(bf16[128,2048]{1,0:T(8,128)(2,1)S(1)} %collective-permute-done.4), channel_id=1, source_target_pairs={{0,2},{1,3},{2,0},{3,1},{4,6},{5,7},{6,4},{7,5},{8,10},{9,11},{10,... | collective-permute-start | bytes 1572872 | tf_op jit(solution)/shard_map/ppermute | solution.py:291
  66.1 20.4 %collective-permute-start.11 = (f16[512,768]{1,0:T(8,128)(2,1)S(1)}, f16[512,768]{1,0:T(8,128)(2,1)S(1)}, u32[]{:S(2)}, u32[]{:S(2)}) collective-permute-start(f16[512,768]{1,0:T(8,128)(2,1)S(1)} %add_convert_fusion.3), channel_id=1, source_target_pairs={{0,4},{12,8},{1,5},{13,9},{2,6},{14,10},{3,7},{15,11},{16,20},{28,... | collective-permute-start | bytes 2359304 | tf_op jit(solution)/shard_map/ppermute | solution.py:327
  86.5 7.3 %collective-permute-start.16 = (bf16[256,2048]{1,0:T(8,128)(2,1)S(1)}, bf16[256,2048]{1,0:T(8,128)(2,1)S(1)}, u32[]{:S(2)}, u32[]{:S(2)}) collective-permute-start(bf16[256,2048]{1,0:T(8,128)(2,1)S(1)} %pad_maximum_fusion.5), channel_id=1, source_target_pairs={{0,1},{1,0},{2,3},{3,2},{4,5},{5,4},{6,7},{7,6},{8,9},{9,8},{10,11... | collective-permute-start | bytes 3145736 | tf_op jit(solution)/shard_map/ppermute | solution.py:291
  86.5 38.0 %collective-permute-start.21 = (f16[512,512]{1,0:T(8,128)(2,1)}, f16[512,512]{1,0:T(8,128)(2,1)}, u32[]{:S(2)}, u32[]{:S(2)}) collective-permute-start(f16[512,512]{1,0:T(8,128)(2,1)} %fusion), channel_id=1, source_target_pairs={{0,4},{12,8},{1,5},{13,9},{2,6},{14,10},{3,7},{15,11},{16,20},{28,... | collective-permute-start | bytes 1572872 | tf_op jit(solution)/shard_map/ppermute | solution.py:327
  87.8 19.4 %collective-permute-start.18 = (bf16[256,2048]{1,0:T(8,128)(2,1)S(1)}, bf16[256,2048]{1,0:T(8,128)(2,1)S(1)}, u32[]{:S(2)}, u32[]{:S(2)}) collective-permute-start(bf16[256,2048]{1,0:T(8,128)(2,1)S(1)} %pad_maximum_fusion.6), channel_id=1, source_target_pairs={{0,1},{1,0},{2,3},{3,2},{4,5},{5,4},{6,7},{7,6},{8,9},{9,8},{10,11... | collective-permute-start | bytes 3145736 | tf_op jit(solution)/shard_map/ppermute | solution.py:291
  88.4 15.1 %collective-permute-start.15 = (f32[1,1408]{1,0:T(1,128)S(1)}, f32[1,1408]{1,0:T(1,128)S(1)}, u32[]{:S(2)}, u32[]{:S(2)}) collective-permute-start(f32[1,1408]{1,0:T(1,128)S(1)} %add.84), channel_id=1, source_target_pairs={{0,8},{4,12},{8,0},{12,4},{1,9},{5,13},{9,1},{13,5},{2,10},{6,14},... | collective-permute-start | bytes 16904 | tf_op jit(solution)/shard_map/ppermute | solution.py:287
  91.9 16.8 %collective-permute-start.17 = (bf16[256,2048]{1,0:T(8,128)(2,1)S(1)}, bf16[256,2048]{1,0:T(8,128)(2,1)S(1)}, u32[]{:S(2)}, u32[]{:S(2)}) collective-permute-start(bf16[256,2048]{1,0:T(8,128)(2,1)S(1)} %collective-permute-done.9), channel_id=1, source_target_pairs={{4,5},{5,4},{6,7},{7,6},{8,9},{9,8},{10,11},{11,10},{20,21},{21,20... | collective-permute-start | bytes 3145736 | tf_op jit(solution)/shard_map/ppermute | solution.py:291
  98.5 26.1 %collective-permute-start.19 = (f16[512,768]{1,0:T(8,128)(2,1)}, f16[512,768]{1,0:T(8,128)(2,1)}, u32[]{:S(2)}, u32[]{:S(2)}) collective-permute-start(f16[512,768]{1,0:T(8,128)(2,1)} %add_convert_fusion.2), channel_id=1, source_target_pairs={{0,4},{12,8},{1,5},{13,9},{2,6},{14,10},{3,7},{15,11},{16,20},{28,... | collective-permute-start | bytes 2359304 | tf_op jit(solution)/shard_map/ppermute | solution.py:327
  103.5 21.1 %collective-permute-start.20 = (f16[512,768]{1,0:T(8,128)(2,1)}, f16[512,768]{1,0:T(8,128)(2,1)}, u32[]{:S(2)}, u32[]{:S(2)}) collective-permute-start(f16[512,768]{1,0:T(8,128)(2,1)} %add_convert_fusion.2), channel_id=1, source_target_pairs={{4,8},{8,4},{5,9},{9,5},{6,10},{10,6},{7,11},{11,7},{20,24},{24,20... | collective-permute-start | bytes 2359304 | tf_op jit(solution)/shard_map/ppermute | solution.py:330
  115.1 9.5 %copy-start.3 = (f32[512,512]{1,0:T(8,128)S(1)}, f32[512,512]{1,0:T(8,128)}, u32[]{:S(2)}) copy-start(f32[512,512]{1,0:T(8,128)} %convolution_add_fusion.7) | copy-start | bytes 3145732
  124.6 8.0 %copy-start.6 = (bf16[1024,768]{1,0:T(8,128)(2,1)S(1)}, bf16[1024,768]{1,0:T(8,128)(2,1)}, u32[]{:S(2)}) copy-start(bf16[1024,768]{1,0:T(8,128)(2,1)} %get-tuple-element.239) | copy-start | bytes 4718596
  126.0 6.7 %copy-start = (bf16[512,2048]{1,0:T(8,128)(2,1)S(1)}, bf16[512,2048]{1,0:T(8,128)(2,1)}, u32[]{:S(2)}) copy-start(bf16[512,2048]{1,0:T(8,128)(2,1)} %pad_maximum_fusion.2) | copy-start | bytes 6291460
  126.0 18.8 %collective-permute-start.24 = (f16[512,512]{1,0:T(8,128)(2,1)S(1)}, f16[512,512]{1,0:T(8,128)(2,1)S(1)}, u32[]{:S(2)}, u32[]{:S(2)}) collective-permute-start(f16[512,512]{1,0:T(8,128)(2,1)S(1)} %add_convert_fusion.6), channel_id=1, source_target_pairs={{0,4},{12,8},{1,5},{13,9},{2,6},{14,10},{3,7},{15,11},{16,20},{28,... | collective-permute-start | bytes 1572872 | tf_op jit(solution)/shard_map/ppermute | solution.py:327
  127.4 17.3 %collective-permute-start.25 = (f16[512,512]{1,0:T(8,128)(2,1)S(1)}, f16[512,512]{1,0:T(8,128)(2,1)S(1)}, u32[]{:S(2)}, u32[]{:S(2)}) collective-permute-start(f16[512,512]{1,0:T(8,128)(2,1)S(1)} %add_convert_fusion.6), channel_id=1, source_target_pairs={{4,8},{8,4},{5,9},{9,5},{6,10},{10,6},{7,11},{11,7},{20,24},{24,20... | collective-permute-start | bytes 1572872 | tf_op jit(solution)/shard_map/ppermute | solution.py:330
  136.0 2.4 %copy-start.12 = (f32[1,128]{1,0:T(1,128)S(1)}, f32[1,128]{1,0:T(1,128)}, u32[]{:S(2)}) copy-start(f32[1,128]{1,0:T(1,128)} %get-tuple-element.367) | copy-start | bytes 1540
  136.0 8.7 %copy-start.8 = (bf16[1024,512]{1,0:T(8,128)(2,1)S(1)}, bf16[1024,512]{1,0:T(8,128)(2,1)}, u32[]{:S(2)}) copy-start(bf16[1024,512]{1,0:T(8,128)(2,1)} %get-tuple-element.278) | copy-start | bytes 3145732
  138.4 1.1 collective-permute-start.22
  139.5 4.7 %collective-permute-start.23 = (f32[1,128]{1,0:T(1,128)S(1)}, f32[1,128]{1,0:T(1,128)S(1)}, u32[]{:S(2)}, u32[]{:S(2)}) collective-permute-start(f32[1,128]{1,0:T(1,128)S(1)} %add.97), channel_id=1, source_target_pairs={{0,2},{1,3},{2,0},{3,1},{4,6},{5,7},{6,4},{7,5},{8,10},{9,11},{10,... | collective-permute-start | bytes 1544 | tf_op jit(solution)/shard_map/ppermute | solution.py:287
  140.8 20.7 %collective-permute-start.28 = (f16[512,768]{1,0:T(8,128)(2,1)}, f16[512,768]{1,0:T(8,128)(2,1)}, u32[]{:S(2)}, u32[]{:S(2)}) collective-permute-start(f16[512,768]{1,0:T(8,128)(2,1)} %add_convert_fusion), channel_id=1, source_target_pairs={{0,4},{4,0},{8,12},{12,8},{1,5},{5,1},{9,13},{13,9},{2,6},{6,2},{1... | collective-permute-start | bytes 2359304 | tf_op jit(solution)/shard_map/ppermute | solution.py:287
  140.9 22.6 %collective-permute-start.29 = (f16[512,768]{1,0:T(8,128)(2,1)}, f16[512,768]{1,0:T(8,128)(2,1)}, u32[]{:S(2)}, u32[]{:S(2)}) collective-permute-start(f16[512,768]{1,0:T(8,128)(2,1)} %add_convert_fusion.1), channel_id=1, source_target_pairs={{4,8},{8,4},{5,9},{9,5},{6,10},{10,6},{7,11},{11,7},{20,24},{24,20... | collective-permute-start | bytes 2359304 | tf_op jit(solution)/shard_map/ppermute | solution.py:330
  147.2 24.6 %collective-permute-start.26 = (f16[512,512]{1,0:T(8,128)(2,1)}, f16[512,512]{1,0:T(8,128)(2,1)}, u32[]{:S(2)}, u32[]{:S(2)}) collective-permute-start(f16[512,512]{1,0:T(8,128)(2,1)} %add_convert_fusion.5), channel_id=1, source_target_pairs={{0,4},{4,0},{8,12},{12,8},{1,5},{5,1},{9,13},{13,9},{2,6},{6,2},{1... | collective-permute-start | bytes 1572872 | tf_op jit(solution)/shard_map/ppermute | solution.py:287
  148.8 2.9 %copy-start.2 = (bf16[512,2048]{1,0:T(8,128)(2,1)S(1)}, bf16[512,2048]{1,0:T(8,128)(2,1)}, u32[]{:S(2)}) copy-start(bf16[512,2048]{1,0:T(8,128)(2,1)} %shard_map.132) | copy-start | bytes 6291460
  149.0 24.5 %collective-permute-start.27 = (f16[512,512]{1,0:T(8,128)(2,1)S(1)}, f16[512,512]{1,0:T(8,128)(2,1)S(1)}, u32[]{:S(2)}, u32[]{:S(2)}) collective-permute-start(f16[512,512]{1,0:T(8,128)(2,1)S(1)} %add_convert_fusion.4), channel_id=1, source_target_pairs={{4,8},{8,4},{5,9},{9,5},{6,10},{10,6},{7,11},{11,7},{20,24},{24,20... | collective-permute-start | bytes 1572872 | tf_op jit(solution)/shard_map/ppermute | solution.py:330

commit v4 on v3

--- a/solution.py
+++ b/solution.py
@@ -425,9 +425,8 @@
     rows3e = joint(pair, c3e)
     a3 = [out(note(product(after(rows3e), w[0]).astype(HALF))), None]
     y1 = swap_tp(after(x1), 2, everyone)
-    p0 = [note(product(after(rows0), w[0])), None]
+    pair1 = joint(x1, y1)
     pair2 = joint(x2, y2)
-    pair1 = joint(x1, y1)
     w[1] = (own_w[1], arrived(other_w[1]))
     a3[1] = out(note(product(after(rows3e), w[1]).astype(HALF)))
     a3[0] = arrived(a3[0])
@@ -461,7 +460,7 @@
     a1p[1] = swap(joined(p1[1], a2m[1]), "fsdp", 1, line)
     p3m[1] = note(product(after(rows3m), w[1]))
     a1m[1] = across(joined(p3m[1], a2e[1]))
-    p0[1] = note(product(after(rows0), w[1]))
+    p0 = [note(product(after(rows0), w[c])) for c in range(2)]
     states = note(
         whole(
             functools.partial(state_kernel, widths, tp_count),

time: 181 us -> 181 us (level)
    ppermute x7, waiting for transfers between devices: 8.68 us -> 18.3 us  [swap_tp(): return send(x, ('fsdp', 'tp'), pairs)]
    ppermute x13, waiting for transfers between devices: 29.6 us -> 22 us  [swap(): return send(x, axis, [(i, i ^ mask) for i in range(size)])]
    ppermute x4, waiting for transfers between devices: 4.41 us -> 0.01 us  [out(): return send(x, 'fsdp', [(0, 1), (3, 2)])]
  transfers between devices with their start and end apart: 30 -> 30, of which waited for: 13 -> 12; matrix products, arithmetic and copies ran while one was open for 25% -> 25% of each run, Pallas kernels for 12% -> 12%
where the time goes in v4:
time: 181 us; the launch traced here: 180 us
  waiting for transfers between devices  52.3 us (29%)
  starting transfers between devices  45.1 us (25%)
  Pallas kernels  29.8 us (16%)
  matrix products  28.5 us (16%)
  other arithmetic  18.9 us (10%)
  local copies, waits for them, and re-layouts  3.69 us (2%)
    ppermute x13, waiting for transfers between devices, swap(): return send(x, axis, [(i, i ^ mask) for i in range(size)])  22 us
    dot_general x10, matrix products, product(): jnp.dot(x[:, deep:], w[1], preferred_element_type=F32)  18.7 us
    ppermute x7, waiting for transfers between devices, swap_tp(): return send(x, ('fsdp', 'tp'), pairs)  18.3 us
    ppermute x13, starting transfers between devices, swap(): return send(x, axis, [(i, i ^ mask) for i in range(size)])  18 us
    ppermute x5, starting transfers between devices, across(): return send(x, 'fsdp', [(1, 2), (2, 1)])  15.1 us
    ppermute x5, waiting for transfers between devices, across(): return send(x, 'fsdp', [(1, 2), (2, 1)])  12 us
    pallas_call x3, Pallas kernels, gather_blocks(): pl.pallas_call(kernel, out_shape=outs, grid_spec=pltpu.PrefetchScalarGrid...  11.5 us
    dot_general x10, matrix products, product(): jnp.dot(x[:, :deep], w[0], preferred_element_type=F32)  9.87 us
  transfers between devices with their start and end apart: 30, of which 12 were waited for; matrix products, arithmetic and copies ran while one was open for 25% of the time, Pallas kernels for 12%

profile of v4, /device:TPU:8, one launch (start us, length us, event | category | flops | bytes accessed | tf_op | source)
XLA Modules:
  0.0 179.6 jit_solution(5165392881683661405)
XLA Ops:
  1.3 3.6 %shard_map.128 = (bf16[128,2048]{1,0:T(8,128)(2,1)}, bf16[1024,768]{1,0:T(8,128)(2,1)}) custom-call(s32[3]{0:T(128)} %pad_add_fusion.where_ref.place, bf16[512,8192]{1,0:T(8,128)(2,1)} %refs_0_.5, bf16[1024,128]{1,0:T(8,128)(2,1)} %wk.3, bf16[1024,128]{1,0:T(8,128)(2,1)} %wv.3, bf16[1024,1024]{1,0:T(8,128)(2,1)} %wq.3), custom_call_target="tpu_custom_call" | custom-call | flops 1 | bytes 1 | tf_op jit(solution)/shard_map/pallas_call | solution.py:167
  4.9 1.6 collective-permute-start.3
  7.1 4.3 %shard_map.129 = (bf16[128,2048]{1,0:T(8,128)(2,1)}, bf16[128,2048]{1,0:T(8,128)(2,1)}, bf16[256,2048]{1,0:T(8,128)(2,1)}, bf16[1024,512]{1,0:T(8,128)(2,1)}) custom-call(s32[3]{0:T(128)} %pad_add_fusion.where_ref.place, bf16[512,8192]{1,0:T(8,128)(2,1)} %refs_0_.5, bf16[1024,1024]{1,0:T(8,128)(2,1)} %wq.3), custom_call_target="tpu_custom_call" | custom-call | flops 1 | bytes 1 | tf_op jit(solution)/shard_map/pallas_call | solution.py:167
  11.4 3.2 %shard_map.130 = f32[3,1024]{1,0:T(4,128)} custom-call(bf16[1024,1024]{1,0:T(8,128)(2,1)} %wq.3, bf16[1024,128]{1,0:T(8,128)(2,1)} %wk.3, bf16[1024,128]{1,0:T(8,128)(2,1)} %wv.3, f32[1,1024]{1,0:T(1,128)} %bitcast.33, f32[1,128]{1,0:T(1,128)} %bitcast.34, f32[1,128]{1,0:T(1,128)} %bitcast.35), custom_call_target="tpu_custom_call" | custom-call | flops 1 | bytes 1 | tf_op jit(solution)/shard_map/pallas_call | solution.py:147
  14.6 1.4 collective-permute-done
  16.0 0.7 add.81
  16.7 1.5 collective-permute-start.1
  18.3 4.0 %collective-permute-start.5 = (bf16[128,2048]{1,0:T(8,128)(2,1)S(1)}, bf16[128,2048]{1,0:T(8,128)(2,1)S(1)}, u32[]{:S(2)}, u32[]{:S(2)}) collective-permute-start(bf16[128,2048]{1,0:T(8,128)(2,1)S(1)} %copy-done.10), channel_id=1, source_target_pairs={{0,8},{4,12},{8,0},{12,4},{1,9},{5,13},{9,1},{13,5},{2,10},{6,14},... | collective-permute-start | bytes 1572872 | tf_op jit(solution)/shard_map/ppermute | solution.py:287
  22.3 1.3 collective-permute-start.4
  24.2 2.7 %shard_map.131 = f32[1,1408]{1,0:T(1,128)} custom-call(bf16[1024,1024]{1,0:T(8,128)(2,1)} %wq.3, bf16[1024,128]{1,0:T(8,128)(2,1)} %wk.3, bf16[1024,128]{1,0:T(8,128)(2,1)} %wv.3, f32[3,1024]{1,0:T(4,128)} %add.82.image), custom_call_target="tpu_custom_call" | custom-call | flops 1 | bytes 1 | tf_op jit(solution)/shard_map/pallas_call | solution.py:147
  27.0 0.8 collective-permute-start.7
  28.4 3.6 %shard_map.132 = bf16[512,2048]{1,0:T(8,128)(2,1)} custom-call(s32[3]{0:T(128)} %pad_add_fusion.where_ref.place, bf16[512,8192]{1,0:T(8,128)(2,1)} %refs_0_.5), custom_call_target="tpu_custom_call" | custom-call | flops 1 | bytes 1 | tf_op jit(solution)/shard_map/pallas_call | solution.py:167
  32.0 13.4 %collective-permute-done.5 = bf16[128,2048]{1,0:T(8,128)(2,1)S(1)} collective-permute-done((bf16[128,2048]{1,0:T(8,128)(2,1)S(1)}, bf16[128,2048]{1,0:T(8,128)(2,1)S(1)}, u32[]{:S(2)}, u32[]{:S(2)}) %collective-permute-start.5) | collective-permute-done | bytes 524320 | tf_op jit(solution)/shard_map/ppermute | solution.py:287
  45.4 1.3 collective-permute-done.4
  46.9 0.7 collective-permute-start.10
  47.6 3.1 %collective-permute-start.8 = (f32[1,1408]{1,0:T(1,128)S(1)}, f32[1,1408]{1,0:T(1,128)S(1)}, u32[]{:S(2)}, u32[]{:S(2)}) collective-permute-start(f32[1,1408]{1,0:T(1,128)S(1)} %add.83), channel_id=1, source_target_pairs={{0,4},{4,0},{8,12},{12,8},{1,5},{5,1},{9,13},{13,9},{2,6},{6,2},{1... | collective-permute-start | bytes 16904 | tf_op jit(solution)/shard_map/ppermute | solution.py:287
  51.2 1.1 collective-permute-done.8
  52.6 1.1 copy-done.4
  53.7 1.0 fusion.29
  54.7 2.5 %add_convert_fusion.3 = f16[512,768]{1,0:T(8,128)(2,1)S(1)} fusion(f32[512,768]{1,0:T(8,128)S(1)} %fusion.29, bf16[1024,768]{1,0:T(8,128)(2,1)} %collective-permute-done.3, bf16[512,2048]{1,0:T(8,128)(2,1)S(1)} %pad_maximum_fusion), kind=kOutput, calls=%fused_computation.8 | convolution fusion | flops 806092800 | bytes 4980736 | tf_op jit(solution)/shard_map/dot_general | solution.py:319
  57.8 1.5 collective-permute-start.13
  59.3 3.0 %collective-permute-start.9 = (bf16[256,2048]{1,0:T(8,128)(2,1)S(1)}, bf16[256,2048]{1,0:T(8,128)(2,1)S(1)}, u32[]{:S(2)}, u32[]{:S(2)}) collective-permute-start(bf16[256,2048]{1,0:T(8,128)(2,1)S(1)} %copy-done.8), channel_id=1, source_target_pairs={{4,8},{8,4},{5,9},{9,5},{6,10},{10,6},{7,11},{11,7},{20,24},{24,20... | collective-permute-start | bytes 3145736 | tf_op jit(solution)/shard_map/ppermute | solution.py:330
  62.3 1.3 collective-permute-start.11
  63.6 8.6 %collective-permute-done.14 = bf16[128,2048]{1,0:T(8,128)(2,1)S(1)} collective-permute-done((bf16[128,2048]{1,0:T(8,128)(2,1)S(1)}, bf16[128,2048]{1,0:T(8,128)(2,1)S(1)}, u32[]{:S(2)}, u32[]{:S(2)}) %collective-permute-start.14) | collective-permute-done | bytes 524320 | tf_op jit(solution)/shard_map/ppermute | solution.py:291
  72.2 9.8 %collective-permute-done.13 = bf16[128,2048]{1,0:T(8,128)(2,1)S(1)} collective-permute-done((bf16[128,2048]{1,0:T(8,128)(2,1)S(1)}, bf16[128,2048]{1,0:T(8,128)(2,1)S(1)}, u32[]{:S(2)}, u32[]{:S(2)}) %collective-permute-start.13) | collective-permute-done | bytes 524320 | tf_op jit(solution)/shard_map/ppermute | solution.py:291
  82.8 1.5 fusion
  84.3 1.0 collective-permute-done.9
  85.3 1.3 collective-permute-start.21
  87.2 3.6 %collective-permute-start.15 = (f32[1,1408]{1,0:T(1,128)S(1)}, f32[1,1408]{1,0:T(1,128)S(1)}, u32[]{:S(2)}, u32[]{:S(2)}) collective-permute-start(f32[1,1408]{1,0:T(1,128)S(1)} %add.84), channel_id=1, source_target_pairs={{0,8},{4,12},{8,0},{12,4},{1,9},{5,13},{9,1},{13,5},{2,10},{6,14},... | collective-permute-start | bytes 16904 | tf_op jit(solution)/shard_map/ppermute | solution.py:287
  90.8 1.9 %collective-permute-start.17 = (bf16[256,2048]{1,0:T(8,128)(2,1)S(1)}, bf16[256,2048]{1,0:T(8,128)(2,1)S(1)}, u32[]{:S(2)}, u32[]{:S(2)}) collective-permute-start(bf16[256,2048]{1,0:T(8,128)(2,1)S(1)} %collective-permute-done.9), channel_id=1, source_target_pairs={{4,5},{5,4},{6,7},{7,6},{8,9},{9,8},{10,11},{11,10},{20,21},{21,20... | collective-permute-start | bytes 3145736 | tf_op jit(solution)/shard_map/ppermute | solution.py:291
  92.9 1.0 fusion.23
  93.9 2.4 %convolution_add_fusion.3 = f32[512,768]{1,0:T(8,128)S(1)} fusion(f32[512,768]{1,0:T(8,128)S(1)} %fusion.23, bf16[1024,768]{1,0:T(8,128)(2,1)} %collective-permute-done.3, bf16[512,2048]{1,0:T(8,128)(2,1)S(1)} %pad_maximum_fusion.1), kind=kOutput, calls=%fused_computation.12 | convolution fusion | flops 805699584 | bytes 5767168 | tf_op jit(solution)/shard_map/dot_general | solution.py:319
  96.3 1.1 add_convert_fusion.2
  97.4 1.3 collective-permute-start.19
  98.6 3.7 %collective-permute-done.15 = f32[1,1408]{1,0:T(1,128)S(1)} collective-permute-done((f32[1,1408]{1,0:T(1,128)S(1)}, f32[1,1408]{1,0:T(1,128)S(1)}, u32[]{:S(2)}, u32[]{:S(2)}) %collective-permute-start.15) | collective-permute-done | bytes 5664 | tf_op jit(solution)/shard_map/ppermute | solution.py:287
  102.4 2.9 %collective-permute-start.20 = (f16[512,768]{1,0:T(8,128)(2,1)}, f16[512,768]{1,0:T(8,128)(2,1)}, u32[]{:S(2)}, u32[]{:S(2)}) collective-permute-start(f16[512,768]{1,0:T(8,128)(2,1)} %add_convert_fusion.2), channel_id=1, source_target_pairs={{4,8},{8,4},{5,9},{9,5},{6,10},{10,6},{7,11},{11,7},{20,24},{24,20... | collective-permute-start | bytes 2359304 | tf_op jit(solution)/shard_map/ppermute | solution.py:330
  105.8 1.5 pad_maximum_fusion.2
  108.3 1.7 convolution_add_fusion.7
  110.0 1.4 shard_map.133
  111.3 2.4 %fusion.17 = f32[512,768]{1,0:T(8,128)S(1)} fusion(bf16[1024,768]{1,0:T(8,128)(2,1)} %get-tuple-element.239, bf16[512,2048]{1,0:T(8,128)(2,1)S(1)} %pad_maximum_fusion.3), kind=kOutput, calls=%fused_computation.42 | convolution fusion | flops 805306368 | bytes 4194304 | tf_op jit(solution)/shard_map/dot_general | solution.py:319
  113.7 2.5 %convolution_add_fusion.2 = f32[512,768]{1,0:T(8,128)S(1)} fusion(f32[512,768]{1,0:T(8,128)S(1)} %fusion.17, bf16[1024,768]{1,0:T(8,128)(2,1)} %collective-permute-done.3, bf16[512,2048]{1,0:T(8,128)(2,1)S(1)} %pad_maximum_fusion.3), kind=kOutput, calls=%fused_computation.11 | convolution fusion | flops 805699584 | bytes 5767168 | tf_op jit(solution)/shard_map/dot_general | solution.py:319
  116.2 7.2 %collective-permute-done.20 = f16[512,768]{1,0:T(8,128)(2,1)} collective-permute-done((f16[512,768]{1,0:T(8,128)(2,1)}, f16[512,768]{1,0:T(8,128)(2,1)}, u32[]{:S(2)}, u32[]{:S(2)}) %collective-permute-start.20) | collective-permute-done | bytes 786464 | tf_op jit(solution)/shard_map/ppermute | solution.py:330
  123.5 1.4 add_convert_fusion.6
  124.8 1.4 collective-permute-start.24
  126.3 3.1 %collective-permute-start.25 = (f16[512,512]{1,0:T(8,128)(2,1)S(1)}, f16[512,512]{1,0:T(8,128)(2,1)S(1)}, u32[]{:S(2)}, u32[]{:S(2)}) collective-permute-start(f16[512,512]{1,0:T(8,128)(2,1)S(1)} %add_convert_fusion.6), channel_id=1, source_target_pairs={{4,8},{8,4},{5,9},{9,5},{6,10},{10,6},{7,11},{11,7},{20,24},{24,20... | collective-permute-start | bytes 1572872 | tf_op jit(solution)/shard_map/ppermute | solution.py:330
  129.3 2.3 %add_convert_fusion.1 = f16[512,768]{1,0:T(8,128)(2,1)} fusion(f32[512,768]{1,0:T(8,128)S(1)} %convolution_add_fusion.2, f16[512,768]{1,0:T(8,128)(2,1)} %collective-permute-done.19), kind=kLoop, calls=%fused_computation.6 | loop fusion | flops 1179648 | bytes 3145728 | tf_op jit(solution)/shard_map/convert_element_type | solution.py:403
  131.6 1.0 fusion.14
  132.6 2.4 %convolution_add_fusion.1 = f32[512,768]{1,0:T(8,128)S(1)} fusion(f32[512,768]{1,0:T(8,128)S(1)} %fusion.14, bf16[1024,768]{1,0:T(8,128)(2,1)} %collective-permute-done.3, bf16[512,2048]{1,0:T(8,128)(2,1)S(1)} %copy-done), kind=kOutput, calls=%fused_computation.10 | convolution fusion | flops 805699584 | bytes 5767168 | tf_op jit(solution)/shard_map/dot_general | solution.py:319
  135.0 2.4 %add_convert_fusion = f16[512,768]{1,0:T(8,128)(2,1)} fusion(f32[512,768]{1,0:T(8,128)S(1)} %convolution_add_fusion.1, f16[512,768]{1,0:T(8,128)(2,1)} %collective-permute-done.20), kind=kLoop, calls=%fused_computation.5 | loop fusion | flops 1179648 | bytes 3145728 | tf_op jit(solution)/shard_map/convert_element_type | solution.py:403
  137.4 1.1 collective-permute-done.22
  139.1 1.2 collective-permute-start.28
  140.3 2.5 %collective-permute-start.29 = (f16[512,768]{1,0:T(8,128)(2,1)}, f16[512,768]{1,0:T(8,128)(2,1)}, u32[]{:S(2)}, u32[]{:S(2)}) collective-permute-start(f16[512,768]{1,0:T(8,128)(2,1)} %add_convert_fusion.1), channel_id=1, source_target_pairs={{4,8},{8,4},{5,9},{9,5},{6,10},{10,6},{7,11},{11,7},{20,24},{24,20... | collective-permute-start | bytes 2359304 | tf_op jit(solution)/shard_map/ppermute | solution.py:330
  144.8 1.0 add_convert_fusion.5
  147.5 3.7 %collective-permute-start.27 = (f16[512,512]{1,0:T(8,128)(2,1)S(1)}, f16[512,512]{1,0:T(8,128)(2,1)S(1)}, u32[]{:S(2)}, u32[]{:S(2)}) collective-permute-start(f16[512,512]{1,0:T(8,128)(2,1)S(1)} %add_convert_fusion.4), channel_id=1, source_target_pairs={{4,8},{8,4},{5,9},{9,5},{6,10},{10,6},{7,11},{11,7},{20,24},{24,20... | collective-permute-start | bytes 1572872 | tf_op jit(solution)/shard_map/ppermute | solution.py:330
  151.2 1.0 fusion.5
  152.2 3.6 %convolution_add_fusion = f32[512,768]{1,0:T(8,128)} fusion(f32[512,768]{1,0:T(8,128)S(1)} %fusion.5, bf16[1024,768]{1,0:T(8,128)(2,1)} %collective-permute-done.3, bf16[512,2048]{1,0:T(8,128)(2,1)S(1)} %copy-done.1), kind=kOutput, calls=%fused_computation.9 | convolution fusion | flops 805699584 | bytes 5767168 | tf_op jit(solution)/shard_map/dot_general | solution.py:319
  157.2 1.5 shard_map.134
  160.0 1.1 slice_bitcast_fusion
  161.2 1.8 collective-permute-done.29
  163.0 3.0 %multiply_convert_fusion.packed = bf16[512,768]{1,0:T(8,128)(2,1)} fusion(f16[512,768]{1,0:T(8,128)(2,1)} %collective-permute-done.29, f32[512,768]{1,0:T(8,128)} %convolution_add_fusion, f16[512,768]{1,0:T(8,128)(2,1)} %collective-permute-done.28, f32[768]{0:T(1024)S(1)} %slice_reduce_fusion), kind=kLoop, calls=%fused_computation.4 | loop fusion | flops 2359296 | bytes 3935232 | tf_op jit(solution)/shard_map/convert_element_type | solution.py:478
  166.0 4.8 %shard_map.135 = (bf16[512,1024]{1,0:T(8,128)(2,1)}, bf16[512,128]{1,0:T(8,128)(2,1)}, bf16[512,128]{1,0:T(8,128)(2,1)}) custom-call(s32[3]{0:T(128)} %pad_add_fusion.where_ref.place, s32[1,8]{1,0:T(1,128)} %lengths.1, bf16[512,768]{1,0:T(8,128)(2,1)} %multiply_convert_fusion.packed), custom_call_target="tpu_custom_call" | custom-call | flops 1 | bytes 1 | tf_op jit(solution)/shard_map/pallas_call | solution.py:248
  170.8 1.9 %collective-permute-done.27 = f16[512,512]{1,0:T(8,128)(2,1)S(1)} collective-permute-done((f16[512,512]{1,0:T(8,128)(2,1)S(1)}, f16[512,512]{1,0:T(8,128)(2,1)S(1)}, u32[]{:S(2)}, u32[]{:S(2)}) %collective-permute-start.27) | collective-permute-done | bytes 524320 | tf_op jit(solution)/shard_map/ppermute | solution.py:330
  172.7 2.1 %multiply_convert_fusion.1.packed = bf16[512,512]{1,0:T(8,128)(2,1)} fusion(f16[512,512]{1,0:T(8,128)(2,1)S(1)} %collective-permute-done.27, f32[512,512]{1,0:T(8,128)S(1)} %convolution_add_fusion.4, f16[512,512]{1,0:T(8,128)(2,1)} %collective-permute-done.26, f32[512]{0:T(512)S(1)} %bitcast.32), kind=kLoop, calls=%fused_computation.22 | loop fusion | flops 1572864 | bytes 2623488 | tf_op jit(solution)/shard_map/convert_element_type | solution.py:478
  174.8 4.8 %shard_map.136 = bf16[512,1024]{1,0:T(8,128)(2,1)} custom-call(s32[3]{0:T(128)} %pad_add_fusion.where_ref.place, s32[1,8]{1,0:T(1,128)} %lengths.1, bf16[512,512]{1,0:T(8,128)(2,1)} %multiply_convert_fusion.1.packed, bf16[512,128]{1,0:T(8,128)(2,1)} %get-tuple-element.428.refs_0_, ...), custom_call_target="tpu_custom_call", output_to_operand_aliasing={{}: (5, {})} | custom-call | flops 1 | bytes 1 | tf_op jit(solution)/shard_map/pallas_call | solution.py:248
  (75 shorter events, 14.3 us)
Async XLA Ops:
  4.9 41.9 %collective-permute-start.3 = (bf16[1024,768]{1,0:T(8,128)(2,1)}, bf16[1024,768]{1,0:T(8,128)(2,1)}, u32[]{:S(2)}, u32[]{:S(2)}) collective-permute-start(bf16[1024,768]{1,0:T(8,128)(2,1)} %get-tuple-element.239), channel_id=1, source_target_pairs={{0,16},{16,0},{1,17},{17,1},{2,18},{18,2},{3,19},{19,3},{4,20},{20... | collective-permute-start | bytes 4718600 | tf_op jit(solution)/shard_map/ppermute | solution.py:287
  6.4 20.5 %collective-permute-start.6 = (bf16[128,2048]{1,0:T(8,128)(2,1)}, bf16[128,2048]{1,0:T(8,128)(2,1)S(1)}, u32[]{:S(2)}, u32[]{:S(2)}) collective-permute-start(bf16[128,2048]{1,0:T(8,128)(2,1)} %get-tuple-element.243), channel_id=1, source_target_pairs={{0,12},{12,0},{1,13},{13,1},{2,14},{14,2},{3,15},{15,3},{16,28},{2... | collective-permute-start | bytes 1572872 | tf_op jit(solution)/shard_map/ppermute | solution.py:353
  11.4 6.8 %copy-start.10 = (bf16[128,2048]{1,0:T(8,128)(2,1)S(1)}, bf16[128,2048]{1,0:T(8,128)(2,1)}, u32[]{:S(2)}) copy-start(bf16[128,2048]{1,0:T(8,128)(2,1)} %get-tuple-element.242) | copy-start | bytes 1572868
  11.4 10.9 %copy-start.9 = (bf16[128,2048]{1,0:T(8,128)(2,1)S(1)}, bf16[128,2048]{1,0:T(8,128)(2,1)}, u32[]{:S(2)}) copy-start(bf16[128,2048]{1,0:T(8,128)(2,1)} %get-tuple-element.241) | copy-start | bytes 1572868
  14.6 1.4 collective-permute-start
  16.7 6.9 %collective-permute-start.1 = (f32[3,1024]{1,0:T(4,128)S(1)}, f32[3,1024]{1,0:T(4,128)S(1)}, u32[]{:S(2)}, u32[]{:S(2)}) collective-permute-start(f32[3,1024]{1,0:T(4,128)S(1)} %add.81), channel_id=1, source_target_pairs={{0,2},{1,3},{2,0},{3,1},{4,6},{5,7},{6,4},{7,5},{8,10},{9,11},{10,... | collective-permute-start | bytes 36872 | tf_op jit(solution)/shard_map/ppermute | solution.py:287
  18.3 27.2 %collective-permute-start.5 = (bf16[128,2048]{1,0:T(8,128)(2,1)S(1)}, bf16[128,2048]{1,0:T(8,128)(2,1)S(1)}, u32[]{:S(2)}, u32[]{:S(2)}) collective-permute-start(bf16[128,2048]{1,0:T(8,128)(2,1)S(1)} %copy-done.10), channel_id=1, source_target_pairs={{0,8},{4,12},{8,0},{12,4},{1,9},{5,13},{9,1},{13,5},{2,10},{6,14},... | collective-permute-start | bytes 1572872 | tf_op jit(solution)/shard_map/ppermute | solution.py:287
  22.3 24.4 %collective-permute-start.4 = (bf16[128,2048]{1,0:T(8,128)(2,1)S(1)}, bf16[128,2048]{1,0:T(8,128)(2,1)S(1)}, u32[]{:S(2)}, u32[]{:S(2)}) collective-permute-start(bf16[128,2048]{1,0:T(8,128)(2,1)S(1)} %copy-done.9), channel_id=1, source_target_pairs={{0,4},{4,0},{8,12},{12,8},{1,5},{5,1},{9,13},{13,9},{2,6},{6,2},{1... | collective-permute-start | bytes 1572872 | tf_op jit(solution)/shard_map/ppermute | solution.py:287
  27.0 19.8 %copy-start.3 = (f32[1,1408]{1,0:T(1,128)S(1)}, f32[1,1408]{1,0:T(1,128)}, u32[]{:S(2)}) copy-start(f32[1,1408]{1,0:T(1,128)} %shard_map.131) | copy-start | bytes 16900
  27.0 19.8 %collective-permute-start.7 = (bf16[128,2048]{1,0:T(8,128)(2,1)S(1)}, bf16[128,2048]{1,0:T(8,128)(2,1)S(1)}, u32[]{:S(2)}, u32[]{:S(2)}) collective-permute-start(bf16[128,2048]{1,0:T(8,128)(2,1)S(1)} %collective-permute-done.6), channel_id=1, source_target_pairs={{0,2},{1,3},{2,0},{3,1},{12,14},{13,15},{14,12},{15,13},{16,18},{1... | collective-permute-start | bytes 1572872 | tf_op jit(solution)/shard_map/ppermute | solution.py:291
  27.8 19.0 %collective-permute-start.2 = (f32[1,1408]{1,0:T(1,128)}, f32[1,1408]{1,0:T(1,128)S(1)}, u32[]{:S(2)}, u32[]{:S(2)}) collective-permute-start(f32[1,1408]{1,0:T(1,128)} %shard_map.131), channel_id=1, source_target_pairs={{0,16},{16,0},{1,17},{17,1},{2,18},{18,2},{3,19},{19,3},{4,20},{20... | collective-permute-start | bytes 16904 | tf_op jit(solution)/shard_map/ppermute | solution.py:287
  32.0 18.7 %copy-start.6 = (bf16[1024,512]{1,0:T(8,128)(2,1)S(1)}, bf16[1024,512]{1,0:T(8,128)(2,1)}, u32[]{:S(2)}) copy-start(bf16[1024,512]{1,0:T(8,128)(2,1)} %get-tuple-element.278) | copy-start | bytes 3145732
  46.9 5.4 %collective-permute-start.10 = (bf16[256,2048]{1,0:T(8,128)(2,1)S(1)}, bf16[256,2048]{1,0:T(8,128)(2,1)S(1)}, u32[]{:S(2)}, u32[]{:S(2)}) collective-permute-start(bf16[256,2048]{1,0:T(8,128)(2,1)S(1)} %pad_maximum_fusion.4), channel_id=1, source_target_pairs={{0,1},{1,0},{2,3},{3,2},{12,13},{13,12},{14,15},{15,14},{16,17},{1... | collective-permute-start | bytes 3145736 | tf_op jit(solution)/shard_map/ppermute | solution.py:291
  47.6 4.7 %collective-permute-start.8 = (f32[1,1408]{1,0:T(1,128)S(1)}, f32[1,1408]{1,0:T(1,128)S(1)}, u32[]{:S(2)}, u32[]{:S(2)}) collective-permute-start(f32[1,1408]{1,0:T(1,128)S(1)} %add.83), channel_id=1, source_target_pairs={{0,4},{4,0},{8,12},{12,8},{1,5},{5,1},{9,13},{13,9},{2,6},{6,2},{1... | collective-permute-start | bytes 16904 | tf_op jit(solution)/shard_map/ppermute | solution.py:287
  50.7 31.4 %collective-permute-start.12 = (bf16[1024,512]{1,0:T(8,128)(2,1)S(1)}, bf16[1024,512]{1,0:T(8,128)(2,1)S(1)}, u32[]{:S(2)}, u32[]{:S(2)}) collective-permute-start(bf16[1024,512]{1,0:T(8,128)(2,1)S(1)} %copy-done.6), channel_id=1, source_target_pairs={{0,16},{16,0},{1,17},{17,1},{2,18},{18,2},{3,19},{19,3},{4,20},{20... | collective-permute-start | bytes 3145736 | tf_op jit(solution)/shard_map/ppermute | solution.py:287
  52.3 1.4 copy-start.4
  54.7 4.6 %copy-start.8 = (bf16[256,2048]{1,0:T(8,128)(2,1)S(1)}, bf16[256,2048]{1,0:T(8,128)(2,1)}, u32[]{:S(2)}) copy-start(bf16[256,2048]{1,0:T(8,128)(2,1)} %get-tuple-element.268) | copy-start | bytes 3145732
  57.2 14.9 %collective-permute-start.14 = (bf16[128,2048]{1,0:T(8,128)(2,1)S(1)}, bf16[128,2048]{1,0:T(8,128)(2,1)S(1)}, u32[]{:S(2)}, u32[]{:S(2)}) collective-permute-start(bf16[128,2048]{1,0:T(8,128)(2,1)S(1)} %collective-permute-done.4), channel_id=1, source_target_pairs={{0,2},{1,3},{2,0},{3,1},{4,6},{5,7},{6,4},{7,5},{8,10},{9,11},{10,... | collective-permute-start | bytes 1572872 | tf_op jit(solution)/shard_map/ppermute | solution.py:291
  57.8 24.2 %collective-permute-start.13 = (bf16[128,2048]{1,0:T(8,128)(2,1)S(1)}, bf16[128,2048]{1,0:T(8,128)(2,1)S(1)}, u32[]{:S(2)}, u32[]{:S(2)}) collective-permute-start(bf16[128,2048]{1,0:T(8,128)(2,1)S(1)} %collective-permute-done.5), channel_id=1, source_target_pairs={{0,2},{1,3},{2,0},{3,1},{4,6},{5,7},{6,4},{7,5},{8,10},{9,11},{10,... | collective-permute-start | bytes 1572872 | tf_op jit(solution)/shard_map/ppermute | solution.py:291
  59.3 26.0 %collective-permute-start.9 = (bf16[256,2048]{1,0:T(8,128)(2,1)S(1)}, bf16[256,2048]{1,0:T(8,128)(2,1)S(1)}, u32[]{:S(2)}, u32[]{:S(2)}) collective-permute-start(bf16[256,2048]{1,0:T(8,128)(2,1)S(1)} %copy-done.8), channel_id=1, source_target_pairs={{4,8},{8,4},{5,9},{9,5},{6,10},{10,6},{7,11},{11,7},{20,24},{24,20... | collective-permute-start | bytes 3145736 | tf_op jit(solution)/shard_map/ppermute | solution.py:330
  62.3 22.0 %collective-permute-start.11 = (f16[512,768]{1,0:T(8,128)(2,1)S(1)}, f16[512,768]{1,0:T(8,128)(2,1)S(1)}, u32[]{:S(2)}, u32[]{:S(2)}) collective-permute-start(f16[512,768]{1,0:T(8,128)(2,1)S(1)} %add_convert_fusion.3), channel_id=1, source_target_pairs={{0,4},{12,8},{1,5},{13,9},{2,6},{14,10},{3,7},{15,11},{16,20},{28,... | collective-permute-start | bytes 2359304 | tf_op jit(solution)/shard_map/ppermute | solution.py:327
  85.3 7.4 %collective-permute-start.16 = (bf16[256,2048]{1,0:T(8,128)(2,1)S(1)}, bf16[256,2048]{1,0:T(8,128)(2,1)S(1)}, u32[]{:S(2)}, u32[]{:S(2)}) collective-permute-start(bf16[256,2048]{1,0:T(8,128)(2,1)S(1)} %pad_maximum_fusion.6), channel_id=1, source_target_pairs={{0,1},{1,0},{2,3},{3,2},{4,5},{5,4},{6,7},{7,6},{8,9},{9,8},{10,11... | collective-permute-start | bytes 3145736 | tf_op jit(solution)/shard_map/ppermute | solution.py:291
  85.3 38.1 %collective-permute-start.21 = (f16[512,512]{1,0:T(8,128)(2,1)}, f16[512,512]{1,0:T(8,128)(2,1)}, u32[]{:S(2)}, u32[]{:S(2)}) collective-permute-start(f16[512,512]{1,0:T(8,128)(2,1)} %fusion), channel_id=1, source_target_pairs={{0,4},{12,8},{1,5},{13,9},{2,6},{14,10},{3,7},{15,11},{16,20},{28,... | collective-permute-start | bytes 1572872 | tf_op jit(solution)/shard_map/ppermute | solution.py:327
  86.6 19.2 %collective-permute-start.18 = (bf16[256,2048]{1,0:T(8,128)(2,1)S(1)}, bf16[256,2048]{1,0:T(8,128)(2,1)S(1)}, u32[]{:S(2)}, u32[]{:S(2)}) collective-permute-start(bf16[256,2048]{1,0:T(8,128)(2,1)S(1)} %pad_maximum_fusion.5), channel_id=1, source_target_pairs={{0,1},{1,0},{2,3},{3,2},{4,5},{5,4},{6,7},{7,6},{8,9},{9,8},{10,11... | collective-permute-start | bytes 3145736 | tf_op jit(solution)/shard_map/ppermute | solution.py:291
  87.2 15.2 %collective-permute-start.15 = (f32[1,1408]{1,0:T(1,128)S(1)}, f32[1,1408]{1,0:T(1,128)S(1)}, u32[]{:S(2)}, u32[]{:S(2)}) collective-permute-start(f32[1,1408]{1,0:T(1,128)S(1)} %add.84), channel_id=1, source_target_pairs={{0,8},{4,12},{8,0},{12,4},{1,9},{5,13},{9,1},{13,5},{2,10},{6,14},... | collective-permute-start | bytes 16904 | tf_op jit(solution)/shard_map/ppermute | solution.py:287
  90.8 16.5 %collective-permute-start.17 = (bf16[256,2048]{1,0:T(8,128)(2,1)S(1)}, bf16[256,2048]{1,0:T(8,128)(2,1)S(1)}, u32[]{:S(2)}, u32[]{:S(2)}) collective-permute-start(bf16[256,2048]{1,0:T(8,128)(2,1)S(1)} %collective-permute-done.9), channel_id=1, source_target_pairs={{4,5},{5,4},{6,7},{7,6},{8,9},{9,8},{10,11},{11,10},{20,21},{21,20... | collective-permute-start | bytes 3145736 | tf_op jit(solution)/shard_map/ppermute | solution.py:291
  97.4 26.1 %collective-permute-start.19 = (f16[512,768]{1,0:T(8,128)(2,1)}, f16[512,768]{1,0:T(8,128)(2,1)}, u32[]{:S(2)}, u32[]{:S(2)}) collective-permute-start(f16[512,768]{1,0:T(8,128)(2,1)} %add_convert_fusion.2), channel_id=1, source_target_pairs={{0,4},{12,8},{1,5},{13,9},{2,6},{14,10},{3,7},{15,11},{16,20},{28,... | collective-permute-start | bytes 2359304 | tf_op jit(solution)/shard_map/ppermute | solution.py:327
  102.4 21.1 %collective-permute-start.20 = (f16[512,768]{1,0:T(8,128)(2,1)}, f16[512,768]{1,0:T(8,128)(2,1)}, u32[]{:S(2)}, u32[]{:S(2)}) collective-permute-start(f16[512,768]{1,0:T(8,128)(2,1)} %add_convert_fusion.2), channel_id=1, source_target_pairs={{4,8},{8,4},{5,9},{9,5},{6,10},{10,6},{7,11},{11,7},{20,24},{24,20... | collective-permute-start | bytes 2359304 | tf_op jit(solution)/shard_map/ppermute | solution.py:330
  113.7 9.7 %copy-start.2 = (f32[512,512]{1,0:T(8,128)S(1)}, f32[512,512]{1,0:T(8,128)}, u32[]{:S(2)}) copy-start(f32[512,512]{1,0:T(8,128)} %convolution_add_fusion.7) | copy-start | bytes 3145732
  123.5 8.1 %copy-start.5 = (bf16[1024,768]{1,0:T(8,128)(2,1)S(1)}, bf16[1024,768]{1,0:T(8,128)(2,1)}, u32[]{:S(2)}) copy-start(bf16[1024,768]{1,0:T(8,128)(2,1)} %get-tuple-element.239) | copy-start | bytes 4718596
  124.8 6.8 %copy-start = (bf16[512,2048]{1,0:T(8,128)(2,1)S(1)}, bf16[512,2048]{1,0:T(8,128)(2,1)}, u32[]{:S(2)}) copy-start(bf16[512,2048]{1,0:T(8,128)(2,1)} %pad_maximum_fusion.2) | copy-start | bytes 6291460
  124.8 18.5 %collective-permute-start.24 = (f16[512,512]{1,0:T(8,128)(2,1)S(1)}, f16[512,512]{1,0:T(8,128)(2,1)S(1)}, u32[]{:S(2)}, u32[]{:S(2)}) collective-permute-start(f16[512,512]{1,0:T(8,128)(2,1)S(1)} %add_convert_fusion.6), channel_id=1, source_target_pairs={{0,4},{12,8},{1,5},{13,9},{2,6},{14,10},{3,7},{15,11},{16,20},{28,... | collective-permute-start | bytes 1572872 | tf_op jit(solution)/shard_map/ppermute | solution.py:327
  126.3 17.0 %collective-permute-start.25 = (f16[512,512]{1,0:T(8,128)(2,1)S(1)}, f16[512,512]{1,0:T(8,128)(2,1)S(1)}, u32[]{:S(2)}, u32[]{:S(2)}) collective-permute-start(f16[512,512]{1,0:T(8,128)(2,1)S(1)} %add_convert_fusion.6), channel_id=1, source_target_pairs={{4,8},{8,4},{5,9},{9,5},{6,10},{10,6},{7,11},{11,7},{20,24},{24,20... | collective-permute-start | bytes 1572872 | tf_op jit(solution)/shard_map/ppermute | solution.py:330
  135.0 2.4 %copy-start.11 = (f32[1,128]{1,0:T(1,128)S(1)}, f32[1,128]{1,0:T(1,128)}, u32[]{:S(2)}) copy-start(f32[1,128]{1,0:T(1,128)} %get-tuple-element.363) | copy-start | bytes 1540
  135.0 8.3 %copy-start.7 = (bf16[1024,512]{1,0:T(8,128)(2,1)S(1)}, bf16[1024,512]{1,0:T(8,128)(2,1)}, u32[]{:S(2)}) copy-start(bf16[1024,512]{1,0:T(8,128)(2,1)} %get-tuple-element.278) | copy-start | bytes 3145732
  137.4 1.1 collective-permute-start.22
  138.5 4.3 %collective-permute-start.23 = (f32[1,128]{1,0:T(1,128)S(1)}, f32[1,128]{1,0:T(1,128)S(1)}, u32[]{:S(2)}, u32[]{:S(2)}) collective-permute-start(f32[1,128]{1,0:T(1,128)S(1)} %add.96), channel_id=1, source_target_pairs={{0,2},{1,3},{2,0},{3,1},{4,6},{5,7},{6,4},{7,5},{8,10},{9,11},{10,... | collective-permute-start | bytes 1544 | tf_op jit(solution)/shard_map/ppermute | solution.py:287
  139.1 22.0 %collective-permute-start.28 = (f16[512,768]{1,0:T(8,128)(2,1)}, f16[512,768]{1,0:T(8,128)(2,1)}, u32[]{:S(2)}, u32[]{:S(2)}) collective-permute-start(f16[512,768]{1,0:T(8,128)(2,1)} %add_convert_fusion), channel_id=1, source_target_pairs={{0,4},{4,0},{8,12},{12,8},{1,5},{5,1},{9,13},{13,9},{2,6},{6,2},{1... | collective-permute-start | bytes 2359304 | tf_op jit(solution)/shard_map/ppermute | solution.py:287
  140.3 22.7 %collective-permute-start.29 = (f16[512,768]{1,0:T(8,128)(2,1)}, f16[512,768]{1,0:T(8,128)(2,1)}, u32[]{:S(2)}, u32[]{:S(2)}) collective-permute-start(f16[512,768]{1,0:T(8,128)(2,1)} %add_convert_fusion.1), channel_id=1, source_target_pairs={{4,8},{8,4},{5,9},{9,5},{6,10},{10,6},{7,11},{11,7},{20,24},{24,20... | collective-permute-start | bytes 2359304 | tf_op jit(solution)/shard_map/ppermute | solution.py:330
  145.8 25.0 %collective-permute-start.26 = (f16[512,512]{1,0:T(8,128)(2,1)}, f16[512,512]{1,0:T(8,128)(2,1)}, u32[]{:S(2)}, u32[]{:S(2)}) collective-permute-start(f16[512,512]{1,0:T(8,128)(2,1)} %add_convert_fusion.5), channel_id=1, source_target_pairs={{0,4},{4,0},{8,12},{12,8},{1,5},{5,1},{9,13},{13,9},{2,6},{6,2},{1... | collective-permute-start | bytes 1572872 | tf_op jit(solution)/shard_map/ppermute | solution.py:287
  147.2 3.9 %copy-start.1 = (bf16[512,2048]{1,0:T(8,128)(2,1)S(1)}, bf16[512,2048]{1,0:T(8,128)(2,1)}, u32[]{:S(2)}) copy-start(bf16[512,2048]{1,0:T(8,128)(2,1)} %shard_map.132) | copy-start | bytes 6291460
  147.5 25.3 %collective-permute-start.27 = (f16[512,512]{1,0:T(8,128)(2,1)S(1)}, f16[512,512]{1,0:T(8,128)(2,1)S(1)}, u32[]{:S(2)}, u32[]{:S(2)}) collective-permute-start(f16[512,512]{1,0:T(8,128)(2,1)S(1)} %add_convert_fusion.4), channel_id=1, source_target_pairs={{4,8},{8,4},{5,9},{9,5},{6,10},{10,6},{7,11},{11,7},{20,24},{24,20... | collective-permute-start | bytes 1572872 | tf_op jit(solution)/shard_map/ppermute | solution.py:330

commit v5 on v4

--- a/solution.py
+++ b/solution.py
@@ -211,10 +211,10 @@
         ).reshape(heads, block, high - low)
         s = jnp.where(allowed, s * HD ** (-0.5), MASKED)
         e = jnp.exp(s - jnp.max(s, axis=2, keepdims=True))
-        p = (e * (1.0 / jnp.sum(e, axis=2, keepdims=True))).astype(BF16)
-        mixed = jnp.dot(
-            p.reshape(heads * block, high - low), values[low:high, :], preferred_element_type=F32
-        ).astype(BF16)
+        total = jnp.sum(e, axis=2, keepdims=True).reshape(heads * block, 1)
+        p = e.astype(BF16).reshape(heads * block, high - low)
+        mixed = jnp.dot(p, values[low:high, :], preferred_element_type=F32)
+        mixed = (mixed * (1.0 / total)).astype(BF16)
         for h in range(heads):
             ctx[i * block : high, h * HD : (h + 1) * HD] = mixed[h * block : (h + 1) * block, :]
 

time: 181 us -> 180 us (level)
  transfers between devices with their start and end apart: 30 -> 30, of which waited for: 12 -> 12; matrix products, arithmetic and copies ran while one was open for 25% -> 26% of each run, Pallas kernels for 12% -> 12%
where the time goes in v5:
time: 180 us; the launch traced here: 179 us
  waiting for transfers between devices  52.8 us (29%)
  starting transfers between devices  45.1 us (25%)
  Pallas kernels  28.8 us (16%)
  matrix products  28.5 us (16%)
  other arithmetic  18.9 us (10%)
  local copies, waits for them, and re-layouts  3.69 us (2%)
    ppermute x13, waiting for transfers between devices, swap(): return send(x, axis, [(i, i ^ mask) for i in range(size)])  22 us
    dot_general x10, matrix products, product(): jnp.dot(x[:, deep:], w[1], preferred_element_type=F32)  18.7 us
    ppermute x7, waiting for transfers between devices, swap_tp(): return send(x, ('fsdp', 'tp'), pairs)  18.3 us
    ppermute x13, starting transfers between devices, swap(): return send(x, axis, [(i, i ^ mask) for i in range(size)])  18 us
    ppermute x5, starting transfers between devices, across(): return send(x, 'fsdp', [(1, 2), (2, 1)])  15.1 us
    ppermute x5, waiting for transfers between devices, across(): return send(x, 'fsdp', [(1, 2), (2, 1)])  12.5 us
    pallas_call x3, Pallas kernels, gather_blocks(): pl.pallas_call(kernel, out_shape=outs, grid_spec=pltpu.PrefetchScalarGrid...  11.5 us
    dot_general x10, matrix products, product(): jnp.dot(x[:, :deep], w[0], preferred_element_type=F32)  9.87 us
  transfers between devices with their start and end apart: 30, of which 12 were waited for; matrix products, arithmetic and copies ran while one was open for 26% of the time, Pallas kernels for 12%

profile of v5, /device:TPU:8, one launch (start us, length us, event | category | flops | bytes accessed | tf_op | source)
XLA Modules:
  0.0 179.1 jit_solution(16636981633651895610)
XLA Ops:
  1.3 3.6 %shard_map.128 = (bf16[128,2048]{1,0:T(8,128)(2,1)}, bf16[1024,768]{1,0:T(8,128)(2,1)}) custom-call(s32[3]{0:T(128)} %pad_add_fusion.where_ref.place, bf16[512,8192]{1,0:T(8,128)(2,1)} %refs_0_.5, bf16[1024,128]{1,0:T(8,128)(2,1)} %wk.3, bf16[1024,128]{1,0:T(8,128)(2,1)} %wv.3, bf16[1024,1024]{1,0:T(8,128)(2,1)} %wq.3), custom_call_target="tpu_custom_call" | custom-call | flops 1 | bytes 1 | tf_op jit(solution)/shard_map/pallas_call | solution.py:167
  4.9 1.6 collective-permute-start.3
  7.1 4.3 %shard_map.129 = (bf16[128,2048]{1,0:T(8,128)(2,1)}, bf16[128,2048]{1,0:T(8,128)(2,1)}, bf16[256,2048]{1,0:T(8,128)(2,1)}, bf16[1024,512]{1,0:T(8,128)(2,1)}) custom-call(s32[3]{0:T(128)} %pad_add_fusion.where_ref.place, bf16[512,8192]{1,0:T(8,128)(2,1)} %refs_0_.5, bf16[1024,1024]{1,0:T(8,128)(2,1)} %wq.3), custom_call_target="tpu_custom_call" | custom-call | flops 1 | bytes 1 | tf_op jit(solution)/shard_map/pallas_call | solution.py:167
  11.4 3.2 %shard_map.130 = f32[3,1024]{1,0:T(4,128)} custom-call(bf16[1024,1024]{1,0:T(8,128)(2,1)} %wq.3, bf16[1024,128]{1,0:T(8,128)(2,1)} %wk.3, bf16[1024,128]{1,0:T(8,128)(2,1)} %wv.3, f32[1,1024]{1,0:T(1,128)} %bitcast.33, f32[1,128]{1,0:T(1,128)} %bitcast.34, f32[1,128]{1,0:T(1,128)} %bitcast.35), custom_call_target="tpu_custom_call" | custom-call | flops 1 | bytes 1 | tf_op jit(solution)/shard_map/pallas_call | solution.py:147
  14.6 1.4 collective-permute-done
  16.0 0.7 add.81
  16.7 1.5 collective-permute-start.1
  18.3 4.0 %collective-permute-start.5 = (bf16[128,2048]{1,0:T(8,128)(2,1)S(1)}, bf16[128,2048]{1,0:T(8,128)(2,1)S(1)}, u32[]{:S(2)}, u32[]{:S(2)}) collective-permute-start(bf16[128,2048]{1,0:T(8,128)(2,1)S(1)} %copy-done.10), channel_id=1, source_target_pairs={{0,8},{4,12},{8,0},{12,4},{1,9},{5,13},{9,1},{13,5},{2,10},{6,14},... | collective-permute-start | bytes 1572872 | tf_op jit(solution)/shard_map/ppermute | solution.py:287
  22.3 1.3 collective-permute-start.4
  24.2 2.7 %shard_map.131 = f32[1,1408]{1,0:T(1,128)} custom-call(bf16[1024,1024]{1,0:T(8,128)(2,1)} %wq.3, bf16[1024,128]{1,0:T(8,128)(2,1)} %wk.3, bf16[1024,128]{1,0:T(8,128)(2,1)} %wv.3, f32[3,1024]{1,0:T(4,128)} %add.82.image), custom_call_target="tpu_custom_call" | custom-call | flops 1 | bytes 1 | tf_op jit(solution)/shard_map/pallas_call | solution.py:147
  27.0 0.8 collective-permute-start.7
  28.4 3.6 %shard_map.132 = bf16[512,2048]{1,0:T(8,128)(2,1)} custom-call(s32[3]{0:T(128)} %pad_add_fusion.where_ref.place, bf16[512,8192]{1,0:T(8,128)(2,1)} %refs_0_.5), custom_call_target="tpu_custom_call" | custom-call | flops 1 | bytes 1 | tf_op jit(solution)/shard_map/pallas_call | solution.py:167
  32.0 13.4 %collective-permute-done.5 = bf16[128,2048]{1,0:T(8,128)(2,1)S(1)} collective-permute-done((bf16[128,2048]{1,0:T(8,128)(2,1)S(1)}, bf16[128,2048]{1,0:T(8,128)(2,1)S(1)}, u32[]{:S(2)}, u32[]{:S(2)}) %collective-permute-start.5) | collective-permute-done | bytes 524320 | tf_op jit(solution)/shard_map/ppermute | solution.py:287
  45.4 1.3 collective-permute-done.4
  46.9 0.7 collective-permute-start.10
  47.6 3.1 %collective-permute-start.8 = (f32[1,1408]{1,0:T(1,128)S(1)}, f32[1,1408]{1,0:T(1,128)S(1)}, u32[]{:S(2)}, u32[]{:S(2)}) collective-permute-start(f32[1,1408]{1,0:T(1,128)S(1)} %add.83), channel_id=1, source_target_pairs={{0,4},{4,0},{8,12},{12,8},{1,5},{5,1},{9,13},{13,9},{2,6},{6,2},{1... | collective-permute-start | bytes 16904 | tf_op jit(solution)/shard_map/ppermute | solution.py:287
  51.2 1.1 collective-permute-done.8
  52.6 1.1 copy-done.4
  53.7 1.0 fusion.29
  54.7 2.5 %add_convert_fusion.3 = f16[512,768]{1,0:T(8,128)(2,1)S(1)} fusion(f32[512,768]{1,0:T(8,128)S(1)} %fusion.29, bf16[1024,768]{1,0:T(8,128)(2,1)} %collective-permute-done.3, bf16[512,2048]{1,0:T(8,128)(2,1)S(1)} %pad_maximum_fusion), kind=kOutput, calls=%fused_computation.8 | convolution fusion | flops 806092800 | bytes 4980736 | tf_op jit(solution)/shard_map/dot_general | solution.py:319
  57.8 1.5 collective-permute-start.13
  59.3 3.0 %collective-permute-start.9 = (bf16[256,2048]{1,0:T(8,128)(2,1)S(1)}, bf16[256,2048]{1,0:T(8,128)(2,1)S(1)}, u32[]{:S(2)}, u32[]{:S(2)}) collective-permute-start(bf16[256,2048]{1,0:T(8,128)(2,1)S(1)} %copy-done.8), channel_id=1, source_target_pairs={{4,8},{8,4},{5,9},{9,5},{6,10},{10,6},{7,11},{11,7},{20,24},{24,20... | collective-permute-start | bytes 3145736 | tf_op jit(solution)/shard_map/ppermute | solution.py:330
  62.3 1.3 collective-permute-start.11
  63.6 8.6 %collective-permute-done.14 = bf16[128,2048]{1,0:T(8,128)(2,1)S(1)} collective-permute-done((bf16[128,2048]{1,0:T(8,128)(2,1)S(1)}, bf16[128,2048]{1,0:T(8,128)(2,1)S(1)}, u32[]{:S(2)}, u32[]{:S(2)}) %collective-permute-start.14) | collective-permute-done | bytes 524320 | tf_op jit(solution)/shard_map/ppermute | solution.py:291
  72.2 9.8 %collective-permute-done.13 = bf16[128,2048]{1,0:T(8,128)(2,1)S(1)} collective-permute-done((bf16[128,2048]{1,0:T(8,128)(2,1)S(1)}, bf16[128,2048]{1,0:T(8,128)(2,1)S(1)}, u32[]{:S(2)}, u32[]{:S(2)}) %collective-permute-start.13) | collective-permute-done | bytes 524320 | tf_op jit(solution)/shard_map/ppermute | solution.py:291
  82.8 1.5 fusion
  84.3 1.0 collective-permute-done.9
  85.3 1.3 collective-permute-start.21
  87.2 3.6 %collective-permute-start.15 = (f32[1,1408]{1,0:T(1,128)S(1)}, f32[1,1408]{1,0:T(1,128)S(1)}, u32[]{:S(2)}, u32[]{:S(2)}) collective-permute-start(f32[1,1408]{1,0:T(1,128)S(1)} %add.84), channel_id=1, source_target_pairs={{0,8},{4,12},{8,0},{12,4},{1,9},{5,13},{9,1},{13,5},{2,10},{6,14},... | collective-permute-start | bytes 16904 | tf_op jit(solution)/shard_map/ppermute | solution.py:287
  90.8 1.9 %collective-permute-start.17 = (bf16[256,2048]{1,0:T(8,128)(2,1)S(1)}, bf16[256,2048]{1,0:T(8,128)(2,1)S(1)}, u32[]{:S(2)}, u32[]{:S(2)}) collective-permute-start(bf16[256,2048]{1,0:T(8,128)(2,1)S(1)} %collective-permute-done.9), channel_id=1, source_target_pairs={{4,5},{5,4},{6,7},{7,6},{8,9},{9,8},{10,11},{11,10},{20,21},{21,20... | collective-permute-start | bytes 3145736 | tf_op jit(solution)/shard_map/ppermute | solution.py:291
  92.9 1.0 fusion.23
  93.9 2.4 %convolution_add_fusion.3 = f32[512,768]{1,0:T(8,128)S(1)} fusion(f32[512,768]{1,0:T(8,128)S(1)} %fusion.23, bf16[1024,768]{1,0:T(8,128)(2,1)} %collective-permute-done.3, bf16[512,2048]{1,0:T(8,128)(2,1)S(1)} %pad_maximum_fusion.1), kind=kOutput, calls=%fused_computation.12 | convolution fusion | flops 805699584 | bytes 5767168 | tf_op jit(solution)/shard_map/dot_general | solution.py:319
  96.3 1.1 add_convert_fusion.2
  97.4 1.3 collective-permute-start.19
  98.6 3.7 %collective-permute-done.15 = f32[1,1408]{1,0:T(1,128)S(1)} collective-permute-done((f32[1,1408]{1,0:T(1,128)S(1)}, f32[1,1408]{1,0:T(1,128)S(1)}, u32[]{:S(2)}, u32[]{:S(2)}) %collective-permute-start.15) | collective-permute-done | bytes 5664 | tf_op jit(solution)/shard_map/ppermute | solution.py:287
  102.4 2.9 %collective-permute-start.20 = (f16[512,768]{1,0:T(8,128)(2,1)}, f16[512,768]{1,0:T(8,128)(2,1)}, u32[]{:S(2)}, u32[]{:S(2)}) collective-permute-start(f16[512,768]{1,0:T(8,128)(2,1)} %add_convert_fusion.2), channel_id=1, source_target_pairs={{4,8},{8,4},{5,9},{9,5},{6,10},{10,6},{7,11},{11,7},{20,24},{24,20... | collective-permute-start | bytes 2359304 | tf_op jit(solution)/shard_map/ppermute | solution.py:330
  105.8 1.5 pad_maximum_fusion.2
  108.3 1.7 convolution_add_fusion.7
  110.0 1.4 shard_map.133
  111.3 2.4 %fusion.17 = f32[512,768]{1,0:T(8,128)S(1)} fusion(bf16[1024,768]{1,0:T(8,128)(2,1)} %get-tuple-element.239, bf16[512,2048]{1,0:T(8,128)(2,1)S(1)} %pad_maximum_fusion.3), kind=kOutput, calls=%fused_computation.42 | convolution fusion | flops 805306368 | bytes 4194304 | tf_op jit(solution)/shard_map/dot_general | solution.py:319
  113.7 2.5 %convolution_add_fusion.2 = f32[512,768]{1,0:T(8,128)S(1)} fusion(f32[512,768]{1,0:T(8,128)S(1)} %fusion.17, bf16[1024,768]{1,0:T(8,128)(2,1)} %collective-permute-done.3, bf16[512,2048]{1,0:T(8,128)(2,1)S(1)} %pad_maximum_fusion.3), kind=kOutput, calls=%fused_computation.11 | convolution fusion | flops 805699584 | bytes 5767168 | tf_op jit(solution)/shard_map/dot_general | solution.py:319
  116.2 7.2 %collective-permute-done.20 = f16[512,768]{1,0:T(8,128)(2,1)} collective-permute-done((f16[512,768]{1,0:T(8,128)(2,1)}, f16[512,768]{1,0:T(8,128)(2,1)}, u32[]{:S(2)}, u32[]{:S(2)}) %collective-permute-start.20) | collective-permute-done | bytes 786464 | tf_op jit(solution)/shard_map/ppermute | solution.py:330
  123.5 1.4 add_convert_fusion.6
  124.8 1.4 collective-permute-start.24
  126.3 3.1 %collective-permute-start.25 = (f16[512,512]{1,0:T(8,128)(2,1)S(1)}, f16[512,512]{1,0:T(8,128)(2,1)S(1)}, u32[]{:S(2)}, u32[]{:S(2)}) collective-permute-start(f16[512,512]{1,0:T(8,128)(2,1)S(1)} %add_convert_fusion.6), channel_id=1, source_target_pairs={{4,8},{8,4},{5,9},{9,5},{6,10},{10,6},{7,11},{11,7},{20,24},{24,20... | collective-permute-start | bytes 1572872 | tf_op jit(solution)/shard_map/ppermute | solution.py:330
  129.3 2.3 %add_convert_fusion.1 = f16[512,768]{1,0:T(8,128)(2,1)} fusion(f32[512,768]{1,0:T(8,128)S(1)} %convolution_add_fusion.2, f16[512,768]{1,0:T(8,128)(2,1)} %collective-permute-done.19), kind=kLoop, calls=%fused_computation.6 | loop fusion | flops 1179648 | bytes 3145728 | tf_op jit(solution)/shard_map/convert_element_type | solution.py:403
  131.6 1.0 fusion.14
  132.6 2.4 %convolution_add_fusion.1 = f32[512,768]{1,0:T(8,128)S(1)} fusion(f32[512,768]{1,0:T(8,128)S(1)} %fusion.14, bf16[1024,768]{1,0:T(8,128)(2,1)} %collective-permute-done.3, bf16[512,2048]{1,0:T(8,128)(2,1)S(1)} %copy-done), kind=kOutput, calls=%fused_computation.10 | convolution fusion | flops 805699584 | bytes 5767168 | tf_op jit(solution)/shard_map/dot_general | solution.py:319
  135.0 2.4 %add_convert_fusion = f16[512,768]{1,0:T(8,128)(2,1)} fusion(f32[512,768]{1,0:T(8,128)S(1)} %convolution_add_fusion.1, f16[512,768]{1,0:T(8,128)(2,1)} %collective-permute-done.20), kind=kLoop, calls=%fused_computation.5 | loop fusion | flops 1179648 | bytes 3145728 | tf_op jit(solution)/shard_map/convert_element_type | solution.py:403
  137.4 1.1 collective-permute-done.22
  139.1 1.2 collective-permute-start.28
  140.3 2.5 %collective-permute-start.29 = (f16[512,768]{1,0:T(8,128)(2,1)}, f16[512,768]{1,0:T(8,128)(2,1)}, u32[]{:S(2)}, u32[]{:S(2)}) collective-permute-start(f16[512,768]{1,0:T(8,128)(2,1)} %add_convert_fusion.1), channel_id=1, source_target_pairs={{4,8},{8,4},{5,9},{9,5},{6,10},{10,6},{7,11},{11,7},{20,24},{24,20... | collective-permute-start | bytes 2359304 | tf_op jit(solution)/shard_map/ppermute | solution.py:330
  144.8 1.0 add_convert_fusion.5
  147.5 3.7 %collective-permute-start.27 = (f16[512,512]{1,0:T(8,128)(2,1)S(1)}, f16[512,512]{1,0:T(8,128)(2,1)S(1)}, u32[]{:S(2)}, u32[]{:S(2)}) collective-permute-start(f16[512,512]{1,0:T(8,128)(2,1)S(1)} %add_convert_fusion.4), channel_id=1, source_target_pairs={{4,8},{8,4},{5,9},{9,5},{6,10},{10,6},{7,11},{11,7},{20,24},{24,20... | collective-permute-start | bytes 1572872 | tf_op jit(solution)/shard_map/ppermute | solution.py:330
  151.2 1.0 fusion.5
  152.2 3.6 %convolution_add_fusion = f32[512,768]{1,0:T(8,128)} fusion(f32[512,768]{1,0:T(8,128)S(1)} %fusion.5, bf16[1024,768]{1,0:T(8,128)(2,1)} %collective-permute-done.3, bf16[512,2048]{1,0:T(8,128)(2,1)S(1)} %copy-done.1), kind=kOutput, calls=%fused_computation.9 | convolution fusion | flops 805699584 | bytes 5767168 | tf_op jit(solution)/shard_map/dot_general | solution.py:319
  157.2 1.5 shard_map.134
  160.0 1.1 slice_bitcast_fusion
  161.2 1.8 collective-permute-done.29
  163.0 3.0 %multiply_convert_fusion.packed = bf16[512,768]{1,0:T(8,128)(2,1)} fusion(f16[512,768]{1,0:T(8,128)(2,1)} %collective-permute-done.29, f32[512,768]{1,0:T(8,128)} %convolution_add_fusion, f16[512,768]{1,0:T(8,128)(2,1)} %collective-permute-done.28, f32[768]{0:T(1024)S(1)} %slice_reduce_fusion), kind=kLoop, calls=%fused_computation.4 | loop fusion | flops 2359296 | bytes 3935232 | tf_op jit(solution)/shard_map/convert_element_type | solution.py:478
  166.0 4.3 %shard_map.135 = (bf16[512,1024]{1,0:T(8,128)(2,1)}, bf16[512,128]{1,0:T(8,128)(2,1)}, bf16[512,128]{1,0:T(8,128)(2,1)}) custom-call(s32[3]{0:T(128)} %pad_add_fusion.where_ref.place, s32[1,8]{1,0:T(1,128)} %lengths.1, bf16[512,768]{1,0:T(8,128)(2,1)} %multiply_convert_fusion.packed), custom_call_target="tpu_custom_call" | custom-call | flops 1 | bytes 1 | tf_op jit(solution)/shard_map/pallas_call | solution.py:248
  170.3 2.5 %collective-permute-done.27 = f16[512,512]{1,0:T(8,128)(2,1)S(1)} collective-permute-done((f16[512,512]{1,0:T(8,128)(2,1)S(1)}, f16[512,512]{1,0:T(8,128)(2,1)S(1)}, u32[]{:S(2)}, u32[]{:S(2)}) %collective-permute-start.27) | collective-permute-done | bytes 524320 | tf_op jit(solution)/shard_map/ppermute | solution.py:330
  172.7 2.1 %multiply_convert_fusion.1.packed = bf16[512,512]{1,0:T(8,128)(2,1)} fusion(f16[512,512]{1,0:T(8,128)(2,1)S(1)} %collective-permute-done.27, f32[512,512]{1,0:T(8,128)S(1)} %convolution_add_fusion.4, f16[512,512]{1,0:T(8,128)(2,1)} %collective-permute-done.26, f32[512]{0:T(512)S(1)} %bitcast.32), kind=kLoop, calls=%fused_computation.22 | loop fusion | flops 1572864 | bytes 2623488 | tf_op jit(solution)/shard_map/convert_element_type | solution.py:478
  174.8 4.3 %shard_map.136 = bf16[512,1024]{1,0:T(8,128)(2,1)} custom-call(s32[3]{0:T(128)} %pad_add_fusion.where_ref.place, s32[1,8]{1,0:T(1,128)} %lengths.1, bf16[512,512]{1,0:T(8,128)(2,1)} %multiply_convert_fusion.1.packed, bf16[512,128]{1,0:T(8,128)(2,1)} %get-tuple-element.428.refs_0_, ...), custom_call_target="tpu_custom_call", output_to_operand_aliasing={{}: (5, {})} | custom-call | flops 1 | bytes 1 | tf_op jit(solution)/shard_map/pallas_call | solution.py:248
  (75 shorter events, 14.3 us)
Async XLA Ops:
  4.9 41.9 %collective-permute-start.3 = (bf16[1024,768]{1,0:T(8,128)(2,1)}, bf16[1024,768]{1,0:T(8,128)(2,1)}, u32[]{:S(2)}, u32[]{:S(2)}) collective-permute-start(bf16[1024,768]{1,0:T(8,128)(2,1)} %get-tuple-element.239), channel_id=1, source_target_pairs={{0,16},{16,0},{1,17},{17,1},{2,18},{18,2},{3,19},{19,3},{4,20},{20... | collective-permute-start | bytes 4718600 | tf_op jit(solution)/shard_map/ppermute | solution.py:287
  6.4 20.5 %collective-permute-start.6 = (bf16[128,2048]{1,0:T(8,128)(2,1)}, bf16[128,2048]{1,0:T(8,128)(2,1)S(1)}, u32[]{:S(2)}, u32[]{:S(2)}) collective-permute-start(bf16[128,2048]{1,0:T(8,128)(2,1)} %get-tuple-element.243), channel_id=1, source_target_pairs={{0,12},{12,0},{1,13},{13,1},{2,14},{14,2},{3,15},{15,3},{16,28},{2... | collective-permute-start | bytes 1572872 | tf_op jit(solution)/shard_map/ppermute | solution.py:353
  11.4 6.8 %copy-start.10 = (bf16[128,2048]{1,0:T(8,128)(2,1)S(1)}, bf16[128,2048]{1,0:T(8,128)(2,1)}, u32[]{:S(2)}) copy-start(bf16[128,2048]{1,0:T(8,128)(2,1)} %get-tuple-element.242) | copy-start | bytes 1572868
  11.4 10.9 %copy-start.9 = (bf16[128,2048]{1,0:T(8,128)(2,1)S(1)}, bf16[128,2048]{1,0:T(8,128)(2,1)}, u32[]{:S(2)}) copy-start(bf16[128,2048]{1,0:T(8,128)(2,1)} %get-tuple-element.241) | copy-start | bytes 1572868
  14.6 1.4 collective-permute-start
  16.7 6.9 %collective-permute-start.1 = (f32[3,1024]{1,0:T(4,128)S(1)}, f32[3,1024]{1,0:T(4,128)S(1)}, u32[]{:S(2)}, u32[]{:S(2)}) collective-permute-start(f32[3,1024]{1,0:T(4,128)S(1)} %add.81), channel_id=1, source_target_pairs={{0,2},{1,3},{2,0},{3,1},{4,6},{5,7},{6,4},{7,5},{8,10},{9,11},{10,... | collective-permute-start | bytes 36872 | tf_op jit(solution)/shard_map/ppermute | solution.py:287
  18.3 27.2 %collective-permute-start.5 = (bf16[128,2048]{1,0:T(8,128)(2,1)S(1)}, bf16[128,2048]{1,0:T(8,128)(2,1)S(1)}, u32[]{:S(2)}, u32[]{:S(2)}) collective-permute-start(bf16[128,2048]{1,0:T(8,128)(2,1)S(1)} %copy-done.10), channel_id=1, source_target_pairs={{0,8},{4,12},{8,0},{12,4},{1,9},{5,13},{9,1},{13,5},{2,10},{6,14},... | collective-permute-start | bytes 1572872 | tf_op jit(solution)/shard_map/ppermute | solution.py:287
  22.3 24.4 %collective-permute-start.4 = (bf16[128,2048]{1,0:T(8,128)(2,1)S(1)}, bf16[128,2048]{1,0:T(8,128)(2,1)S(1)}, u32[]{:S(2)}, u32[]{:S(2)}) collective-permute-start(bf16[128,2048]{1,0:T(8,128)(2,1)S(1)} %copy-done.9), channel_id=1, source_target_pairs={{0,4},{4,0},{8,12},{12,8},{1,5},{5,1},{9,13},{13,9},{2,6},{6,2},{1... | collective-permute-start | bytes 1572872 | tf_op jit(solution)/shard_map/ppermute | solution.py:287
  27.0 19.8 %copy-start.3 = (f32[1,1408]{1,0:T(1,128)S(1)}, f32[1,1408]{1,0:T(1,128)}, u32[]{:S(2)}) copy-start(f32[1,1408]{1,0:T(1,128)} %shard_map.131) | copy-start | bytes 16900
  27.0 19.8 %collective-permute-start.7 = (bf16[128,2048]{1,0:T(8,128)(2,1)S(1)}, bf16[128,2048]{1,0:T(8,128)(2,1)S(1)}, u32[]{:S(2)}, u32[]{:S(2)}) collective-permute-start(bf16[128,2048]{1,0:T(8,128)(2,1)S(1)} %collective-permute-done.6), channel_id=1, source_target_pairs={{0,2},{1,3},{2,0},{3,1},{12,14},{13,15},{14,12},{15,13},{16,18},{1... | collective-permute-start | bytes 1572872 | tf_op jit(solution)/shard_map/ppermute | solution.py:291
  27.8 19.0 %collective-permute-start.2 = (f32[1,1408]{1,0:T(1,128)}, f32[1,1408]{1,0:T(1,128)S(1)}, u32[]{:S(2)}, u32[]{:S(2)}) collective-permute-start(f32[1,1408]{1,0:T(1,128)} %shard_map.131), channel_id=1, source_target_pairs={{0,16},{16,0},{1,17},{17,1},{2,18},{18,2},{3,19},{19,3},{4,20},{20... | collective-permute-start | bytes 16904 | tf_op jit(solution)/shard_map/ppermute | solution.py:287
  32.0 18.7 %copy-start.6 = (bf16[1024,512]{1,0:T(8,128)(2,1)S(1)}, bf16[1024,512]{1,0:T(8,128)(2,1)}, u32[]{:S(2)}) copy-start(bf16[1024,512]{1,0:T(8,128)(2,1)} %get-tuple-element.278) | copy-start | bytes 3145732
  46.9 5.4 %collective-permute-start.10 = (bf16[256,2048]{1,0:T(8,128)(2,1)S(1)}, bf16[256,2048]{1,0:T(8,128)(2,1)S(1)}, u32[]{:S(2)}, u32[]{:S(2)}) collective-permute-start(bf16[256,2048]{1,0:T(8,128)(2,1)S(1)} %pad_maximum_fusion.4), channel_id=1, source_target_pairs={{0,1},{1,0},{2,3},{3,2},{12,13},{13,12},{14,15},{15,14},{16,17},{1... | collective-permute-start | bytes 3145736 | tf_op jit(solution)/shard_map/ppermute | solution.py:291
  47.6 4.7 %collective-permute-start.8 = (f32[1,1408]{1,0:T(1,128)S(1)}, f32[1,1408]{1,0:T(1,128)S(1)}, u32[]{:S(2)}, u32[]{:S(2)}) collective-permute-start(f32[1,1408]{1,0:T(1,128)S(1)} %add.83), channel_id=1, source_target_pairs={{0,4},{4,0},{8,12},{12,8},{1,5},{5,1},{9,13},{13,9},{2,6},{6,2},{1... | collective-permute-start | bytes 16904 | tf_op jit(solution)/shard_map/ppermute | solution.py:287
  50.7 31.4 %collective-permute-start.12 = (bf16[1024,512]{1,0:T(8,128)(2,1)S(1)}, bf16[1024,512]{1,0:T(8,128)(2,1)S(1)}, u32[]{:S(2)}, u32[]{:S(2)}) collective-permute-start(bf16[1024,512]{1,0:T(8,128)(2,1)S(1)} %copy-done.6), channel_id=1, source_target_pairs={{0,16},{16,0},{1,17},{17,1},{2,18},{18,2},{3,19},{19,3},{4,20},{20... | collective-permute-start | bytes 3145736 | tf_op jit(solution)/shard_map/ppermute | solution.py:287
  52.3 1.4 copy-start.4
  54.7 4.6 %copy-start.8 = (bf16[256,2048]{1,0:T(8,128)(2,1)S(1)}, bf16[256,2048]{1,0:T(8,128)(2,1)}, u32[]{:S(2)}) copy-start(bf16[256,2048]{1,0:T(8,128)(2,1)} %get-tuple-element.268) | copy-start | bytes 3145732
  57.2 14.9 %collective-permute-start.14 = (bf16[128,2048]{1,0:T(8,128)(2,1)S(1)}, bf16[128,2048]{1,0:T(8,128)(2,1)S(1)}, u32[]{:S(2)}, u32[]{:S(2)}) collective-permute-start(bf16[128,2048]{1,0:T(8,128)(2,1)S(1)} %collective-permute-done.4), channel_id=1, source_target_pairs={{0,2},{1,3},{2,0},{3,1},{4,6},{5,7},{6,4},{7,5},{8,10},{9,11},{10,... | collective-permute-start | bytes 1572872 | tf_op jit(solution)/shard_map/ppermute | solution.py:291
  57.8 24.2 %collective-permute-start.13 = (bf16[128,2048]{1,0:T(8,128)(2,1)S(1)}, bf16[128,2048]{1,0:T(8,128)(2,1)S(1)}, u32[]{:S(2)}, u32[]{:S(2)}) collective-permute-start(bf16[128,2048]{1,0:T(8,128)(2,1)S(1)} %collective-permute-done.5), channel_id=1, source_target_pairs={{0,2},{1,3},{2,0},{3,1},{4,6},{5,7},{6,4},{7,5},{8,10},{9,11},{10,... | collective-permute-start | bytes 1572872 | tf_op jit(solution)/shard_map/ppermute | solution.py:291
  59.3 26.0 %collective-permute-start.9 = (bf16[256,2048]{1,0:T(8,128)(2,1)S(1)}, bf16[256,2048]{1,0:T(8,128)(2,1)S(1)}, u32[]{:S(2)}, u32[]{:S(2)}) collective-permute-start(bf16[256,2048]{1,0:T(8,128)(2,1)S(1)} %copy-done.8), channel_id=1, source_target_pairs={{4,8},{8,4},{5,9},{9,5},{6,10},{10,6},{7,11},{11,7},{20,24},{24,20... | collective-permute-start | bytes 3145736 | tf_op jit(solution)/shard_map/ppermute | solution.py:330
  62.3 22.0 %collective-permute-start.11 = (f16[512,768]{1,0:T(8,128)(2,1)S(1)}, f16[512,768]{1,0:T(8,128)(2,1)S(1)}, u32[]{:S(2)}, u32[]{:S(2)}) collective-permute-start(f16[512,768]{1,0:T(8,128)(2,1)S(1)} %add_convert_fusion.3), channel_id=1, source_target_pairs={{0,4},{12,8},{1,5},{13,9},{2,6},{14,10},{3,7},{15,11},{16,20},{28,... | collective-permute-start | bytes 2359304 | tf_op jit(solution)/shard_map/ppermute | solution.py:327
  85.3 7.4 %collective-permute-start.16 = (bf16[256,2048]{1,0:T(8,128)(2,1)S(1)}, bf16[256,2048]{1,0:T(8,128)(2,1)S(1)}, u32[]{:S(2)}, u32[]{:S(2)}) collective-permute-start(bf16[256,2048]{1,0:T(8,128)(2,1)S(1)} %pad_maximum_fusion.6), channel_id=1, source_target_pairs={{0,1},{1,0},{2,3},{3,2},{4,5},{5,4},{6,7},{7,6},{8,9},{9,8},{10,11... | collective-permute-start | bytes 3145736 | tf_op jit(solution)/shard_map/ppermute | solution.py:291
  85.3 38.1 %collective-permute-start.21 = (f16[512,512]{1,0:T(8,128)(2,1)}, f16[512,512]{1,0:T(8,128)(2,1)}, u32[]{:S(2)}, u32[]{:S(2)}) collective-permute-start(f16[512,512]{1,0:T(8,128)(2,1)} %fusion), channel_id=1, source_target_pairs={{0,4},{12,8},{1,5},{13,9},{2,6},{14,10},{3,7},{15,11},{16,20},{28,... | collective-permute-start | bytes 1572872 | tf_op jit(solution)/shard_map/ppermute | solution.py:327
  86.6 19.2 %collective-permute-start.18 = (bf16[256,2048]{1,0:T(8,128)(2,1)S(1)}, bf16[256,2048]{1,0:T(8,128)(2,1)S(1)}, u32[]{:S(2)}, u32[]{:S(2)}) collective-permute-start(bf16[256,2048]{1,0:T(8,128)(2,1)S(1)} %pad_maximum_fusion.5), channel_id=1, source_target_pairs={{0,1},{1,0},{2,3},{3,2},{4,5},{5,4},{6,7},{7,6},{8,9},{9,8},{10,11... | collective-permute-start | bytes 3145736 | tf_op jit(solution)/shard_map/ppermute | solution.py:291
  87.2 15.2 %collective-permute-start.15 = (f32[1,1408]{1,0:T(1,128)S(1)}, f32[1,1408]{1,0:T(1,128)S(1)}, u32[]{:S(2)}, u32[]{:S(2)}) collective-permute-start(f32[1,1408]{1,0:T(1,128)S(1)} %add.84), channel_id=1, source_target_pairs={{0,8},{4,12},{8,0},{12,4},{1,9},{5,13},{9,1},{13,5},{2,10},{6,14},... | collective-permute-start | bytes 16904 | tf_op jit(solution)/shard_map/ppermute | solution.py:287
  90.8 16.5 %collective-permute-start.17 = (bf16[256,2048]{1,0:T(8,128)(2,1)S(1)}, bf16[256,2048]{1,0:T(8,128)(2,1)S(1)}, u32[]{:S(2)}, u32[]{:S(2)}) collective-permute-start(bf16[256,2048]{1,0:T(8,128)(2,1)S(1)} %collective-permute-done.9), channel_id=1, source_target_pairs={{4,5},{5,4},{6,7},{7,6},{8,9},{9,8},{10,11},{11,10},{20,21},{21,20... | collective-permute-start | bytes 3145736 | tf_op jit(solution)/shard_map/ppermute | solution.py:291
  97.4 26.1 %collective-permute-start.19 = (f16[512,768]{1,0:T(8,128)(2,1)}, f16[512,768]{1,0:T(8,128)(2,1)}, u32[]{:S(2)}, u32[]{:S(2)}) collective-permute-start(f16[512,768]{1,0:T(8,128)(2,1)} %add_convert_fusion.2), channel_id=1, source_target_pairs={{0,4},{12,8},{1,5},{13,9},{2,6},{14,10},{3,7},{15,11},{16,20},{28,... | collective-permute-start | bytes 2359304 | tf_op jit(solution)/shard_map/ppermute | solution.py:327
  102.4 21.1 %collective-permute-start.20 = (f16[512,768]{1,0:T(8,128)(2,1)}, f16[512,768]{1,0:T(8,128)(2,1)}, u32[]{:S(2)}, u32[]{:S(2)}) collective-permute-start(f16[512,768]{1,0:T(8,128)(2,1)} %add_convert_fusion.2), channel_id=1, source_target_pairs={{4,8},{8,4},{5,9},{9,5},{6,10},{10,6},{7,11},{11,7},{20,24},{24,20... | collective-permute-start | bytes 2359304 | tf_op jit(solution)/shard_map/ppermute | solution.py:330
  113.7 9.7 %copy-start.2 = (f32[512,512]{1,0:T(8,128)S(1)}, f32[512,512]{1,0:T(8,128)}, u32[]{:S(2)}) copy-start(f32[512,512]{1,0:T(8,128)} %convolution_add_fusion.7) | copy-start | bytes 3145732
  123.5 8.1 %copy-start.5 = (bf16[1024,768]{1,0:T(8,128)(2,1)S(1)}, bf16[1024,768]{1,0:T(8,128)(2,1)}, u32[]{:S(2)}) copy-start(bf16[1024,768]{1,0:T(8,128)(2,1)} %get-tuple-element.239) | copy-start | bytes 4718596
  124.8 6.8 %copy-start = (bf16[512,2048]{1,0:T(8,128)(2,1)S(1)}, bf16[512,2048]{1,0:T(8,128)(2,1)}, u32[]{:S(2)}) copy-start(bf16[512,2048]{1,0:T(8,128)(2,1)} %pad_maximum_fusion.2) | copy-start | bytes 6291460
  124.8 18.5 %collective-permute-start.24 = (f16[512,512]{1,0:T(8,128)(2,1)S(1)}, f16[512,512]{1,0:T(8,128)(2,1)S(1)}, u32[]{:S(2)}, u32[]{:S(2)}) collective-permute-start(f16[512,512]{1,0:T(8,128)(2,1)S(1)} %add_convert_fusion.6), channel_id=1, source_target_pairs={{0,4},{12,8},{1,5},{13,9},{2,6},{14,10},{3,7},{15,11},{16,20},{28,... | collective-permute-start | bytes 1572872 | tf_op jit(solution)/shard_map/ppermute | solution.py:327
  126.3 17.0 %collective-permute-start.25 = (f16[512,512]{1,0:T(8,128)(2,1)S(1)}, f16[512,512]{1,0:T(8,128)(2,1)S(1)}, u32[]{:S(2)}, u32[]{:S(2)}) collective-permute-start(f16[512,512]{1,0:T(8,128)(2,1)S(1)} %add_convert_fusion.6), channel_id=1, source_target_pairs={{4,8},{8,4},{5,9},{9,5},{6,10},{10,6},{7,11},{11,7},{20,24},{24,20... | collective-permute-start | bytes 1572872 | tf_op jit(solution)/shard_map/ppermute | solution.py:330
  135.0 2.4 %copy-start.11 = (f32[1,128]{1,0:T(1,128)S(1)}, f32[1,128]{1,0:T(1,128)}, u32[]{:S(2)}) copy-start(f32[1,128]{1,0:T(1,128)} %get-tuple-element.363) | copy-start | bytes 1540
  135.0 8.3 %copy-start.7 = (bf16[1024,512]{1,0:T(8,128)(2,1)S(1)}, bf16[1024,512]{1,0:T(8,128)(2,1)}, u32[]{:S(2)}) copy-start(bf16[1024,512]{1,0:T(8,128)(2,1)} %get-tuple-element.278) | copy-start | bytes 3145732
  137.4 1.1 collective-permute-start.22
  138.5 4.3 %collective-permute-start.23 = (f32[1,128]{1,0:T(1,128)S(1)}, f32[1,128]{1,0:T(1,128)S(1)}, u32[]{:S(2)}, u32[]{:S(2)}) collective-permute-start(f32[1,128]{1,0:T(1,128)S(1)} %add.96), channel_id=1, source_target_pairs={{0,2},{1,3},{2,0},{3,1},{4,6},{5,7},{6,4},{7,5},{8,10},{9,11},{10,... | collective-permute-start | bytes 1544 | tf_op jit(solution)/shard_map/ppermute | solution.py:287
  139.1 22.0 %collective-permute-start.28 = (f16[512,768]{1,0:T(8,128)(2,1)}, f16[512,768]{1,0:T(8,128)(2,1)}, u32[]{:S(2)}, u32[]{:S(2)}) collective-permute-start(f16[512,768]{1,0:T(8,128)(2,1)} %add_convert_fusion), channel_id=1, source_target_pairs={{0,4},{4,0},{8,12},{12,8},{1,5},{5,1},{9,13},{13,9},{2,6},{6,2},{1... | collective-permute-start | bytes 2359304 | tf_op jit(solution)/shard_map/ppermute | solution.py:287
  140.3 22.7 %collective-permute-start.29 = (f16[512,768]{1,0:T(8,128)(2,1)}, f16[512,768]{1,0:T(8,128)(2,1)}, u32[]{:S(2)}, u32[]{:S(2)}) collective-permute-start(f16[512,768]{1,0:T(8,128)(2,1)} %add_convert_fusion.1), channel_id=1, source_target_pairs={{4,8},{8,4},{5,9},{9,5},{6,10},{10,6},{7,11},{11,7},{20,24},{24,20... | collective-permute-start | bytes 2359304 | tf_op jit(solution)/shard_map/ppermute | solution.py:330
  145.8 24.5 %collective-permute-start.26 = (f16[512,512]{1,0:T(8,128)(2,1)}, f16[512,512]{1,0:T(8,128)(2,1)}, u32[]{:S(2)}, u32[]{:S(2)}) collective-permute-start(f16[512,512]{1,0:T(8,128)(2,1)} %add_convert_fusion.5), channel_id=1, source_target_pairs={{0,4},{4,0},{8,12},{12,8},{1,5},{5,1},{9,13},{13,9},{2,6},{6,2},{1... | collective-permute-start | bytes 1572872 | tf_op jit(solution)/shard_map/ppermute | solution.py:287
  147.2 3.9 %copy-start.1 = (bf16[512,2048]{1,0:T(8,128)(2,1)S(1)}, bf16[512,2048]{1,0:T(8,128)(2,1)}, u32[]{:S(2)}) copy-start(bf16[512,2048]{1,0:T(8,128)(2,1)} %shard_map.132) | copy-start | bytes 6291460
  147.5 25.3 %collective-permute-start.27 = (f16[512,512]{1,0:T(8,128)(2,1)S(1)}, f16[512,512]{1,0:T(8,128)(2,1)S(1)}, u32[]{:S(2)}, u32[]{:S(2)}) collective-permute-start(f16[512,512]{1,0:T(8,128)(2,1)S(1)} %add_convert_fusion.4), channel_id=1, source_target_pairs={{4,8},{8,4},{5,9},{9,5},{6,10},{10,6},{7,11},{11,7},{20,24},{24,20... | collective-permute-start | bytes 1572872 | tf_op jit(solution)/shard_map/ppermute | solution.py:330
